TPU v7x, 32 devices: a whole 2x2x4 slice. The times are simulated.
32 devices in a mesh: seq: 8 (over z, y), head: 4 (over x, core).
Axes of the slice: x: 2, y: 2, z: 4, core: 2. Of those that a mesh axis runs over, the one named last changes fastest.
Arguments:
- tokens: bfloat16 [2048, 2048], P('seq'), may hold values from -6 to 6
- first_gain: float32 [2048], replicated, may hold values from 0.5 to 1.5
- query_weight: bfloat16 [2048, 2048], P(None, 'head'), may hold values from -0.125 to 0.125
- key_weight: bfloat16 [2048, 2048], P(None, 'head'), may hold values from -0.125 to 0.125
- value_weight: bfloat16 [2048, 4096], P(None, 'head'), may hold values from -0.125 to 0.125
- gate_weight: bfloat16 [2048, 4096], P(None, 'head'), may hold values from -0.125 to 0.125
- output_weight: bfloat16 [4096, 2048], P('head'), may hold values from -0.125 to 0.125
- second_gain: float32 [2048], replicated, may hold values from 0.5 to 1.5
- gelu_weight: bfloat16 [2048, 4096], P(None, 'head'), may hold values from -0.125 to 0.125
- linear_weight: bfloat16 [2048, 4096], P(None, 'head'), may hold values from -0.125 to 0.125
- down_weight: bfloat16 [4096, 2048], P('head'), may hold values from -0.09375 to 0.09375
- log_decay: float32 [8, 2048], P('head', 'seq'), may hold values from -1 to 0, as said below
- first_start: int32 [8], P('seq'), may hold values from 0 to 256, as said below
- cotangent: bfloat16 [2048, 2048], P('seq'), may hold values from -6 to 6
Outputs:
- output: bfloat16 [2048, 2048], P('seq')
- grad_tokens: bfloat16 [2048, 2048], P('seq')
- grad_first_gain: float32 [2048], P('seq')
- grad_query: float32 [2048, 2048], P('seq', 'head')
- grad_key: float32 [2048, 2048], P('seq', 'head')
- grad_value: float32 [2048, 4096], P('seq', 'head')
- grad_gate: float32 [2048, 4096], P('seq', 'head')
- grad_output: float32 [4096, 2048], P('head', 'seq')
- grad_second_gain: float32 [2048], P('seq')
- grad_gelu: float32 [2048, 4096], P('seq', 'head')
- grad_linear: float32 [2048, 4096], P('seq', 'head')
- grad_down: float32 [4096, 2048], P('head', 'seq')
Inputs may be any that keep to these rules, and one draw needn't show every extreme that they name: `first_start`: each shard of 256 tokens holds at most one sequence start; the value 256 means that no sequence starts in the shard; the first shard's value is 0. `log_decay`: every entry is negative.
All inputs are finite; a program needn't handle non-finite values.
Results may differ from a plain program's by a relative error of at most 0.011.
The roundings to bfloat16 on the way count: a program that leaves them out, or rounds other values in their place, can miss the bound.
Values sent between devices are 32-bit elements; how exact they have to be, the bound alone decides.
No kernel may reach another device: no remote copies, remote signals or barrier semaphores. Data moves between devices by JAX's collectives and lax.ppermute only.
A program may use at most 256 MiB of HBM per device.

v0:
```python
import math

import jax
import jax.numpy as jnp
from jax import lax
from jax.sharding import PartitionSpec as P

DK = 256
DV = 512
BLK = 256


maximum_precision = lax.Precision.HIGHEST
eps_norm = 1e-05


def carried_in(part, axis, combine, identity, reverse):
    count = lax.axis_size(axis)
    place = lax.axis_index(axis)
    ahead = count - 1 - place if reverse else place
    gathered = jax.tree.map(lambda a: lax.all_gather(a, axis), part)
    state = jax.tree.map(lambda a, e: jnp.zeros_like(a) + jnp.asarray(e, a.dtype), part, identity)

    def one(hop, state):
        source = count - 1 - hop if reverse else hop
        return combine(
            state, jax.tree.map(lambda a: lax.dynamic_index_in_dim(a, source, 0, False), gathered)
        )

    return lax.fori_loop(0, ahead, one, state)


def matmul(left_side, right_side):
    return jnp.dot(left_side, right_side, preferred_element_type=jnp.float32)


def transpose_left(left_side, right_side):
    return lax.dot_general(
        left_side, right_side, (((0,), (0,)), ((), ())), preferred_element_type=jnp.float32
    )


def transpose_right(left_side, right_side):
    return lax.dot_general(
        left_side, right_side, (((1,), (1,)), ((), ())), preferred_element_type=jnp.float32
    )


def layer_norm(activity, gain_row):
    centre = jnp.mean(activity, axis=-1, keepdims=True)
    centred = activity - centre
    spread = jnp.mean(centred * centred, axis=-1, keepdims=True)
    return centred * lax.rsqrt(spread + eps_norm) * gain_row


def group_norm(activity):
    centre = jnp.mean(activity, axis=-1, keepdims=True)
    centred = activity - centre
    spread = jnp.mean(centred * centred, axis=-1, keepdims=True)
    return centred * lax.rsqrt(spread + eps_norm)


def retain_block(carried, query_slice, key_slice, value_slice, rate_part, flag_part):
    cumulative = jnp.cumsum(rate_part, axis=1)
    started = jnp.cumsum(flag_part)
    block_len = flag_part.shape[0]
    position = jnp.arange(block_len)
    causal_same = (started[:, None] == started[None, :]) & (position[:, None] >= position[None, :])
    log_gap = cumulative[:, :, None] - cumulative[:, None, :]
    weight_matrix = jnp.where(
        causal_same[None], jnp.exp(jnp.where(causal_same[None], log_gap, 0.0)), 0.0
    )
    attention_scores = (
        jnp.einsum("keu,reu->ekr", query_slice, key_slice, precision=maximum_precision)
        * weight_matrix
    )
    within = jnp.einsum("hnm,mhe->nhe", attention_scores, value_slice, precision=maximum_precision)
    before = (started == 0).astype(jnp.float32)
    reach_in = jnp.exp(cumulative) * before[None, :]
    across = jnp.einsum(
        "nhd,hde->nhe", query_slice * reach_in.T[:, :, None], carried, precision=maximum_precision
    )
    last_count = started[-1]
    trailing_weight = (
        jnp.exp(cumulative[:, -1:] - cumulative)
        * (started == last_count).astype(jnp.float32)[None, :]
    )
    keep_factor = jnp.exp(cumulative[:, -1]) * (last_count == 0).astype(jnp.float32)
    zeroed_state = jnp.einsum(
        "ygc,ygs->gcs",
        key_slice * trailing_weight.T[:, :, None],
        value_slice,
        precision=maximum_precision,
    )
    return (keep_factor[:, None, None] * carried + zeroed_state, within + across)


def retain(queries, key_heads, value_heads, log_rates, start_flag, initial):
    block_count = queries.shape[0] // BLK
    head_count = queries.shape[1]
    query_blocks = queries.reshape(block_count, BLK, head_count, queries.shape[2])
    key_blocks = key_heads.reshape(block_count, BLK, head_count, key_heads.shape[2])
    value_blocks = value_heads.reshape(block_count, BLK, head_count, value_heads.shape[2])
    rate_blocks = log_rates.reshape(head_count, block_count, BLK).transpose(1, 0, 2)
    flag_blocks = start_flag.reshape(block_count, BLK)

    def scan_step(carried, block_items):
        return retain_block(carried, *block_items)

    final_state, block_outputs = lax.scan(
        jax.checkpoint(scan_step),
        initial,
        (query_blocks, key_blocks, value_blocks, rate_blocks, flag_blocks),
    )
    return (block_outputs.reshape(block_count * BLK, head_count, value_heads.shape[2]), final_state)


def link_maps(earlier, later):
    return (earlier[0] * later[0], later[0][:, None, None] * earlier[1] + later[1])


def local(
    tokens,
    first_gain,
    query_weight,
    key_weight,
    value_weight,
    gate_weight,
    output_weight,
    second_gain,
    gelu_weight,
    linear_weight,
    down_weight,
    log_decay,
    first_start,
    cotangent,
):
    token_rows = tokens.shape[0]
    head_count = query_weight.shape[1] // DK
    key_scale = 1.0 / math.sqrt(DK)
    position = jnp.arange(token_rows, dtype=jnp.int32)
    start_flag = (position == first_start[0]).astype(jnp.float32)
    before = (position < first_start[0]).astype(jnp.float32)
    reach_in = jnp.exp(jnp.cumsum(log_decay, axis=1)) * before[None, :]
    shard_keep = jnp.exp(jnp.sum(log_decay, axis=1)) * (first_start[0] == token_rows).astype(
        jnp.float32
    )
    empty_state = jnp.zeros((head_count, DK, DV), jnp.float32)
    inputs = tokens.astype(jnp.float32)
    normed_in = layer_norm(inputs, first_gain).astype(jnp.bfloat16)
    queries = matmul(normed_in, query_weight)
    scaled_keys = matmul(normed_in, key_weight) * key_scale
    values = matmul(normed_in, value_weight)
    gate_pre = matmul(normed_in, gate_weight)
    query_heads = queries.reshape(token_rows, head_count, DK)
    key_heads = scaled_keys.reshape(token_rows, head_count, DK)
    value_heads = values.reshape(token_rows, head_count, DV)
    local_out, local_end = retain(
        query_heads, key_heads, value_heads, log_decay, start_flag, empty_state
    )
    weighted_query = query_heads * reach_in.T[:, :, None]
    incoming = carried_in(
        (shard_keep, local_end), "seq", link_maps, (jnp.ones_like(shard_keep), empty_state), False
    )[1]
    retained = local_out + jnp.einsum(
        "nhd,hde->nhe", weighted_query, incoming, precision=maximum_precision
    )

    def gate_mix(gate_in, retained_in):
        return jax.nn.silu(gate_in) * group_norm(retained_in).reshape(token_rows, head_count * DV)

    gated_rows = gate_mix(gate_pre, retained).astype(jnp.bfloat16)
    residual = inputs + lax.psum(matmul(gated_rows, output_weight), "head")
    normed_mid = layer_norm(residual, second_gain).astype(jnp.bfloat16)
    up_gate = matmul(normed_mid, gelu_weight)
    up_proj = matmul(normed_mid, linear_weight)

    def hidden_mix(pre_gate, up_branch):
        return jax.nn.gelu(pre_gate, approximate=False) * up_branch

    hidden = hidden_mix(up_gate, up_proj).astype(jnp.bfloat16)
    result = residual + lax.psum(matmul(hidden, down_weight), "head")
    output_rows = result.astype(jnp.bfloat16)
    grad_hidden = transpose_right(cotangent, down_weight)
    wgrad_down = transpose_left(hidden, cotangent)
    _, hidden_back = jax.vjp(hidden_mix, up_gate, up_proj)
    grad_up_gate, grad_up = hidden_back(grad_hidden)
    grad_up_gate = grad_up_gate.astype(jnp.bfloat16)
    grad_up = grad_up.astype(jnp.bfloat16)
    grad_mid_in = lax.psum(
        transpose_right(grad_up_gate, gelu_weight) + transpose_right(grad_up, linear_weight), "head"
    )
    wgrad_gelu = transpose_left(normed_mid, grad_up_gate)
    wgrad_linear = transpose_left(normed_mid, grad_up)
    _, second_back = jax.vjp(layer_norm, residual, second_gain)
    grad_mid_norm, wgrad_second = second_back(grad_mid_in)
    grad_residual = cotangent.astype(jnp.float32) + grad_mid_norm
    grad_branch = grad_residual.astype(jnp.bfloat16)
    grad_gated = transpose_right(grad_branch, output_weight)
    wgrad_output = transpose_left(gated_rows, grad_branch)
    _, gate_back = jax.vjp(gate_mix, gate_pre, retained)
    grad_gate_pre, grad_retained = gate_back(grad_gated)
    grad_gate_pre = grad_gate_pre.astype(jnp.bfloat16)
    local_in = jnp.einsum(
        "nhd,nhe->hde", weighted_query, grad_retained, precision=maximum_precision
    )
    beyond = carried_in(
        (shard_keep, local_in), "seq", link_maps, (jnp.ones_like(shard_keep), empty_state), True
    )[1]

    def local_retain(query_in, key_in, value_in):
        return retain(query_in, key_in, value_in, log_decay, start_flag, incoming)

    _, retain_back = jax.vjp(local_retain, query_heads, key_heads, value_heads)
    grad_q, grad_k, grad_v = retain_back((grad_retained, beyond))
    grad_queries = grad_q.reshape(token_rows, head_count * DK).astype(jnp.bfloat16)
    grad_keys = (grad_k * key_scale).reshape(token_rows, head_count * DK).astype(jnp.bfloat16)
    grad_values = grad_v.reshape(token_rows, head_count * DV).astype(jnp.bfloat16)
    grad_in = lax.psum(
        transpose_right(grad_queries, query_weight)
        + transpose_right(grad_keys, key_weight)
        + transpose_right(grad_values, value_weight)
        + transpose_right(grad_gate_pre, gate_weight),
        "head",
    )
    wgrad_query = transpose_left(normed_in, grad_queries)
    wgrad_key = transpose_left(normed_in, grad_keys)
    wgrad_value = transpose_left(normed_in, grad_values)
    wgrad_gate = transpose_left(normed_in, grad_gate_pre)
    _, first_back = jax.vjp(layer_norm, inputs, first_gain)
    grad_in_norm, wgrad_first = first_back(grad_in)
    grad_tokens = (grad_residual + grad_in_norm).astype(jnp.bfloat16)
    summed = tuple(
        (
            lax.psum_scatter(wgrad_first, "seq", scatter_dimension=0, tiled=True),
            lax.psum_scatter(wgrad_query, "seq", scatter_dimension=0, tiled=True),
            lax.psum_scatter(wgrad_key, "seq", scatter_dimension=0, tiled=True),
            lax.psum_scatter(wgrad_value, "seq", scatter_dimension=0, tiled=True),
            lax.psum_scatter(wgrad_gate, "seq", scatter_dimension=0, tiled=True),
            lax.psum_scatter(wgrad_output, "seq", scatter_dimension=1, tiled=True),
            lax.psum_scatter(wgrad_second, "seq", scatter_dimension=0, tiled=True),
            lax.psum_scatter(wgrad_gelu, "seq", scatter_dimension=0, tiled=True),
            lax.psum_scatter(wgrad_linear, "seq", scatter_dimension=0, tiled=True),
            lax.psum_scatter(wgrad_down, "seq", scatter_dimension=1, tiled=True),
        )
    )
    return (output_rows, grad_tokens) + summed


def solution(mesh):
    return jax.shard_map(
        local,
        mesh=mesh,
        in_specs=(
            P("seq", None),
            P(),
            P(None, "head"),
            P(None, "head"),
            P(None, "head"),
            P(None, "head"),
            P("head", None),
            P(),
            P(None, "head"),
            P(None, "head"),
            P("head", None),
            P("head", "seq"),
            P("seq"),
            P("seq", None),
        ),
        out_specs=(
            P("seq", None),
            P("seq", None),
            P("seq"),
            P("seq", "head"),
            P("seq", "head"),
            P("seq", "head"),
            P("seq", "head"),
            P("head", "seq"),
            P("seq"),
            P("seq", "head"),
            P("seq", "head"),
            P("head", "seq"),
        ),
        check_vma=False,
    )
```

profile of v0, /device:TPU:0, one launch (start us, length us, event | category | flops | bytes accessed | tf_op | source)
XLA Modules:
  0.0 1682.1 jit_solution(6416357535188683666)
XLA Ops:
  10.5 3.1 convolution_multiply_fusion
  20.2 4.5 fusion.79
  26.8 3.4 convolution_add_fusion.4
  31.9 23.9 %all-reduce = f32[16]{0:T(128)S(1)} all-reduce(f32[16]{0:T(128)S(1)} %multiply_dynamic-update-slice_fusion), channel_id=2, replica_groups=mesh['seq'=8,'head'=4] {'seq'}, use_global_device_ids=true, to_apply=%add | all-reduce | flops 16 | bytes 128
  67.8 90.0 %all-gather.6.cloned.1.call-done = f32[16,256,512]{2,1,0:T(8,128)} async-done(((f32[2,256,512]{2,1,0:T(8,128)}), f32[16,256,512]{2,1,0:T(8,128)}) %all-gather.6.cloned.1.call-update) | async-done | bytes 8388624 | tf_op jit(solution)/shard_map/all_gather | solution.py:21
  159.3 3.6 fusion.87
  164.9 2.5 copy.103
  167.5 5.0 multiply_convert_fusion.3
  173.3 2.6 fusion.88
  175.9 69.1 %all-reduce.9.cloned.1.call-done = f32[256,2048]{1,0:T(8,128)} async-done(((f32[256,2048]{1,0:T(8,128)}), f32[256,2048]{1,0:T(8,128)}) %all-reduce.9.cloned.1.call-update) | async-done | bytes 2097168 | tf_op jit(solution)/shard_map/psum | solution.py:173
  252.7 3.5 multiply_convert_fusion.1
  260.0 2.6 convolution_add_fusion.1
  262.8 51.4 %all-reduce.11.cloned.1.call-done = f32[256,2048]{1,0:T(8,128)} async-done(((f32[256,2048]{1,0:T(8,128)}), f32[256,2048]{1,0:T(8,128)}) %all-reduce.11.cloned.1.call-update) | async-done | bytes 2097168 | tf_op jit(solution)/shard_map/psum | solution.py:190
  314.2 3.0 multiply_reduce_fusion
  321.9 2.8 fusion.62
  324.8 2.5 copy.104
  333.0 3.1 squeeze.85
  336.1 5.1 fusion.90
  341.2 2.7 fusion.94
  343.9 113.8 %all-gather.8.cloned.1.call-done = f32[16,256,512]{2,1,0:T(8,128)} async-done(((f32[2,256,512]{2,1,0:T(8,128)}), f32[16,256,512]{2,1,0:T(8,128)}) %all-gather.8.cloned.1.call-update) | async-done | bytes 8388624 | tf_op jit(solution)/shard_map/all_gather | solution.py:21
  458.8 19.6 %while.17 = (s32[]{:T(128)}, f32[2,256,512]{2,1,0:T(8,128)}, s32[]{:T(128)}, f32[8,2]{1,0:T(8,128)S(1)}, f32[8,2,256,512]{3,2,1,0:T(8,128)}, /*index=5*/s32[]{:T(128)}, s32[]{:T(128)}, s32[]{:T(128)}, s32[]{:T(128)}) while((s32[]{:T(128)}, f32[2,256,512]{2,1,0:T(8,128)}, s32[]{:T(128)}, f32[8,2]{1,0:T(8,128)S(1)}, ...), condition=%wide.region_21.22_spmd, body=%wide.region_20.21_spmd.sunk | while | flops 524294 | bytes 3145899 | solution.py:30
  458.8 2.8 bitcast_add_fusion.5
  461.6 2.8 bitcast_add_fusion.5
  464.4 2.8 bitcast_add_fusion.5
  467.2 2.8 bitcast_add_fusion.5
  470.0 2.8 bitcast_add_fusion.5
  472.8 2.8 bitcast_add_fusion.5
  475.6 2.8 bitcast_add_fusion.5
  483.9 2.9 fusion.16
  502.6 4.5 fusion.96
  508.1 4.5 fusion.97
  514.0 4.5 fusion.98
  519.9 4.5 fusion.95
  525.5 4.7 fusion.68
  531.1 2.8 fusion.72
  534.0 2.9 fusion.74
  537.0 4.6 fusion.70
  542.3 41.8 %all-reduce.13.cloned.1.call-done = (f32[256,2048]{1,0:T(8,128)}, f32[256,2048]{1,0:T(8,128)}) async-done(((f32[256,2048]{1,0:T(8,128)}, f32[256,2048]{1,0:T(8,128)}), (f32[256,2048]{1,0:T(8,128)}, f32[256,2048]{1,0:T(8,128)})) %all-reduce.13.cloned.1.call-update) | async-done | bytes 4194320 | tf_op jit(solution)/shard_map/psum | solution.py:182
  587.3 39.1 %all-reduce.3 = (f32[2048]{0:T(1024)S(1)}, f32[2048]{0:T(1024)S(1)}) all-reduce(f32[2048]{0:T(1024)S(1)} %get-tuple-element.241, f32[2048]{0:T(1024)S(1)} %get-tuple-element.239), channel_id=5, replica_groups=mesh['seq'=8,'head'=4] {'seq'}, use_global_device_ids=true, to_apply=%region_30.31.clone | all-reduce | flops 4096 | bytes 32768
  627.7 3.8 add_convert_fusion.1
  634.0 102.4 %reduce-scatter.19.cloned.1.call-done = f32[256,1024]{1,0:T(8,128)} async-done(((f32[2048,1024]{1,0:T(8,128)}), f32[256,1024]{1,0:T(8,128)}) %reduce-scatter.19.cloned.1.call-update) | async-done | bytes 1048592 | tf_op jit(solution)/shard_map/reduce_scatter | solution.py:242
  736.3 150.8 %reduce-scatter.21.cloned.1.call-done = f32[256,1024]{1,0:T(8,128)} async-done(((f32[2048,1024]{1,0:T(8,128)}), f32[256,1024]{1,0:T(8,128)}) %reduce-scatter.21.cloned.1.call-update) | async-done | bytes 1048592 | tf_op jit(solution)/shard_map/reduce_scatter | solution.py:243
  887.1 151.2 %reduce-scatter.23.cloned.1.call-done = f32[1024,256]{1,0:T(8,128)} async-done(((f32[1024,2048]{1,0:T(8,128)}), f32[1024,256]{1,0:T(8,128)}) %reduce-scatter.23.cloned.1.call-update) | async-done | bytes 1048592 | tf_op jit(solution)/shard_map/reduce_scatter | solution.py:244
  1038.3 151.2 %reduce-scatter.17.cloned.1.call-done = f32[1024,256]{1,0:T(8,128)} async-done(((f32[1024,2048]{1,0:T(8,128)}), f32[1024,256]{1,0:T(8,128)}) %reduce-scatter.17.cloned.1.call-update) | async-done | bytes 1048592 | tf_op jit(solution)/shard_map/reduce_scatter | solution.py:240
  1189.5 150.6 %reduce-scatter.15.cloned.1.call-done = f32[256,1024]{1,0:T(8,128)} async-done(((f32[2048,1024]{1,0:T(8,128)}), f32[256,1024]{1,0:T(8,128)}) %reduce-scatter.15.cloned.1.call-update) | async-done | bytes 1048592 | tf_op jit(solution)/shard_map/reduce_scatter | solution.py:239
  1340.1 91.6 %reduce-scatter.11.cloned.1.call-done = f32[256,512]{1,0:T(8,128)} async-done(((f32[2048,512]{1,0:T(8,128)}), f32[256,512]{1,0:T(8,128)}) %reduce-scatter.11.cloned.1.call-update) | async-done | bytes 524304 | tf_op jit(solution)/shard_map/reduce_scatter | solution.py:237
  1431.8 92.0 %reduce-scatter.9.cloned.1.call-done = f32[256,512]{1,0:T(8,128)} async-done(((f32[2048,512]{1,0:T(8,128)}), f32[256,512]{1,0:T(8,128)}) %reduce-scatter.9.cloned.1.call-update) | async-done | bytes 524304 | tf_op jit(solution)/shard_map/reduce_scatter | solution.py:236
  1523.8 151.3 %reduce-scatter.13.cloned.1.call-done = f32[256,1024]{1,0:T(8,128)} async-done(((f32[2048,1024]{1,0:T(8,128)}), f32[256,1024]{1,0:T(8,128)}) %reduce-scatter.13.cloned.1.call-update) | async-done | bytes 1048592 | tf_op jit(solution)/shard_map/reduce_scatter | solution.py:238
  (244 shorter events, 85.1 us)
Async XLA Ops:
  7.2 48.7 %copy-start = (bf16[2048,512]{1,0:T(8,128)(2,1)S(1)}, bf16[2048,512]{1,0:T(8,128)(2,1)}, u32[]{:S(2)}) copy-start(bf16[2048,512]{1,0:T(8,128)(2,1)} %param.20) | copy-start | bytes 6291460
  7.2 3.3 copy-start.2
  7.2 3.3 copy-start.38
  7.2 150.5 %all-gather.6.cloned.1.call-start = ((), (), s32[]{:S(2)}) async-start(), calls=%async_computation.18 | async-start | bytes 9437184 | tf_op jit(solution)/shard_map/all_gather | solution.py:21
  13.7 5.5 copy-start.48
  24.7 5.8 copy-start.49
  30.3 214.7 %all-reduce.9.cloned.1.call-start = ((), (), s32[]{:S(2)}) async-start(), calls=%async_computation.8 | async-start | bytes 4194304 | tf_op jit(solution)/shard_map/psum | solution.py:173
  61.7 2.1 copy-start.22
  61.8 3.9 copy-start.27
  167.5 5.8 copy-start.51
  175.9 138.3 %all-reduce.11.cloned.1.call-start = ((), (), s32[]{:S(2)}) async-start(), calls=%async_computation.9 | async-start | bytes 4194304 | tf_op jit(solution)/shard_map/psum | solution.py:190
  246.9 2.9 copy-start.50
  249.8 6.4 copy-start.16
  249.8 2.9 copy-start.53
  252.7 3.5 copy-start.31
  256.2 3.7 copy-start.34
  262.6 195.1 %all-gather.8.cloned.1.call-start = ((), (), s32[]{:S(2)}) async-start(), calls=%async_computation.19 | async-start | bytes 9437184 | tf_op jit(solution)/shard_map/all_gather | solution.py:21
  314.2 3.0 copy-start.4
  314.2 3.5 copy-start.26
  317.7 3.6 copy-start.52
  318.9 2.7 copy-start.39
  318.9 3.0 copy-start.56
  319.6 5.1 copy-start.29
  327.3 2.2 copy-start.15
  333.0 251.2 %all-reduce.13.cloned.1.call-start = ((), (), s32[]{:S(2)}) async-start(), calls=%async_computation.20 | async-start | bytes 8388608 | tf_op jit(solution)/shard_map/psum | solution.py:182
  336.1 5.1 copy-start.43
  336.1 5.1 copy-start.54
  483.8 3.0 copy-start.5
  483.8 3.0 copy-start.25
  483.8 4.9 copy-start.10
  483.8 4.9 copy-start.23
  486.8 3.9 copy-start.24
  492.5 5.4 copy-start.32
  494.4 2.2 copy-start.55
  496.6 2.2 copy-start.37
  501.2 235.1 %reduce-scatter.19.cloned.1.call-start = ((), (), s32[]{:S(2)}) async-start(), calls=%async_computation.15 | async-start | bytes 9437184 | tf_op jit(solution)/shard_map/reduce_scatter | solution.py:242
  507.1 380.0 %reduce-scatter.21.cloned.1.call-start = ((), (), s32[]{:S(2)}) async-start(), calls=%async_computation.16 | async-start | bytes 9437184 | tf_op jit(solution)/shard_map/reduce_scatter | solution.py:243
  512.7 525.7 %reduce-scatter.23.cloned.1.call-start = ((), (), s32[]{:S(2)}) async-start(), calls=%async_computation.17 | async-start | bytes 9437184 | tf_op jit(solution)/shard_map/reduce_scatter | solution.py:244
  518.6 670.9 %reduce-scatter.17.cloned.1.call-start = ((), (), s32[]{:S(2)}) async-start(), calls=%async_computation.14 | async-start | bytes 9437184 | tf_op jit(solution)/shard_map/reduce_scatter | solution.py:240
  524.5 815.7 %reduce-scatter.15.cloned.1.call-start = ((), (), s32[]{:S(2)}) async-start(), calls=%async_computation.13 | async-start | bytes 9437184 | tf_op jit(solution)/shard_map/reduce_scatter | solution.py:239
  530.2 901.6 %reduce-scatter.11.cloned.1.call-start = ((), (), s32[]{:S(2)}) async-start(), calls=%async_computation.11 | async-start | bytes 4718592 | tf_op jit(solution)/shard_map/reduce_scatter | solution.py:237
  534.0 989.9 %reduce-scatter.9.cloned.1.call-start = ((), (), s32[]{:S(2)}) async-start(), calls=%async_computation.10 | async-start | bytes 4718592 | tf_op jit(solution)/shard_map/reduce_scatter | solution.py:236
  537.0 1138.2 %reduce-scatter.13.cloned.1.call-start = ((), (), s32[]{:S(2)}) async-start(), calls=%async_computation.12 | async-start | bytes 9437184 | tf_op jit(solution)/shard_map/reduce_scatter | solution.py:238
  584.1 2.2 copy-start.13
  627.7 3.9 copy-start.12
  627.7 3.9 copy-start.14
  627.7 4.4 copy-start.21
  627.7 1047.5 %copy-start.1 = (bf16[2048,512]{1,0:T(8,128)(2,1)S(1)}, bf16[2048,512]{1,0:T(8,128)(2,1)}, u32[]{:S(2)}) copy-start(bf16[2048,512]{1,0:T(8,128)(2,1)} %param.20) | copy-start | bytes 6291460
  (22 other events, 27.7 us)
Sparse Core Ops, SparseCore 0:
  30.4 127.2 all-gather.5
  176.0 68.9 all-reduce.8
  262.7 51.4 all-reduce.10
  333.1 124.5 all-gather.7
  501.4 82.7 all-reduce.12
  588.2 148.0 reduce-scatter.18
  740.5 146.5 reduce-scatter.20
  891.3 146.9 reduce-scatter.22
  1042.5 146.9 reduce-scatter.16
  1193.6 146.5 reduce-scatter.14
  1344.4 87.3 reduce-scatter.10
  1435.8 87.9 reduce-scatter.8
  1528.0 147.0 reduce-scatter.12
where the time goes:
time: 1690 us; the launch traced here: 1680 us
  waiting for transfers between devices  1410 us (83%)
  matrix products  102 us (6%)
  blocking collectives  62.9 us (4%)
  other arithmetic  46.3 us (3%)
  local copies, waits for them, and re-layouts  44.3 us (3%)
  between operations  17.6 us (1%)
    all_gather x2, waiting for transfers between devices, carried_in(): gathered = jax.tree.map(lambda a: lax.all_gather(a, axis), part)  204 us
    reduce_scatter x1, waiting for transfers between devices, local(): lax.psum_scatter(wgrad_value, 'seq', scatter_dimension=0, tiled=True)  151 us
    reduce_scatter x1, waiting for transfers between devices, local(): lax.psum_scatter(wgrad_down, 'seq', scatter_dimension=1, tiled=True)  151 us
    reduce_scatter x1, waiting for transfers between devices, local(): lax.psum_scatter(wgrad_output, 'seq', scatter_dimension=1, tiled=True)  151 us
    reduce_scatter x1, waiting for transfers between devices, local(): lax.psum_scatter(wgrad_linear, 'seq', scatter_dimension=0, tiled=True)  151 us
    reduce_scatter x1, waiting for transfers between devices, local(): lax.psum_scatter(wgrad_gate, 'seq', scatter_dimension=0, tiled=True)  151 us
    reduce_scatter x1, waiting for transfers between devices, local(): lax.psum_scatter(wgrad_gelu, 'seq', scatter_dimension=0, tiled=True)  102 us
    reduce_scatter x1, waiting for transfers between devices, local(): lax.psum_scatter(wgrad_query, 'seq', scatter_dimension=0, tiled=True)  92 us
  transfers between devices with their start and end apart: 13, of which 13 were waited for; matrix products, arithmetic and copies ran while one was open for 4% of the time, Pallas kernels for 0%

commit v1 on v0

--- a/solution.py
+++ b/solution.py
@@ -1,10 +1,16 @@
+import functools
 import math
 
 import jax
 import jax.numpy as jnp
 from jax import lax
+from jax.experimental import pallas as pl
+from jax.experimental.pallas import tpu as pltpu
 from jax.sharding import PartitionSpec as P
 
+
+SEQ = "seq"
+HEAD = "head"
 DK = 256
 DV = 512
 BLK = 256
@@ -119,7 +125,7 @@
     return (earlier[0] * later[0], later[0][:, None, None] * earlier[1] + later[1])
 
 
-def local(
+def local_scatter(
     tokens,
     first_gain,
     query_weight,
@@ -160,7 +166,7 @@
     )
     weighted_query = query_heads * reach_in.T[:, :, None]
     incoming = carried_in(
-        (shard_keep, local_end), "seq", link_maps, (jnp.ones_like(shard_keep), empty_state), False
+        (shard_keep, local_end), SEQ, link_maps, (jnp.ones_like(shard_keep), empty_state), False
     )[1]
     retained = local_out + jnp.einsum(
         "nhd,hde->nhe", weighted_query, incoming, precision=maximum_precision
@@ -170,7 +176,7 @@
         return jax.nn.silu(gate_in) * group_norm(retained_in).reshape(token_rows, head_count * DV)
 
     gated_rows = gate_mix(gate_pre, retained).astype(jnp.bfloat16)
-    residual = inputs + lax.psum(matmul(gated_rows, output_weight), "head")
+    residual = inputs + lax.psum(matmul(gated_rows, output_weight), HEAD)
     normed_mid = layer_norm(residual, second_gain).astype(jnp.bfloat16)
     up_gate = matmul(normed_mid, gelu_weight)
     up_proj = matmul(normed_mid, linear_weight)
@@ -179,7 +185,7 @@
         return jax.nn.gelu(pre_gate, approximate=False) * up_branch
 
     hidden = hidden_mix(up_gate, up_proj).astype(jnp.bfloat16)
-    result = residual + lax.psum(matmul(hidden, down_weight), "head")
+    result = residual + lax.psum(matmul(hidden, down_weight), HEAD)
     output_rows = result.astype(jnp.bfloat16)
     grad_hidden = transpose_right(cotangent, down_weight)
     wgrad_down = transpose_left(hidden, cotangent)
@@ -188,7 +194,7 @@
     grad_up_gate = grad_up_gate.astype(jnp.bfloat16)
     grad_up = grad_up.astype(jnp.bfloat16)
     grad_mid_in = lax.psum(
-        transpose_right(grad_up_gate, gelu_weight) + transpose_right(grad_up, linear_weight), "head"
+        transpose_right(grad_up_gate, gelu_weight) + transpose_right(grad_up, linear_weight), HEAD
     )
     wgrad_gelu = transpose_left(normed_mid, grad_up_gate)
     wgrad_linear = transpose_left(normed_mid, grad_up)
@@ -205,7 +211,7 @@
         "nhd,nhe->hde", weighted_query, grad_retained, precision=maximum_precision
     )
     beyond = carried_in(
-        (shard_keep, local_in), "seq", link_maps, (jnp.ones_like(shard_keep), empty_state), True
+        (shard_keep, local_in), SEQ, link_maps, (jnp.ones_like(shard_keep), empty_state), True
     )[1]
 
     def local_retain(query_in, key_in, value_in):
@@ -221,7 +227,7 @@
         + transpose_right(grad_keys, key_weight)
         + transpose_right(grad_values, value_weight)
         + transpose_right(grad_gate_pre, gate_weight),
-        "head",
+        HEAD,
     )
     wgrad_query = transpose_left(normed_in, grad_queries)
     wgrad_key = transpose_left(normed_in, grad_keys)
@@ -232,19 +238,625 @@
     grad_tokens = (grad_residual + grad_in_norm).astype(jnp.bfloat16)
     summed = tuple(
         (
-            lax.psum_scatter(wgrad_first, "seq", scatter_dimension=0, tiled=True),
-            lax.psum_scatter(wgrad_query, "seq", scatter_dimension=0, tiled=True),
-            lax.psum_scatter(wgrad_key, "seq", scatter_dimension=0, tiled=True),
-            lax.psum_scatter(wgrad_value, "seq", scatter_dimension=0, tiled=True),
-            lax.psum_scatter(wgrad_gate, "seq", scatter_dimension=0, tiled=True),
-            lax.psum_scatter(wgrad_output, "seq", scatter_dimension=1, tiled=True),
-            lax.psum_scatter(wgrad_second, "seq", scatter_dimension=0, tiled=True),
-            lax.psum_scatter(wgrad_gelu, "seq", scatter_dimension=0, tiled=True),
-            lax.psum_scatter(wgrad_linear, "seq", scatter_dimension=0, tiled=True),
-            lax.psum_scatter(wgrad_down, "seq", scatter_dimension=1, tiled=True),
+            lax.psum_scatter(wgrad_first, SEQ, scatter_dimension=0, tiled=True),
+            lax.psum_scatter(wgrad_query, SEQ, scatter_dimension=0, tiled=True),
+            lax.psum_scatter(wgrad_key, SEQ, scatter_dimension=0, tiled=True),
+            lax.psum_scatter(wgrad_value, SEQ, scatter_dimension=0, tiled=True),
+            lax.psum_scatter(wgrad_gate, SEQ, scatter_dimension=0, tiled=True),
+            lax.psum_scatter(wgrad_output, SEQ, scatter_dimension=1, tiled=True),
+            lax.psum_scatter(wgrad_second, SEQ, scatter_dimension=0, tiled=True),
+            lax.psum_scatter(wgrad_gelu, SEQ, scatter_dimension=0, tiled=True),
+            lax.psum_scatter(wgrad_linear, SEQ, scatter_dimension=0, tiled=True),
+            lax.psum_scatter(wgrad_down, SEQ, scatter_dimension=1, tiled=True),
         )
     )
     return (output_rows, grad_tokens) + summed
+
+
+def exchange_sum(rows, axis):
+    count = lax.axis_size(axis)
+    bit = count // 2
+    while bit:
+        rows = rows + lax.ppermute(rows, axis, [(i, i ^ bit) for i in range(count)])
+        bit //= 2
+    return rows
+
+
+CHIP = [(0, 1), (1, 0), (2, 3), (3, 2)]
+ACROSS = [(0, 2), (2, 0), (1, 3), (3, 1)]
+
+
+def of_rows(a, start, size):
+    return lax.dynamic_slice_in_dim(a, start, size, 0)
+
+
+def after(a, *others):
+    return lax.optimization_barrier((a, *others))[0]
+
+
+def head_total(mine, other):
+    other = lax.ppermute(other, HEAD, CHIP)
+    both = mine + other
+    return both + lax.ppermute(both, HEAD, ACROSS)
+
+
+def other_core(a):
+    return lax.ppermute(a, HEAD, CHIP)
+
+
+def ring_order(count):
+    return list(range(0, count, 2)) + list(range(count - 1, 0, -2))
+
+
+def ring_gather(half, split):
+    count = lax.axis_size(SEQ)
+    order = ring_order(count)
+    up = [(order[i], order[(i + 1) % count]) for i in range(count)]
+    down = [(target, source) for source, target in up]
+    steps = []
+    rising = falling = half
+    for hop in range(1, count // 2 + 1):
+        if hop == count // 2:
+            rising, falling = rising[:split], falling[split:]
+        rising, falling = lax.ppermute(rising, SEQ, up), lax.ppermute(falling, SEQ, down)
+        others = other_core(rising), other_core(falling)
+        if hop == count // 2:
+            steps.append([rising, falling, *others])
+        else:
+            steps.append([rising, others[0], falling, others[1]])
+    return steps
+
+
+def ring_slots():
+    count = lax.axis_size(SEQ)
+    index = jnp.arange(count, dtype=jnp.int32)
+
+    def position(shard):
+        return jnp.where(shard % 2 == 0, shard // 2, count - 1 - shard // 2)
+
+    behind = (position(lax.axis_index(SEQ).astype(jnp.int32)) - position(index)) % count
+    steps = jnp.where(behind < count // 2, 2 * behind - 2, 2 * (count - behind) - 1)
+    return jnp.where(behind == 0, count - 2, jnp.where(behind == count // 2, count - 1, steps))
+
+
+def dot_nt(left, right):
+    return lax.dot_general(left, right, (((1,), (1,)), ((), ())), preferred_element_type=jnp.float32)
+
+
+def dot_tn(left, right):
+    return lax.dot_general(left, right, (((0,), (0,)), ((), ())), preferred_element_type=jnp.float32)
+
+
+def dot_nn(left, right):
+    return lax.dot_general(left, right, (((1,), (0,)), ((), ())), preferred_element_type=jnp.float32)
+
+
+def split_dot(left, right, dot):
+    left_high, right_high = left.astype(jnp.bfloat16), right.astype(jnp.bfloat16)
+    left_low = (left - left_high.astype(jnp.float32)).astype(jnp.bfloat16)
+    right_low = (right - right_high.astype(jnp.float32)).astype(jnp.bfloat16)
+    return dot(left_high, right_high) + (dot(left_low, right_high) + dot(left_high, right_low))
+
+
+def half_split_dot(left, right, dot):
+    left_high = left.astype(jnp.bfloat16)
+    left_low = (left - left_high.astype(jnp.float32)).astype(jnp.bfloat16)
+    return dot(left_high, right) + dot(left_low, right)
+
+
+def norm_parts(retained):
+    centre = jnp.mean(retained, axis=-1, keepdims=True)
+    centred = retained - centre
+    inverse = lax.rsqrt(jnp.mean(centred * centred, axis=-1, keepdims=True) + eps_norm)
+    return centred * inverse, inverse
+
+
+def norm_start_kernel(core_ref, first_ref, tokens_ref, gain_ref, rates_ref, normed_ref, half_ref):
+    half = tokens_ref.shape[0] // 2
+    for index, core in enumerate((core_ref[0], 1 - core_ref[0])):
+        rows = tokens_ref[pl.ds(pl.multiple_of(core * half, half), half), :].astype(jnp.float32)
+        normed = (norm_parts(rows)[0] * gain_ref[...]).astype(jnp.bfloat16)
+        normed_ref[index * half : (index + 1) * half, :] = normed
+        if index == 0:
+            half_ref[:half, :] = normed.astype(jnp.float32)
+    heads, size = rates_ref.shape
+    half_ref[half:, :] = jnp.full((8, half_ref.shape[1]), first_ref[0], jnp.int32).astype(jnp.float32)
+    for head in range(heads):
+        half_ref[half : half + 1, head * size : (head + 1) * size] = rates_ref[head : head + 1, :]
+
+
+def norm_start(core, first_start, tokens, gain, log_decay):
+    rows, width = tokens.shape
+    vmem, smem = pl.BlockSpec(memory_space=pltpu.VMEM), pl.BlockSpec(memory_space=pltpu.SMEM)
+    return pl.pallas_call(
+        norm_start_kernel,
+        in_specs=[smem, smem, vmem, vmem, vmem],
+        out_specs=[vmem, vmem],
+        out_shape=[
+            jax.ShapeDtypeStruct((rows, width), jnp.bfloat16),
+            jax.ShapeDtypeStruct((rows // 2 + 8, width), jnp.float32),
+        ],
+        name="norm_start",
+    )(core[None], first_start, tokens, gain[None], log_decay)
+
+
+def gain_part_kernel(core_ref, tokens_ref, mine_ref, other_ref, out_ref):
+    half = mine_ref.shape[0]
+    total = jnp.zeros(out_ref.shape, jnp.float32)
+    for grad_ref, core in ((mine_ref, core_ref[0]), (other_ref, 1 - core_ref[0])):
+        rows = tokens_ref[pl.ds(pl.multiple_of(core * half, half), half), :].astype(jnp.float32)
+        total = total + jnp.sum(grad_ref[...] * norm_parts(rows)[0], axis=0, keepdims=True)
+    out_ref[...] = total
+
+
+def gain_part(core, tokens, mine, other):
+    vmem, smem = pl.BlockSpec(memory_space=pltpu.VMEM), pl.BlockSpec(memory_space=pltpu.SMEM)
+    return pl.pallas_call(
+        gain_part_kernel,
+        in_specs=[smem, vmem, vmem, vmem],
+        out_specs=vmem,
+        out_shape=jax.ShapeDtypeStruct((1, tokens.shape[1]), jnp.float32),
+        cost_estimate=pl.CostEstimate(flops=10 * tokens.size, bytes_accessed=6 * tokens.size, transcendentals=0),
+        name="gain_part",
+    )(core[None], tokens, mine, other)
+
+
+def rows_product_kernel(parts, weights, tiles, scales, turned, shard_ref, *refs):
+    part_refs, slab_refs = refs[:parts], refs[parts : 2 * parts]
+    weight_refs = refs[2 * parts : 2 * parts + weights]
+    outs = refs[len(refs) - weights - 2 : len(refs) - 1]
+    x = refs[-1]
+    step = pl.program_id(0)
+    size = x.shape[0] // parts
+
+    @pl.when(step == 0)
+    def _():
+        for index in range(parts):
+            at = slice(index * size, (index + 1) * size)
+            x[at, :] = part_refs[index][...].astype(jnp.bfloat16)
+            outs[0][at, :] = slab_refs[index][...].astype(jnp.bfloat16)
+
+    start = 0
+    for weight, out, count, scale in zip(weight_refs, outs[1:], tiles, scales):
+
+        @pl.when((step >= start) & (step < start + count))
+        def _(weight=weight, out=out, scale=scale):
+            found = (dot_nt if turned else dot_nn)(x[...], weight[...])
+            out[...] = (found * scale if scale != 1.0 else found).astype(out.dtype)
+
+        start += count
+
+
+def rows_product(parts, size, weights, kinds, scales, turned, shard, block, total, buffers=None):
+    count, width = len(parts), parts[0].shape[1]
+    rows = count * size
+    tile = 512
+    columns = [w.shape[0] if turned else w.shape[1] for w in weights]
+    tiles = [c // tile for c in columns]
+    starts = [sum(tiles[:i]) for i in range(len(tiles))]
+    slab = width // lax.axis_size(SEQ)
+
+    def at(j, start, number):
+        return jnp.clip(j - start, 0, number - 1)
+
+    in_specs = [pl.BlockSpec((size, width), lambda j, s: (0, 0)) for _ in parts]
+    in_specs += [pl.BlockSpec((size, slab), lambda j, s: (0, s[0])) for _ in parts]
+    for start, number in zip(starts, tiles):
+        if turned:
+            in_specs.append(pl.BlockSpec((tile, width), lambda j, s, a=start, n=number: (at(j, a, n), 0)))
+        else:
+            in_specs.append(pl.BlockSpec((width, tile), lambda j, s, a=start, n=number: (0, at(j, a, n))))
+    out_specs = [pl.BlockSpec((rows, slab), lambda j, s: (block, 0))]
+    for start, number in zip(starts, tiles):
+        out_specs.append(pl.BlockSpec((rows, tile), lambda j, s, a=start, n=number: (block, at(j, a, n))))
+    out_shape = [jax.ShapeDtypeStruct((total, slab), jnp.bfloat16)]
+    out_shape += [jax.ShapeDtypeStruct((total, c), kind) for c, kind in zip(columns, kinds)]
+    operands = [*parts, *parts, *weights]
+    aliases = {}
+    if buffers is not None:
+        aliases = {1 + len(operands) + i: i for i in range(len(buffers))}
+        in_specs += [pl.BlockSpec(memory_space=pl.ANY)] * len(buffers)
+        operands += buffers
+    return pl.pallas_call(
+        functools.partial(rows_product_kernel, count, len(weights), tiles, scales, turned),
+        grid_spec=pltpu.PrefetchScalarGridSpec(
+            num_scalar_prefetch=1,
+            grid=(sum(tiles),),
+            in_specs=in_specs,
+            out_specs=out_specs,
+            scratch_shapes=[pltpu.VMEM((rows, width), jnp.bfloat16)],
+        ),
+        out_shape=out_shape,
+        input_output_aliases=aliases,
+        cost_estimate=pl.CostEstimate(
+            flops=2 * rows * width * sum(columns),
+            bytes_accessed=4 * rows * width + 2 * width * sum(columns) + 4 * rows * sum(columns),
+            transcendentals=0,
+        ),
+        name="rows_product",
+    )(shard[None], *operands)
+
+
+def round_rows_kernel(*refs):
+    out = refs[-1]
+    at = 0
+    for part in refs[:-1]:
+        size = part.shape[0]
+        out[at : at + size, :] = (2.0 * part[...]).astype(jnp.bfloat16)
+        at += size
+
+
+def round_rows(parts):
+    vmem = pl.BlockSpec(memory_space=pltpu.VMEM)
+    rows, width = sum(part.shape[0] for part in parts), parts[0].shape[1]
+    return pl.pallas_call(
+        round_rows_kernel,
+        in_specs=[vmem] * len(parts),
+        out_specs=vmem,
+        out_shape=jax.ShapeDtypeStruct((rows, width), jnp.bfloat16),
+        cost_estimate=pl.CostEstimate(flops=rows * width, bytes_accessed=6 * rows * width, transcendentals=0),
+        name="round_rows",
+    )(*parts)
+
+
+def causal(first, places):
+    size = places.shape[1]
+    column = jnp.broadcast_to(places, (size, size))
+    row = column.T
+    return (row >= column) & ((column >= first) | (row < first)), row
+
+
+def block_decay(rates, first, seen, row):
+    size = rates.shape[1]
+    nth = lax.broadcasted_iota(jnp.int32, (size, size), 1).astype(jnp.float32)
+    per_row = jnp.sum(jnp.where(nth <= row, rates, 0.0), axis=1, keepdims=True)
+    down = jnp.broadcast_to(per_row, (size, size))
+    weights = jnp.exp(jnp.where(seen, down - down.T, -jnp.inf))
+    place = row[:, :1]
+    last = jnp.sum(rates, axis=1, keepdims=True)
+    whole = first >= size
+    reach = jnp.where(place < first, jnp.exp(per_row), 0.0)
+    trail = jnp.where((place >= first) | whole, jnp.exp(last - per_row), 0.0)
+    keep = jnp.where(whole, jnp.exp(last), 0.0)
+    return weights, reach, trail, keep
+
+
+def head_lanes(head):
+    return slice(head * DK, (head + 1) * DK), slice(head * DV, (head + 1) * DV), slice(head * BLK, (head + 1) * BLK)
+
+
+def retain_forward_kernel(
+    slot_ref, info_ref, places_ref, q_ref, k_ref, v_ref, gate_ref, retained_ref, gated_ref, state_ref, state
+):
+    @pl.when(pl.program_id(0) == 0)
+    def _():
+        state[...] = jnp.zeros_like(state)
+
+    first = info_ref[0, 1:2, :1]
+    seen, row = causal(first, places_ref[...])
+    for head in range(state.shape[0]):
+        key, val, lane = head_lanes(head)
+        weights, reach, trail, keep = block_decay(info_ref[0, 0:1, lane], first, seen, row)
+        q, k, v = q_ref[:, key], k_ref[:, key], v_ref[:, val]
+        held = state[head].astype(jnp.bfloat16)
+        state_ref[head, 0] = held
+        scores = (split_dot(q, k, dot_nt) * weights).astype(jnp.bfloat16)
+        retained = dot_nn(scores, v) + reach * dot_nn(q.astype(jnp.bfloat16), held)
+        state[head] = keep * state[head] + dot_tn((k * trail).astype(jnp.bfloat16), v)
+        retained_ref[:, val] = retained
+        normed, _ = norm_parts(retained)
+        gate = gate_ref[:, val]
+        gated_ref[:, val] = (gate * jax.nn.sigmoid(gate) * normed).astype(jnp.bfloat16)
+
+
+def retain_backward_kernel(
+    slot_ref, info_ref, places_ref, q_ref, k_ref, v_ref, gate_ref, retained_ref, state_ref, up_ref,
+    dq_ref, dk_ref, dv_ref, dgate_ref, beyond,
+):
+    @pl.when(pl.program_id(0) == 0)
+    def _():
+        beyond[...] = jnp.zeros_like(beyond)
+
+    first = info_ref[0, 1:2, :1]
+    seen, row = causal(first, places_ref[...])
+    for head in range(beyond.shape[0]):
+        key, val, lane = head_lanes(head)
+        weights, reach, trail, keep = block_decay(info_ref[0, 0:1, lane], first, seen, row)
+        q, k, v = q_ref[:, key], k_ref[:, key], v_ref[:, val]
+        gate, up = gate_ref[:, val], up_ref[:, val]
+        normed, inverse = norm_parts(retained_ref[:, val])
+        sig = jax.nn.sigmoid(gate)
+        silu = gate * sig
+        dgate_ref[:, val] = (up * normed * (sig + silu * (1.0 - sig))).astype(jnp.bfloat16)
+        g = up * silu
+        mean_g = jnp.mean(g, axis=-1, keepdims=True)
+        mean_gn = jnp.mean(g * normed, axis=-1, keepdims=True)
+        grad = (g - mean_g - normed * mean_gn) * inverse
+        after_block = beyond[head].astype(jnp.bfloat16)
+        scores = (split_dot(q, k, dot_nt) * weights).astype(jnp.bfloat16)
+        dscores = (half_split_dot(grad, v, dot_nt) * weights).astype(jnp.bfloat16)
+        grad = grad.astype(jnp.bfloat16)
+        q_reach = (q * reach).astype(jnp.bfloat16)
+        q, k = q.astype(jnp.bfloat16), k.astype(jnp.bfloat16)
+        dq_ref[:, key] = (dot_nn(dscores, k) + reach * dot_nt(grad, state_ref[head, 0])).astype(jnp.bfloat16)
+        dk = dot_tn(dscores, q) + trail * dot_nt(v, after_block)
+        dk_ref[:, key] = (dk * (1.0 / math.sqrt(DK))).astype(jnp.bfloat16)
+        dv_ref[:, val] = (dot_tn(scores, grad) + trail * dot_nn(k, after_block)).astype(jnp.bfloat16)
+        beyond[head] = keep * beyond[head] + dot_tn(q_reach, grad)
+
+
+def retain_specs(heads, blocks, width, reverse):
+    at = (lambda b: blocks - 1 - b) if reverse else (lambda b: b)
+    info = pl.BlockSpec((1, 8, width), lambda b, slot: (slot[at(b)], 0, 0))
+    places = pl.BlockSpec((1, BLK), lambda b, slot: (0, 0))
+    key = pl.BlockSpec((BLK, heads * DK), lambda b, slot: (slot[at(b)], 0))
+    val = pl.BlockSpec((BLK, heads * DV), lambda b, slot: (slot[at(b)], 0))
+    state = pl.BlockSpec((heads, 1, DK, DV), lambda b, slot: (0, at(b), 0, 0))
+    return info, places, key, val, state
+
+
+def retain_forward(slot, info, places, q, k, v, gate):
+    rows, heads = q.shape[0], q.shape[1] // DK
+    blocks = rows // BLK
+    info_at, places_at, key, val, state = retain_specs(heads, blocks, info.shape[2], False)
+    return pl.pallas_call(
+        retain_forward_kernel,
+        grid_spec=pltpu.PrefetchScalarGridSpec(
+            num_scalar_prefetch=1,
+            grid=(blocks,),
+            in_specs=[info_at, places_at, key, key, val, val],
+            out_specs=[val, val, state],
+            scratch_shapes=[pltpu.VMEM((heads, DK, DV), jnp.float32)],
+        ),
+        out_shape=[
+            jax.ShapeDtypeStruct((rows, heads * DV), jnp.float32),
+            jax.ShapeDtypeStruct((rows, heads * DV), jnp.bfloat16),
+            jax.ShapeDtypeStruct((heads, blocks, DK, DV), jnp.bfloat16),
+        ],
+        cost_estimate=pl.CostEstimate(
+            flops=2 * heads * rows * (BLK * (3 * DK + DV) + 2 * DK * DV),
+            bytes_accessed=rows * heads * (8 * DK + 12 * DV),
+            transcendentals=rows * heads * (BLK + DV),
+        ),
+        name="retain_forward",
+    )(slot, info, places, q, k, v, gate)
+
+
+def retain_backward(slot, info, places, q, k, v, gate, retained, states, up):
+    rows, heads = q.shape[0], q.shape[1] // DK
+    blocks = rows // BLK
+    info_at, places_at, key, val, state = retain_specs(heads, blocks, info.shape[2], True)
+    return pl.pallas_call(
+        retain_backward_kernel,
+        grid_spec=pltpu.PrefetchScalarGridSpec(
+            num_scalar_prefetch=1,
+            grid=(blocks,),
+            in_specs=[info_at, places_at, key, key, val, val, val, state, val],
+            out_specs=[key, key, val, val],
+            scratch_shapes=[pltpu.VMEM((heads, DK, DV), jnp.float32)],
+        ),
+        out_shape=[
+            jax.ShapeDtypeStruct((rows, heads * DK), jnp.bfloat16),
+            jax.ShapeDtypeStruct((rows, heads * DK), jnp.bfloat16),
+            jax.ShapeDtypeStruct((rows, heads * DV), jnp.bfloat16),
+            jax.ShapeDtypeStruct((rows, heads * DV), jnp.bfloat16),
+        ],
+        cost_estimate=pl.CostEstimate(
+            flops=2 * heads * rows * (BLK * (5 * DK + 3 * DV) + 4 * DK * DV),
+            bytes_accessed=rows * heads * (12 * DK + 20 * DV),
+            transcendentals=rows * heads * (BLK + DV),
+        ),
+        name="retain_backward",
+    )(slot, info, places, q, k, v, gate, retained, states, up)
+
+
+def norm_grad(grad, gain, centred_unit, inverse):
+    e = grad * gain
+    mean_e = jnp.mean(e, axis=-1, keepdims=True)
+    mean_en = jnp.mean(e * centred_unit, axis=-1, keepdims=True)
+    return (e - mean_e - centred_unit * mean_en) * inverse
+
+
+def local_gather(
+    tokens,
+    first_gain,
+    query_weight,
+    key_weight,
+    value_weight,
+    gate_weight,
+    output_weight,
+    second_gain,
+    gelu_weight,
+    linear_weight,
+    down_weight,
+    log_decay,
+    first_start,
+    cotangent,
+):
+    bf16, f32 = jnp.bfloat16, jnp.float32
+    shards = lax.axis_size(SEQ)
+    shard, group = lax.axis_index(SEQ), lax.axis_index(HEAD)
+    rows, width = tokens.shape
+    half = rows // 2
+    total = shards * rows
+    own = (shards - 2) * rows
+    quarter = half // 2
+    slab = width // shards
+    key_scale = 1.0 / math.sqrt(DK)
+    chip, core = (group // 2).astype(jnp.int32), (group % 2).astype(jnp.int32)
+    place = shard.astype(jnp.int32)
+
+    def narrow(a):
+        return (2.0 * a).astype(bf16)
+
+    def slab_of(a, at):
+        return lax.dynamic_slice_in_dim(a, at * slab, slab, 1)
+
+    def in_order(mine, other):
+        return jnp.where(core == 0, jnp.concatenate([mine, other]), jnp.concatenate([other, mine]))
+
+    def far_hops():
+        return [[(i, (i + hop) % shards) for i in range(shards)] for hop in range(2, shards, 2)]
+
+    def over_steps(own_rows, steps, weights, kinds, scales, turned):
+        common = (weights, kinds, scales, turned, place)
+        found = rows_product([own_rows], rows, *common, shards - 2, total)
+        for index, parts in enumerate(steps):
+            last = index + 1 == len(steps)
+            found = rows_product(parts, quarter if last else half, *common, shards - 1 if last else index, total, found)
+        return found
+
+    normed_own, normed_half = norm_start(core, first_start, tokens, first_gain, log_decay)
+    came = ring_gather(normed_half, quarter)
+    info = [item[half:] for step in came[:-1] for item in (step[0], step[2])]
+    info = jnp.stack(info + [normed_half[half:], came[-1][1][quarter:]])
+    slot = ring_slots()
+    lanes = jnp.arange(half)
+    places = jnp.concatenate([core * half + lanes, (1 - core) * half + lanes]).astype(f32)[None]
+
+    cotangent_half = of_rows(cotangent, core * half, half)
+    cotangent_own = jnp.concatenate([cotangent_half, of_rows(cotangent, (1 - core) * half, half)], axis=0)
+    cotangent_half = cotangent_half.astype(f32)
+    token_half = of_rows(tokens, core * half, half).astype(f32)
+    first_unit, first_inverse = norm_parts(token_half)
+
+    def far_start(share):
+        share = of_rows(share, chip * quarter, quarter)
+        return [lax.ppermute(share, SEQ, hop) for hop in far_hops()]
+
+    def far_parts(came):
+        parts = []
+        for item in came:
+            both = [item, lax.ppermute(item, HEAD, ACROSS)]
+            parts += both + [other_core(part) for part in both]
+        return parts
+
+    cotangent_far = far_start(after(0.5 * cotangent_half, came[-1][0]))
+    cotangent_far = far_parts(cotangent_far)
+    cotangent_far = round_rows(cotangent_far)
+
+    in_slab, queries, keys, values, gate_pre = over_steps(
+        normed_own,
+        came,
+        [query_weight, key_weight, value_weight, gate_weight],
+        [f32, f32, bf16, f32],
+        [1.0, key_scale, 1.0, 1.0],
+        False,
+    )
+    retained, gated, states = retain_forward(slot, info, places, queries, keys, values, gate_pre)
+
+    out_other = matmul(gated[own + half : own + rows], output_weight)
+    out_mine = matmul(gated[own : own + half], output_weight)
+    residual = token_half + head_total(out_mine, out_other)
+    mid_unit, mid_inverse = norm_parts(residual)
+    normed_mid_half = 0.5 * (mid_unit * second_gain)
+    normed_mid_own = narrow(jnp.concatenate([normed_mid_half, other_core(normed_mid_half)], axis=0))
+    mid_far = far_start(normed_mid_half)
+
+    def hidden_mix(pre_gate, up_branch):
+        return jax.nn.gelu(pre_gate, approximate=False) * up_branch
+
+    def feed_forward(normed, grad_hidden):
+        up_gate = matmul(normed, gelu_weight)
+        up_proj = matmul(normed, linear_weight)
+        hidden, back = jax.vjp(hidden_mix, up_gate, up_proj)
+        grad_up_gate, grad_up = back(grad_hidden)
+        return hidden.astype(bf16), grad_up_gate.astype(bf16), grad_up.astype(bf16)
+
+    hidden, grad_up_gate, grad_up = feed_forward(normed_mid_own, transpose_right(cotangent_own, down_weight))
+
+    def mid_part(at):
+        return transpose_right(grad_up_gate[at : at + half], gelu_weight) + transpose_right(
+            grad_up[at : at + half], linear_weight
+        )
+
+    mid_other = mid_part(half)
+    mid_mine = mid_part(0)
+    grad_mid = head_total(mid_mine, mid_other)
+    grad_residual = cotangent_half + norm_grad(grad_mid, second_gain, mid_unit, mid_inverse)
+    second_part = 0.5 * jnp.sum(grad_mid * mid_unit, axis=0)
+    branch_came = ring_gather(grad_residual, quarter)
+    branch_slab, grad_gated = over_steps(
+        jnp.concatenate([grad_residual, other_core(grad_residual)], axis=0), branch_came, [output_weight], [f32], [1.0], True
+    )
+
+    mid_far = far_parts(mid_far)
+    grad_hidden_far = transpose_right(cotangent_far, down_weight)
+    normed_mid_far = round_rows(mid_far)
+    hidden_far, grad_up_gate_far, grad_up_far = feed_forward(normed_mid_far, grad_hidden_far)
+
+    res_other = matmul(hidden[half:], down_weight)
+    res_mine = matmul(hidden[:half], down_weight)
+    result = 0.5 * (after(residual, branch_came[1][0]) + head_total(res_mine, res_other))
+    output_rows = narrow(in_order(result, other_core(result)))
+
+    def pair_slab(a):
+        return lax.dynamic_slice_in_dim(a, shard // 2 * (2 * slab), 2 * slab, 1)
+
+    def pair_sum(left, right, left_far, right_far, dim):
+        found = transpose_left(left, right)
+        found = found + transpose_left(left_far, right_far)
+        kept = lax.dynamic_slice_in_dim(found, shard % 2 * slab, slab, dim)
+        sent = lax.dynamic_slice_in_dim(found, (1 - shard % 2) * slab, slab, dim)
+        sent = lax.ppermute(after(sent, branch_came[-1][0]), SEQ, [(i, i ^ 1) for i in range(shards)])
+        return kept + sent
+
+    mid_slab, mid_slab_far = pair_slab(normed_mid_own), pair_slab(normed_mid_far)
+    wgrad_down = pair_sum(hidden, pair_slab(cotangent_own), hidden_far, pair_slab(cotangent_far), 1)
+    wgrad_gelu = pair_sum(mid_slab, grad_up_gate, mid_slab_far, grad_up_gate_far, 0)
+    wgrad_linear = pair_sum(mid_slab, grad_up, mid_slab_far, grad_up_far, 0)
+
+    wgrad_output = transpose_left(gated, branch_slab)
+    grad_queries, grad_keys, grad_values, grad_gate_pre = retain_backward(
+        slot, info, places, queries, keys, values, gate_pre, retained, states, grad_gated
+    )
+
+    def in_part(at):
+        at = slice(own + at, own + at + half)
+        return (
+            transpose_right(grad_queries[at], query_weight)
+            + transpose_right(grad_keys[at], key_weight)
+            + transpose_right(grad_values[at], value_weight)
+            + transpose_right(grad_gate_pre[at], gate_weight)
+        )
+
+    in_other = in_part(half)
+    in_mine = in_part(0)
+    grad_in = head_total(in_mine, in_other)
+    wgrad_query = transpose_left(in_slab, grad_queries)
+    wgrad_key = transpose_left(in_slab, grad_keys)
+    wgrad_value = transpose_left(in_slab, grad_values)
+    wgrad_gate = transpose_left(in_slab, grad_gate_pre)
+    first_part = gain_part(core, tokens, in_mine, in_other)
+    gains = exchange_sum(jnp.concatenate([first_part, second_part[None]]), SEQ)
+    gains = gains + other_core(gains)
+    grad_half = 0.5 * (grad_residual + norm_grad(grad_in, first_gain, first_unit, first_inverse))
+    grad_tokens = narrow(in_order(grad_half, other_core(grad_half)))
+    gains = after(gains, grad_in)
+    gains = slab_of(gains + lax.ppermute(gains, HEAD, ACROSS), shard)
+    return (
+        output_rows,
+        grad_tokens,
+        gains[0],
+        wgrad_query,
+        wgrad_key,
+        wgrad_value,
+        wgrad_gate,
+        wgrad_output,
+        gains[1],
+        wgrad_gelu,
+        wgrad_linear,
+        wgrad_down,
+    )
+
+
+def local(*arrays):
+    tokens = lax.axis_size(SEQ) * arrays[0].shape[0]
+    columns = sum(w.shape[1] for w in (*arrays[2:6], *arrays[8:10])) + arrays[6].shape[0] + arrays[10].shape[0]
+    shards, groups = lax.axis_size(SEQ), lax.axis_size(HEAD)
+    if groups == 4 and shards % 2 == 0 and arrays[0].shape[0] == BLK and 4 * tokens <= groups * columns:
+        return local_gather(*arrays)
+    return local_scatter(*arrays)
 
 
 def solution(mesh):
@@ -252,34 +864,34 @@
         local,
         mesh=mesh,
         in_specs=(
-            P("seq", None),
+            P(SEQ, None),
             P(),
-            P(None, "head"),
-            P(None, "head"),
-            P(None, "head"),
-            P(None, "head"),
-            P("head", None),
+            P(None, HEAD),
+            P(None, HEAD),
+            P(None, HEAD),
+            P(None, HEAD),
+            P(HEAD, None),
             P(),
-            P(None, "head"),
-            P(None, "head"),
-            P("head", None),
-            P("head", "seq"),
-            P("seq"),
-            P("seq", None),
+            P(None, HEAD),
+            P(None, HEAD),
+            P(HEAD, None),
+            P(HEAD, SEQ),
+            P(SEQ),
+            P(SEQ, None),
         ),
         out_specs=(
-            P("seq", None),
-            P("seq", None),
-            P("seq"),
-            P("seq", "head"),
-            P("seq", "head"),
-            P("seq", "head"),
-            P("seq", "head"),
-            P("head", "seq"),
-            P("seq"),
-            P("seq", "head"),
-            P("seq", "head"),
-            P("head", "seq"),
+            P(SEQ, None),
+            P(SEQ, None),
+            P(SEQ),
+            P(SEQ, HEAD),
+            P(SEQ, HEAD),
+            P(SEQ, HEAD),
+            P(SEQ, HEAD),
+            P(HEAD, SEQ),
+            P(SEQ),
+            P(SEQ, HEAD),
+            P(SEQ, HEAD),
+            P(HEAD, SEQ),
         ),
         check_vma=False,
     )

time: 1690 us -> 593 us (0.35)
  waiting for transfers between devices: 1410 us -> 207 us
  Pallas kernels: 0 us -> 162 us
  starting transfers between devices: 0.71 us -> 69.3 us
  blocking collectives: 62.9 us -> 0 us
  other arithmetic: 46.3 us -> 22.1 us
    reduce_scatter x8 -> x0, waiting for transfers between devices: 1040 us -> none  [the longest x1 151 us: local(): lax.psum_scatter(wgrad_value, 'seq', scatter_dimension=0, tiled=True)]
    ppermute x0 -> x76, waiting for transfers between devices: none -> 207 us  [the longest x8 77.6 us: ring_gather(): lax.ppermute(rising, SEQ, up)]
    all_gather x2 -> x0, waiting for transfers between devices: 204 us -> none  [carried_in(): gathered = jax.tree.map(lambda a: lax.all_gather(a, axis), part)]
    psum x3 -> x0, waiting for transfers between devices: 162 us -> none  [the longest x1 69.1 us: local(): residual = inputs + lax.psum(matmul(gated_rows, output_weight), 'head')]
    pallas_call x0 -> x16, Pallas kernels: none -> 162 us  [the longest x10 99.3 us: rows_product(): pl.pallas_call(functools.partial(rows_product_kernel, count, len(weights)...]
    ppermute x0 -> x76, starting transfers between devices: none -> 69.3 us  [the longest x8 20.9 us: ring_gather(): lax.ppermute(rising, SEQ, up)]
    unnamed x2 -> x0, blocking collectives: 62.9 us -> none
    dot_general x14 -> x0, matrix products: 26.6 us -> none  [the longest x3 8.24 us: retain_block(): jnp.einsum('ygc,ygs->gcs', key_slice * trailing_weight.T[:, :, None], val...]
  transfers between devices with their start and end apart: 13 -> 76, of which waited for: 13 -> 20; matrix products, arithmetic and copies ran while one was open for 4% -> 22% of each run, Pallas kernels for 0% -> 22%
where the time goes in v1:
time: 593 us; the launch traced here: 587 us
  waiting for transfers between devices  207 us (35%)
  Pallas kernels  162 us (27%)
  matrix products  94.9 us (16%)
  starting transfers between devices  69.3 us (12%)
  local copies, waits for them, and re-layouts  28.9 us (5%)
  other arithmetic  22.1 us (4%)
    pallas_call x10, Pallas kernels, rows_product(): pl.pallas_call(functools.partial(rows_product_kernel, count, len(weights)...  99.3 us
    ppermute x8, waiting for transfers between devices, ring_gather(): lax.ppermute(rising, SEQ, up)  77.6 us
    ppermute x6, waiting for transfers between devices, far_start(): return [lax.ppermute(share, SEQ, hop) for hop in far_hops()]  57.7 us
    dot_general x14, matrix products, transpose_right(): lax.dot_general(left_side, right_side, (((1,), (1,)), ((), ())), preferre...  38.9 us
    dot_general x8, matrix products, matmul(): return jnp.dot(left_side, right_side, preferred_element_type=jnp.float32)  34 us
    ppermute x4, waiting for transfers between devices, head_total(): return both + lax.ppermute(both, HEAD, ACROSS)  34 us
    pallas_call x1, Pallas kernels, retain_backward(): pl.pallas_call(retain_backward_kernel, grid_spec=pltpu.PrefetchScalarGrid...  28 us
    ppermute x6, waiting for transfers between devices, far_parts(): both = [item, lax.ppermute(item, HEAD, ACROSS)]  26.4 us
  transfers between devices with their start and end apart: 76, of which 20 were waited for; matrix products, arithmetic and copies ran while one was open for 22% of the time, Pallas kernels for 22%

profile of v1, /device:TPU:0, one launch (start us, length us, event | category | flops | bytes accessed | tf_op | source)
XLA Modules:
  0.0 586.7 jit_solution(7543855315882416012)
XLA Ops:
  1.3 3.3 norm_start.1
  4.6 3.1 collective-permute-start
  8.8 23.5 %collective-permute-done.refs_0_.refs_4_ = f32[136,2048]{1,0:T(8,128)S(1)} collective-permute-done((f32[136,2048]{1,0:T(8,128)}, f32[136,2048]{1,0:T(8,128)S(1)}, u32[]{:S(2)}, u32[]{:S(2)}) %collective-permute-start) | collective-permute-done | bytes 1114144 | tf_op jit(solution)/shard_map/ppermute | solution.py:301
  34.4 11.3 %rows_product.10 = (bf16[2048,256]{1,0:T(8,128)(2,1)}, f32[2048,512]{1,0:T(8,128)}, f32[2048,512]{1,0:T(8,128)}, bf16[2048,1024]{1,0:T(8,128)(2,1)}, f32[2048,1024]{1,0:T(8,128)}) custom-call(s32[1]{0:T(128)} %bitcast.12.shard_ref, bf16[256,2048]{1,0:T(8,128)(2,1)} %get-tuple-element.63.refs_0_.refs_1_, bf16[256,2048]{1,0:T(8,128)(2,1)} %get-tuple-element.63.refs_0_.refs_1_, ...), custom_call_target="tpu_custom_call" | custom-call | flops 3221225472 | bytes 17825792 | tf_op jit(solution)/shard_map/rows_product/pallas_call | solution.py:460
  48.3 10.0 %collective-permute-done.2.refs_0_.refs_4_ = f32[136,2048]{1,0:T(8,128)} collective-permute-done((f32[136,2048]{1,0:T(8,128)S(1)}, f32[136,2048]{1,0:T(8,128)}, u32[]{:S(2)}, u32[]{:S(2)}) %collective-permute-start.2) | collective-permute-done | bytes 1114144 | tf_op jit(solution)/shard_map/ppermute | solution.py:301
  64.3 15.4 %rows_product.11 = (bf16[2048,256]{1,0:T(8,128)(2,1)}, f32[2048,512]{1,0:T(8,128)}, f32[2048,512]{1,0:T(8,128)}, bf16[2048,1024]{1,0:T(8,128)(2,1)}, f32[2048,1024]{1,0:T(8,128)}) custom-call(s32[1]{0:T(128)} %bitcast.12.shard_ref, f32[136,2048]{1,0:T(8,128)} %copy-done.31, ...), custom_call_target="tpu_custom_call", output_to_operand_aliasing={{0}: (13, {}), {1}: (14, {}), {2}: (15, {}), {3}: (16, {}),... | custom-call | flops 6442450944 | bytes 23068672 | tf_op jit(solution)/shard_map/rows_product/pallas_call | solution.py:460
  79.6 7.1 %collective-permute-done.5.refs_2_.refs_6_ = f32[136,2048]{1,0:T(8,128)S(1)} collective-permute-done((f32[136,2048]{1,0:T(8,128)}, f32[136,2048]{1,0:T(8,128)S(1)}, u32[]{:S(2)}, u32[]{:S(2)}) %collective-permute-start.5) | collective-permute-done | bytes 1114144 | tf_op jit(solution)/shard_map/ppermute | solution.py:301
  92.2 15.4 %rows_product.12 = (bf16[2048,256]{1,0:T(8,128)(2,1)}, f32[2048,512]{1,0:T(8,128)}, f32[2048,512]{1,0:T(8,128)}, bf16[2048,1024]{1,0:T(8,128)(2,1)}, f32[2048,1024]{1,0:T(8,128)}) custom-call(s32[1]{0:T(128)} %bitcast.12.shard_ref, ...), custom_call_target="tpu_custom_call", output_to_operand_aliasing={{0}: (13, {}), {1}: (14, {}), {2}: (15, {}), {3}: (16, {}),... | custom-call | flops 6442450944 | bytes 23068672 | tf_op jit(solution)/shard_map/rows_product/pallas_call | solution.py:460
  112.8 15.4 %rows_product.13 = (bf16[2048,256]{1,0:T(8,128)(2,1)}, f32[2048,512]{1,0:T(8,128)}, f32[2048,512]{1,0:T(8,128)}, bf16[2048,1024]{1,0:T(8,128)(2,1)}, f32[2048,1024]{1,0:T(8,128)}) custom-call(s32[1]{0:T(128)} %bitcast.12.shard_ref, f32[136,2048]{1,0:T(8,128)} %copy-done.28, ...), custom_call_target="tpu_custom_call", output_to_operand_aliasing={{0}: (13, {}), {1}: (14, {}), {2}: (15, {}), {3}: (16, {}),... | custom-call | flops 6442450944 | bytes 23068672 | tf_op jit(solution)/shard_map/rows_product/pallas_call | solution.py:460
  128.2 11.8 %rows_product.14 = (bf16[2048,256]{1,0:T(8,128)(2,1)}, f32[2048,512]{1,0:T(8,128)}, f32[2048,512]{1,0:T(8,128)}, bf16[2048,1024]{1,0:T(8,128)(2,1)}, f32[2048,1024]{1,0:T(8,128)}) custom-call(s32[1]{0:T(128)} %bitcast.12.shard_ref, ...), custom_call_target="tpu_custom_call", output_to_operand_aliasing={{0}: (13, {}), {1}: (14, {}), {2}: (15, {}), {3}: (16, {}),... | custom-call | flops 3221225472 | bytes 17825792 | tf_op jit(solution)/shard_map/rows_product/pallas_call | solution.py:460
  140.0 17.9 %retain_forward.1 = (f32[2048,1024]{1,0:T(8,128)}, bf16[2048,1024]{1,0:T(8,128)(2,1)}, bf16[2,8,256,512]{3,2,1,0:T(8,128)(2,1)}) custom-call(s32[8]{0:T(128)} %compare_select_fusion.4.slot_ref, f32[8,8,2048]{2,1,0:T(8,128)} %fusion.63.info_ref, f32[1,256]{1,0:T(1,128)} %add_convert_fusion.3.places_ref, f32[2048,512]{1,0:T(8,128)} %get-tuple-element.84.q_ref, ...), custom_call_target="tpu_custom_call" | custom-call | flops 4831838208 | bytes 33554432 | tf_op jit(solution)/shard_map/retain_forward/pallas_call | solution.py:602
  157.9 3.1 fusion.50
  167.4 11.0 %collective-permute-done.61.refs_0_ = f32[64,2048]{1,0:T(8,128)} collective-permute-done((f32[64,2048]{1,0:T(8,128)S(1)}, f32[64,2048]{1,0:T(8,128)}, u32[]{:S(2)}, u32[]{:S(2)}) %collective-permute-start.61) | collective-permute-done | bytes 524320 | tf_op jit(solution)/shard_map/ppermute | solution.py:725
  179.8 20.6 %collective-permute-done.65.refs_4_ = f32[64,2048]{1,0:T(8,128)} collective-permute-done((f32[64,2048]{1,0:T(8,128)S(1)}, f32[64,2048]{1,0:T(8,128)}, u32[]{:S(2)}, u32[]{:S(2)}) %collective-permute-start.65) | collective-permute-done | bytes 524320 | tf_op jit(solution)/shard_map/ppermute | solution.py:725
  207.1 8.5 %collective-permute-done.66.refs_5_ = f32[64,2048]{1,0:T(8,128)} collective-permute-done((f32[64,2048]{1,0:T(8,128)}, f32[64,2048]{1,0:T(8,128)}, u32[]{:S(2)}, u32[]{:S(2)}) %collective-permute-start.66) | collective-permute-done | bytes 524320 | tf_op jit(solution)/shard_map/ppermute | solution.py:730
  215.5 11.2 %collective-permute-done.70.refs_9_ = f32[64,2048]{1,0:T(8,128)} collective-permute-done((f32[64,2048]{1,0:T(8,128)}, f32[64,2048]{1,0:T(8,128)}, u32[]{:S(2)}, u32[]{:S(2)}) %collective-permute-start.70) | collective-permute-done | bytes 524320 | tf_op jit(solution)/shard_map/ppermute | solution.py:730
  227.4 4.4 fusion.18
  234.2 4.8 round_rows.3
  239.0 9.2 %collective-permute-done.17 = f32[128,2048]{1,0:T(8,128)} collective-permute-done((f32[128,2048]{1,0:T(8,128)S(1)}, f32[128,2048]{1,0:T(8,128)}, u32[]{:S(2)}, u32[]{:S(2)}) %collective-permute-start.17) | collective-permute-done | bytes 1048608 | tf_op jit(solution)/shard_map/ppermute | solution.py:280
  250.4 9.5 %collective-permute-start.49 = (f32[64,2048]{1,0:T(8,128)S(1)}, f32[64,2048]{1,0:T(8,128)S(1)}, u32[]{:S(2)}, u32[]{:S(2)}) collective-permute-start(f32[64,2048]{1,0:T(8,128)S(1)} %constant_dynamic-slice_fusion.5), channel_id=1, source_target_pairs={{0,8},{4,12},{8,16},{12,20},{16,24},{20,28},{24,0},{28,4},{1,9},{5... | collective-permute-start | bytes 1572872 | tf_op jit(solution)/shard_map/ppermute | solution.py:725
  260.0 3.5 collective-permute-start.53
  263.5 5.1 fusion.96
  268.6 7.2 %collective-permute-done.49.refs_0_ = f32[64,2048]{1,0:T(8,128)S(1)} collective-permute-done((f32[64,2048]{1,0:T(8,128)S(1)}, f32[64,2048]{1,0:T(8,128)S(1)}, u32[]{:S(2)}, u32[]{:S(2)}) %collective-permute-start.49) | collective-permute-done | bytes 524320 | tf_op jit(solution)/shard_map/ppermute | solution.py:725
  277.3 19.0 %collective-permute-done.53.refs_4_ = f32[64,2048]{1,0:T(8,128)S(1)} collective-permute-done((f32[64,2048]{1,0:T(8,128)S(1)}, f32[64,2048]{1,0:T(8,128)S(1)}, u32[]{:S(2)}, u32[]{:S(2)}) %collective-permute-start.53) | collective-permute-done | bytes 524320 | tf_op jit(solution)/shard_map/ppermute | solution.py:725
  300.8 3.6 multiply_convert_fusion.4
  314.5 6.7 %collective-permute-done.58.refs_9_ = f32[64,2048]{1,0:T(8,128)S(1)} collective-permute-done((f32[64,2048]{1,0:T(8,128)S(1)}, f32[64,2048]{1,0:T(8,128)S(1)}, u32[]{:S(2)}, u32[]{:S(2)}) %collective-permute-start.58) | collective-permute-done | bytes 524320 | tf_op jit(solution)/shard_map/ppermute | solution.py:730
  327.5 4.8 round_rows.2
  332.3 4.5 fusion.6
  338.4 17.0 %fusion = (f32[768,1024]{1,0:T(8,128)S(1)}, f32[768,1024]{1,0:T(8,128)S(1)}) fusion(bf16[768,2048]{1,0:T(8,128)(2,1)S(1)} %copy-done.29, bf16[2048,1024]{1,0:T(8,128)(2,1)S(1)} %copy-done.9), kind=kOutput, calls=%fused_computation.1 | convolution fusion | flops 3269984256 | bytes 13631488 | tf_op jit(solution)/shard_map/dot_general | solution.py:40
  355.4 6.7 %collective-permute-done.20 = f32[128,2048]{1,0:T(8,128)S(1)} collective-permute-done((f32[128,2048]{1,0:T(8,128)S(1)}, f32[128,2048]{1,0:T(8,128)S(1)}, u32[]{:S(2)}, u32[]{:S(2)}) %collective-permute-start.20) | collective-permute-done | bytes 1048608 | tf_op jit(solution)/shard_map/ppermute | solution.py:280
  363.3 6.0 %collective-permute-start.21 = (f32[128,2048]{1,0:T(8,128)S(1)}, f32[128,2048]{1,0:T(8,128)S(1)}, u32[]{:S(2)}, u32[]{:S(2)}) collective-permute-start(f32[128,2048]{1,0:T(8,128)S(1)} %convert_add_fusion.1), channel_id=1, source_target_pairs={{0,8},{8,16},{16,24},{24,28},{28,20},{20,12},{12,4},{4,0},{1,9},{9... | collective-permute-start | bytes 3145736 | tf_op jit(solution)/shard_map/ppermute | solution.py:301
  369.3 3.4 fusion.97
  376.5 14.6 %collective-permute-done.21.refs_0_.refs_4_ = f32[128,2048]{1,0:T(8,128)S(1)} collective-permute-done((f32[128,2048]{1,0:T(8,128)S(1)}, f32[128,2048]{1,0:T(8,128)S(1)}, u32[]{:S(2)}, u32[]{:S(2)}) %collective-permute-start.21) | collective-permute-done | bytes 1048608 | tf_op jit(solution)/shard_map/ppermute | solution.py:301
  396.2 2.6 convolution_add_fusion.10
  399.0 15.5 %collective-permute-done.22.refs_0_.refs_4_ = f32[128,2048]{1,0:T(8,128)S(1)} collective-permute-done((f32[128,2048]{1,0:T(8,128)S(1)}, f32[128,2048]{1,0:T(8,128)S(1)}, u32[]{:S(2)}, u32[]{:S(2)}) %collective-permute-start.22) | collective-permute-done | bytes 1048608 | tf_op jit(solution)/shard_map/ppermute | solution.py:301
  423.4 14.0 %collective-permute-done.26.refs_0_.refs_4_ = f32[128,2048]{1,0:T(8,128)} collective-permute-done((f32[128,2048]{1,0:T(8,128)S(1)}, f32[128,2048]{1,0:T(8,128)}, u32[]{:S(2)}, u32[]{:S(2)}) %collective-permute-start.26) | collective-permute-done | bytes 1048608 | tf_op jit(solution)/shard_map/ppermute | solution.py:301
  437.3 3.0 collective-permute-done.30.refs_2_.refs_6_
  448.1 4.8 rows_product.15
  452.9 6.9 %rows_product.16 = (bf16[2048,256]{1,0:T(8,128)(2,1)}, f32[2048,1024]{1,0:T(8,128)}) custom-call(s32[1]{0:T(128)} %bitcast.12.shard_ref, f32[128,2048]{1,0:T(8,128)} %copy-done.39, f32[128,2048]{1,0:T(8,128)} %copy-done.42, f32[128,2048]{1,0:T(8,128)} %copy-done.40, f32[128,2048]{1,0:T(8,128)} %copy-done.44, ...), custom_call_target="tpu_custom_call", output_to_operand_aliasing={{0}: (10, {}), {1}: (11, {})} | custom-call | flops 2147483648 | bytes 10485760 | tf_op jit(solution)/shard_map/rows_product/pallas_call | solution.py:460
  460.4 6.8 %rows_product.17 = (bf16[2048,256]{1,0:T(8,128)(2,1)}, f32[2048,1024]{1,0:T(8,128)}) custom-call(s32[1]{0:T(128)} %bitcast.12.shard_ref, f32[128,2048]{1,0:T(8,128)} %copy-done.38, f32[128,2048]{1,0:T(8,128)} %copy-done.45, f32[128,2048]{1,0:T(8,128)} %copy-done.41, f32[128,2048]{1,0:T(8,128)} %copy-done.47, ...), custom_call_target="tpu_custom_call", output_to_operand_aliasing={{0}: (10, {}), {1}: (11, {})} | custom-call | flops 2147483648 | bytes 10485760 | tf_op jit(solution)/shard_map/rows_product/pallas_call | solution.py:460
  467.2 3.6 fusion.9
  473.8 6.9 %rows_product.18 = (bf16[2048,256]{1,0:T(8,128)(2,1)}, f32[2048,1024]{1,0:T(8,128)}) custom-call(s32[1]{0:T(128)} %bitcast.12.shard_ref, f32[128,2048]{1,0:T(8,128)} %collective-permute-done.26.refs_0_.refs_4_, f32[128,2048]{1,0:T(8,128)} %copy-done.43, ...), custom_call_target="tpu_custom_call", output_to_operand_aliasing={{0}: (10, {}), {1}: (11, {})} | custom-call | flops 2147483648 | bytes 10485760 | tf_op jit(solution)/shard_map/rows_product/pallas_call | solution.py:460
  481.7 4.7 rows_product.19
  486.4 28.0 %retain_backward.1 = (bf16[2048,512]{1,0:T(8,128)(2,1)}, bf16[2048,512]{1,0:T(8,128)(2,1)}, bf16[2048,1024]{1,0:T(8,128)(2,1)}, bf16[2048,1024]{1,0:T(8,128)(2,1)}) custom-call(s32[8]{0:T(128)} %compare_select_fusion.4.slot_ref, f32[8,8,2048]{2,1,0:T(8,128)} %fusion.63.info_ref, f32[1,256]{1,0:T(1,128)} %add_convert_fusion.3.places_ref, ...), custom_call_target="tpu_custom_call" | custom-call | flops 10200547328 | bytes 54525952 | tf_op jit(solution)/shard_map/retain_backward/pallas_call | solution.py:629
  531.9 3.6 convolution_add_fusion.3.mine_ref
  535.5 3.4 gain_part.1
  542.1 4.6 fusion.94
  556.9 17.9 %collective-permute-done.42 = f32[128,2048]{1,0:T(8,128)S(1)} collective-permute-done((f32[128,2048]{1,0:T(8,128)S(1)}, f32[128,2048]{1,0:T(8,128)S(1)}, u32[]{:S(2)}, u32[]{:S(2)}) %collective-permute-start.42) | collective-permute-done | bytes 1048608 | tf_op jit(solution)/shard_map/ppermute | solution.py:280
  (366 shorter events, 139.1 us)
Async XLA Ops:
  4.6 27.8 %collective-permute-start = (f32[136,2048]{1,0:T(8,128)}, f32[136,2048]{1,0:T(8,128)S(1)}, u32[]{:S(2)}, u32[]{:S(2)}) collective-permute-start(f32[136,2048]{1,0:T(8,128)} %get-tuple-element.62), channel_id=1, source_target_pairs={{0,8},{8,16},{16,24},{24,28},{28,20},{20,12},{12,4},{4,0},{1,9},{9... | collective-permute-start | bytes 3342344 | tf_op jit(solution)/shard_map/ppermute | solution.py:301
  7.6 26.5 %collective-permute-start.1 = (f32[136,2048]{1,0:T(8,128)}, f32[136,2048]{1,0:T(8,128)}, u32[]{:S(2)}, u32[]{:S(2)}) collective-permute-start(f32[136,2048]{1,0:T(8,128)} %get-tuple-element.62), channel_id=1, source_target_pairs={{8,0},{16,8},{24,16},{28,24},{20,28},{12,20},{4,12},{0,4},{9,1},{1... | collective-permute-start | bytes 3342344 | tf_op jit(solution)/shard_map/ppermute | solution.py:301
  32.4 25.9 %collective-permute-start.2 = (f32[136,2048]{1,0:T(8,128)S(1)}, f32[136,2048]{1,0:T(8,128)}, u32[]{:S(2)}, u32[]{:S(2)}) collective-permute-start(f32[136,2048]{1,0:T(8,128)S(1)} %collective-permute-done.refs_0_.refs_4_), channel_id=1, source_target_pairs={{0,8},{8,16},{16,24},{24,28},{28,20},{20,12},{12,4},{4,0},{1,9},{9... | collective-permute-start | bytes 3342344 | tf_op jit(solution)/shard_map/ppermute | solution.py:301
  34.2 25.7 %collective-permute-start.3 = (f32[136,2048]{1,0:T(8,128)}, f32[136,2048]{1,0:T(8,128)}, u32[]{:S(2)}, u32[]{:S(2)}) collective-permute-start(f32[136,2048]{1,0:T(8,128)} %collective-permute-done.1.refs_2_.refs_6_), channel_id=1, source_target_pairs={{8,0},{16,8},{24,16},{28,24},{20,28},{12,20},{4,12},{0,4},{9,1},{1... | collective-permute-start | bytes 3342344 | tf_op jit(solution)/shard_map/ppermute | solution.py:301
  58.3 33.4 %collective-permute-start.12 = (f32[136,2048]{1,0:T(8,128)}, f32[136,2048]{1,0:T(8,128)}, u32[]{:S(2)}, u32[]{:S(2)}) collective-permute-start(f32[136,2048]{1,0:T(8,128)} %collective-permute-done.2.refs_0_.refs_4_), channel_id=1, source_target_pairs={{0,1},{1,0},{2,3},{3,2},{4,5},{5,4},{6,7},{7,6},{8,9},{9,8},{10,11... | collective-permute-start | bytes 3342344 | tf_op jit(solution)/shard_map/ppermute | solution.py:284
  58.3 29.9 %collective-permute-start.4 = (f32[136,2048]{1,0:T(8,128)}, f32[136,2048]{1,0:T(8,128)S(1)}, u32[]{:S(2)}, u32[]{:S(2)}) collective-permute-start(f32[136,2048]{1,0:T(8,128)} %collective-permute-done.2.refs_0_.refs_4_), channel_id=1, source_target_pairs={{0,8},{8,16},{16,24},{24,28},{28,20},{20,12},{12,4},{4,0},{1,9},{9... | collective-permute-start | bytes 3342344 | tf_op jit(solution)/shard_map/ppermute | solution.py:301
  59.8 26.9 %collective-permute-start.5 = (f32[136,2048]{1,0:T(8,128)}, f32[136,2048]{1,0:T(8,128)S(1)}, u32[]{:S(2)}, u32[]{:S(2)}) collective-permute-start(f32[136,2048]{1,0:T(8,128)} %collective-permute-done.3.refs_2_.refs_6_), channel_id=1, source_target_pairs={{8,0},{16,8},{24,16},{28,24},{20,28},{12,20},{4,12},{0,4},{9,1},{1... | collective-permute-start | bytes 3342344 | tf_op jit(solution)/shard_map/ppermute | solution.py:301
  62.8 29.4 %collective-permute-start.13 = (f32[136,2048]{1,0:T(8,128)}, f32[136,2048]{1,0:T(8,128)}, u32[]{:S(2)}, u32[]{:S(2)}) collective-permute-start(f32[136,2048]{1,0:T(8,128)} %collective-permute-done.3.refs_2_.refs_6_), channel_id=1, source_target_pairs={{0,1},{1,0},{2,3},{3,2},{4,5},{5,4},{6,7},{7,6},{8,9},{9,8},{10,11... | collective-permute-start | bytes 3342344 | tf_op jit(solution)/shard_map/ppermute | solution.py:284
  87.7 22.1 %collective-permute-start.6 = (f32[72,2048]{1,0:T(8,128)}, f32[72,2048]{1,0:T(8,128)}, u32[]{:S(2)}, u32[]{:S(2)}) collective-permute-start(f32[72,2048]{1,0:T(8,128)} %slice.126), channel_id=1, source_target_pairs={{8,0},{16,8},{24,16},{28,24},{20,28},{12,20},{4,12},{0,4},{9,1},{1... | collective-permute-start | bytes 1769480 | tf_op jit(solution)/shard_map/ppermute | solution.py:301
  161.1 40.9 %collective-permute-start.16 = (f32[128,2048]{1,0:T(8,128)S(1)}, f32[128,2048]{1,0:T(8,128)S(1)}, u32[]{:S(2)}, u32[]{:S(2)}) collective-permute-start(f32[128,2048]{1,0:T(8,128)S(1)} %fusion.50), channel_id=1, source_target_pairs={{0,1},{1,0},{2,3},{3,2},{4,5},{5,4},{6,7},{7,6},{8,9},{9,8},{10,11... | collective-permute-start | bytes 3145736 | tf_op jit(solution)/shard_map/ppermute | solution.py:278
  163.2 37.3 %collective-permute-start.65 = (f32[64,2048]{1,0:T(8,128)S(1)}, f32[64,2048]{1,0:T(8,128)}, u32[]{:S(2)}, u32[]{:S(2)}) collective-permute-start(f32[64,2048]{1,0:T(8,128)S(1)} %constant_dynamic-slice_fusion.4), channel_id=1, source_target_pairs={{0,16},{4,20},{8,24},{12,28},{16,0},{20,4},{24,8},{28,12},{1,17},{... | collective-permute-start | bytes 1572872 | tf_op jit(solution)/shard_map/ppermute | solution.py:725
  165.8 36.2 %collective-permute-start.69 = (f32[64,2048]{1,0:T(8,128)S(1)}, f32[64,2048]{1,0:T(8,128)}, u32[]{:S(2)}, u32[]{:S(2)}) collective-permute-start(f32[64,2048]{1,0:T(8,128)S(1)} %constant_dynamic-slice_fusion.4), channel_id=1, source_target_pairs={{0,24},{4,28},{8,0},{12,4},{16,8},{20,12},{24,16},{28,20},{1,25},{... | collective-permute-start | bytes 1572872 | tf_op jit(solution)/shard_map/ppermute | solution.py:725
  178.3 25.9 %collective-permute-start.62 = (f32[64,2048]{1,0:T(8,128)}, f32[64,2048]{1,0:T(8,128)S(1)}, u32[]{:S(2)}, u32[]{:S(2)}) collective-permute-start(f32[64,2048]{1,0:T(8,128)} %collective-permute-done.61.refs_0_), channel_id=1, source_target_pairs={{0,2},{2,0},{1,3},{3,1},{4,6},{6,4},{5,7},{7,5},{8,10},{10,8},{9,1... | collective-permute-start | bytes 1572872 | tf_op jit(solution)/shard_map/ppermute | solution.py:730
  179.8 47.0 %collective-permute-start.63 = (f32[64,2048]{1,0:T(8,128)}, f32[64,2048]{1,0:T(8,128)}, u32[]{:S(2)}, u32[]{:S(2)}) collective-permute-start(f32[64,2048]{1,0:T(8,128)} %collective-permute-done.61.refs_0_), channel_id=1, source_target_pairs={{0,1},{1,0},{2,3},{3,2},{4,5},{5,4},{6,7},{7,6},{8,9},{9,8},{10,11... | collective-permute-start | bytes 1572872 | tf_op jit(solution)/shard_map/ppermute | solution.py:284
  201.9 25.4 %collective-permute-start.67 = (f32[64,2048]{1,0:T(8,128)}, f32[64,2048]{1,0:T(8,128)}, u32[]{:S(2)}, u32[]{:S(2)}) collective-permute-start(f32[64,2048]{1,0:T(8,128)} %collective-permute-done.65.refs_4_), channel_id=1, source_target_pairs={{0,1},{1,0},{2,3},{3,2},{4,5},{5,4},{6,7},{7,6},{8,9},{9,8},{10,11... | collective-permute-start | bytes 1572872 | tf_op jit(solution)/shard_map/ppermute | solution.py:284
  201.9 24.8 %collective-permute-start.70 = (f32[64,2048]{1,0:T(8,128)}, f32[64,2048]{1,0:T(8,128)}, u32[]{:S(2)}, u32[]{:S(2)}) collective-permute-start(f32[64,2048]{1,0:T(8,128)} %collective-permute-done.69.refs_8_), channel_id=1, source_target_pairs={{0,2},{2,0},{1,3},{3,1},{4,6},{6,4},{5,7},{7,5},{8,10},{10,8},{9,1... | collective-permute-start | bytes 1572872 | tf_op jit(solution)/shard_map/ppermute | solution.py:730
  204.3 44.0 %collective-permute-start.17 = (f32[128,2048]{1,0:T(8,128)S(1)}, f32[128,2048]{1,0:T(8,128)}, u32[]{:S(2)}, u32[]{:S(2)}) collective-permute-start(f32[128,2048]{1,0:T(8,128)S(1)} %convolution_add_fusion.9), channel_id=1, source_target_pairs={{0,2},{2,0},{1,3},{3,1},{4,6},{6,4},{5,7},{7,5},{8,10},{10,8},{9,1... | collective-permute-start | bytes 3145736 | tf_op jit(solution)/shard_map/ppermute | solution.py:280
  250.4 25.4 %collective-permute-start.49 = (f32[64,2048]{1,0:T(8,128)S(1)}, f32[64,2048]{1,0:T(8,128)S(1)}, u32[]{:S(2)}, u32[]{:S(2)}) collective-permute-start(f32[64,2048]{1,0:T(8,128)S(1)} %constant_dynamic-slice_fusion.5), channel_id=1, source_target_pairs={{0,8},{4,12},{8,16},{12,20},{16,24},{20,28},{24,0},{28,4},{1,9},{5... | collective-permute-start | bytes 1572872 | tf_op jit(solution)/shard_map/ppermute | solution.py:725
  260.0 36.3 %collective-permute-start.53 = (f32[64,2048]{1,0:T(8,128)S(1)}, f32[64,2048]{1,0:T(8,128)S(1)}, u32[]{:S(2)}, u32[]{:S(2)}) collective-permute-start(f32[64,2048]{1,0:T(8,128)S(1)} %constant_dynamic-slice_fusion.5), channel_id=1, source_target_pairs={{0,16},{4,20},{8,24},{12,28},{16,0},{20,4},{24,8},{28,12},{1,17},{... | collective-permute-start | bytes 1572872 | tf_op jit(solution)/shard_map/ppermute | solution.py:725
  263.4 34.4 %collective-permute-start.57 = (f32[64,2048]{1,0:T(8,128)S(1)}, f32[64,2048]{1,0:T(8,128)S(1)}, u32[]{:S(2)}, u32[]{:S(2)}) collective-permute-start(f32[64,2048]{1,0:T(8,128)S(1)} %constant_dynamic-slice_fusion.5), channel_id=1, source_target_pairs={{0,24},{4,28},{8,0},{12,4},{16,8},{20,12},{24,16},{28,20},{1,25},{... | collective-permute-start | bytes 1572872 | tf_op jit(solution)/shard_map/ppermute | solution.py:725
  263.4 34.4 %collective-permute-start.18 = (f32[128,2048]{1,0:T(8,128)S(1)}, f32[128,2048]{1,0:T(8,128)S(1)}, u32[]{:S(2)}, u32[]{:S(2)}) collective-permute-start(f32[128,2048]{1,0:T(8,128)S(1)} %multiply_multiply_fusion.13), channel_id=1, source_target_pairs={{0,1},{1,0},{2,3},{3,2},{4,5},{5,4},{6,7},{7,6},{8,9},{9,8},{10,11... | collective-permute-start | bytes 3145736 | tf_op jit(solution)/shard_map/ppermute | solution.py:284
  275.8 35.2 %collective-permute-start.50 = (f32[64,2048]{1,0:T(8,128)S(1)}, f32[64,2048]{1,0:T(8,128)S(1)}, u32[]{:S(2)}, u32[]{:S(2)}) collective-permute-start(f32[64,2048]{1,0:T(8,128)S(1)} %collective-permute-done.49.refs_0_), channel_id=1, source_target_pairs={{0,2},{2,0},{1,3},{3,1},{4,6},{6,4},{5,7},{7,5},{8,10},{10,8},{9,1... | collective-permute-start | bytes 1572872 | tf_op jit(solution)/shard_map/ppermute | solution.py:730
  277.3 44.0 %collective-permute-start.51 = (f32[64,2048]{1,0:T(8,128)S(1)}, f32[64,2048]{1,0:T(8,128)S(1)}, u32[]{:S(2)}, u32[]{:S(2)}) collective-permute-start(f32[64,2048]{1,0:T(8,128)S(1)} %collective-permute-done.49.refs_0_), channel_id=1, source_target_pairs={{0,1},{1,0},{2,3},{3,2},{4,5},{5,4},{6,7},{7,6},{8,9},{9,8},{10,11... | collective-permute-start | bytes 1572872 | tf_op jit(solution)/shard_map/ppermute | solution.py:284
  297.8 24.0 %collective-permute-start.55 = (f32[64,2048]{1,0:T(8,128)S(1)}, f32[64,2048]{1,0:T(8,128)S(1)}, u32[]{:S(2)}, u32[]{:S(2)}) collective-permute-start(f32[64,2048]{1,0:T(8,128)S(1)} %collective-permute-done.53.refs_4_), channel_id=1, source_target_pairs={{0,1},{1,0},{2,3},{3,2},{4,5},{5,4},{6,7},{7,6},{8,9},{9,8},{10,11... | collective-permute-start | bytes 1572872 | tf_op jit(solution)/shard_map/ppermute | solution.py:284
  297.8 23.5 %collective-permute-start.58 = (f32[64,2048]{1,0:T(8,128)S(1)}, f32[64,2048]{1,0:T(8,128)S(1)}, u32[]{:S(2)}, u32[]{:S(2)}) collective-permute-start(f32[64,2048]{1,0:T(8,128)S(1)} %collective-permute-done.57.refs_8_), channel_id=1, source_target_pairs={{0,2},{2,0},{1,3},{3,1},{4,6},{6,4},{5,7},{7,5},{8,10},{10,8},{9,1... | collective-permute-start | bytes 1572872 | tf_op jit(solution)/shard_map/ppermute | solution.py:730
  310.9 21.3 %collective-permute-start.19 = (f32[128,2048]{1,0:T(8,128)}, f32[128,2048]{1,0:T(8,128)}, u32[]{:S(2)}, u32[]{:S(2)}) collective-permute-start(f32[128,2048]{1,0:T(8,128)} %convolution_add_fusion.7), channel_id=1, source_target_pairs={{0,1},{1,0},{2,3},{3,2},{4,5},{5,4},{6,7},{7,6},{8,9},{9,8},{10,11... | collective-permute-start | bytes 3145736 | tf_op jit(solution)/shard_map/ppermute | solution.py:278
  325.4 47.3 %collective-permute-start.23 = (f32[128,2048]{1,0:T(8,128)}, f32[128,2048]{1,0:T(8,128)}, u32[]{:S(2)}, u32[]{:S(2)}) collective-permute-start(f32[128,2048]{1,0:T(8,128)} %fusion.37), channel_id=1, source_target_pairs={{0,1},{1,0},{2,3},{3,2},{4,5},{5,4},{6,7},{7,6},{8,9},{9,8},{10,11... | collective-permute-start | bytes 3145736 | tf_op jit(solution)/shard_map/ppermute | solution.py:278
  336.8 25.2 %collective-permute-start.20 = (f32[128,2048]{1,0:T(8,128)S(1)}, f32[128,2048]{1,0:T(8,128)S(1)}, u32[]{:S(2)}, u32[]{:S(2)}) collective-permute-start(f32[128,2048]{1,0:T(8,128)S(1)} %fusion.6), channel_id=1, source_target_pairs={{0,2},{2,0},{1,3},{3,1},{4,6},{6,4},{5,7},{7,5},{8,10},{10,8},{9,1... | collective-permute-start | bytes 3145736 | tf_op jit(solution)/shard_map/ppermute | solution.py:280
  363.3 27.8 %collective-permute-start.21 = (f32[128,2048]{1,0:T(8,128)S(1)}, f32[128,2048]{1,0:T(8,128)S(1)}, u32[]{:S(2)}, u32[]{:S(2)}) collective-permute-start(f32[128,2048]{1,0:T(8,128)S(1)} %convert_add_fusion.1), channel_id=1, source_target_pairs={{0,8},{8,16},{16,24},{24,28},{28,20},{20,12},{12,4},{4,0},{1,9},{9... | collective-permute-start | bytes 3145736 | tf_op jit(solution)/shard_map/ppermute | solution.py:301
  369.3 24.3 %collective-permute-start.28 = (f32[128,2048]{1,0:T(8,128)S(1)}, f32[128,2048]{1,0:T(8,128)S(1)}, u32[]{:S(2)}, u32[]{:S(2)}) collective-permute-start(f32[128,2048]{1,0:T(8,128)S(1)} %convert_add_fusion.1), channel_id=1, source_target_pairs={{8,0},{16,8},{24,16},{28,24},{20,28},{12,20},{4,12},{0,4},{9,1},{1... | collective-permute-start | bytes 3145736 | tf_op jit(solution)/shard_map/ppermute | solution.py:301
  374.9 24.1 %collective-permute-start.24 = (f32[128,2048]{1,0:T(8,128)S(1)}, f32[128,2048]{1,0:T(8,128)S(1)}, u32[]{:S(2)}, u32[]{:S(2)}) collective-permute-start(f32[128,2048]{1,0:T(8,128)S(1)} %convolution_add_fusion.6), channel_id=1, source_target_pairs={{0,2},{2,0},{1,3},{3,1},{4,6},{6,4},{5,7},{7,5},{8,10},{10,8},{9,1... | collective-permute-start | bytes 3145736 | tf_op jit(solution)/shard_map/ppermute | solution.py:280
  391.1 23.5 %collective-permute-start.22 = (f32[128,2048]{1,0:T(8,128)S(1)}, f32[128,2048]{1,0:T(8,128)S(1)}, u32[]{:S(2)}, u32[]{:S(2)}) collective-permute-start(f32[128,2048]{1,0:T(8,128)S(1)} %collective-permute-done.21.refs_0_.refs_4_), channel_id=1, source_target_pairs={{0,8},{8,16},{16,24},{24,28},{28,20},{20,12},{12,4},{4,0},{1,9},{9... | collective-permute-start | bytes 3145736 | tf_op jit(solution)/shard_map/ppermute | solution.py:301
  393.6 23.6 %collective-permute-start.29 = (f32[128,2048]{1,0:T(8,128)S(1)}, f32[128,2048]{1,0:T(8,128)S(1)}, u32[]{:S(2)}, u32[]{:S(2)}) collective-permute-start(f32[128,2048]{1,0:T(8,128)S(1)} %collective-permute-done.28.refs_2_.refs_6_), channel_id=1, source_target_pairs={{8,0},{16,8},{24,16},{28,24},{20,28},{12,20},{4,12},{0,4},{9,1},{1... | collective-permute-start | bytes 3145736 | tf_op jit(solution)/shard_map/ppermute | solution.py:301
  395.6 22.9 %collective-permute-start.40 = (f32[128,2048]{1,0:T(8,128)S(1)}, f32[128,2048]{1,0:T(8,128)S(1)}, u32[]{:S(2)}, u32[]{:S(2)}) collective-permute-start(f32[128,2048]{1,0:T(8,128)S(1)} %convert_add_fusion.1), channel_id=1, source_target_pairs={{0,1},{1,0},{2,3},{3,2},{4,5},{5,4},{6,7},{7,6},{8,9},{9,8},{10,11... | collective-permute-start | bytes 3145736 | tf_op jit(solution)/shard_map/ppermute | solution.py:284
  395.7 22.9 %collective-permute-start.38 = (f32[128,2048]{1,0:T(8,128)S(1)}, f32[128,2048]{1,0:T(8,128)S(1)}, u32[]{:S(2)}, u32[]{:S(2)}) collective-permute-start(f32[128,2048]{1,0:T(8,128)S(1)} %collective-permute-done.21.refs_0_.refs_4_), channel_id=1, source_target_pairs={{0,1},{1,0},{2,3},{3,2},{4,5},{5,4},{6,7},{7,6},{8,9},{9,8},{10,11... | collective-permute-start | bytes 3145736 | tf_op jit(solution)/shard_map/ppermute | solution.py:284
  399.0 23.0 %collective-permute-start.39 = (f32[128,2048]{1,0:T(8,128)S(1)}, f32[128,2048]{1,0:T(8,128)S(1)}, u32[]{:S(2)}, u32[]{:S(2)}) collective-permute-start(f32[128,2048]{1,0:T(8,128)S(1)} %collective-permute-done.28.refs_2_.refs_6_), channel_id=1, source_target_pairs={{0,1},{1,0},{2,3},{3,2},{4,5},{5,4},{6,7},{7,6},{8,9},{9,8},{10,11... | collective-permute-start | bytes 3145736 | tf_op jit(solution)/shard_map/ppermute | solution.py:284
  414.6 22.7 %collective-permute-start.26 = (f32[128,2048]{1,0:T(8,128)S(1)}, f32[128,2048]{1,0:T(8,128)}, u32[]{:S(2)}, u32[]{:S(2)}) collective-permute-start(f32[128,2048]{1,0:T(8,128)S(1)} %collective-permute-done.22.refs_0_.refs_4_), channel_id=1, source_target_pairs={{0,8},{8,16},{16,24},{24,28},{28,20},{20,12},{12,4},{4,0},{1,9},{9... | collective-permute-start | bytes 3145736 | tf_op jit(solution)/shard_map/ppermute | solution.py:301
  417.2 23.0 %collective-permute-start.30 = (f32[128,2048]{1,0:T(8,128)S(1)}, f32[128,2048]{1,0:T(8,128)}, u32[]{:S(2)}, u32[]{:S(2)}) collective-permute-start(f32[128,2048]{1,0:T(8,128)S(1)} %collective-permute-done.29.refs_2_.refs_6_), channel_id=1, source_target_pairs={{8,0},{16,8},{24,16},{28,24},{20,28},{12,20},{4,12},{0,4},{9,1},{1... | collective-permute-start | bytes 3145736 | tf_op jit(solution)/shard_map/ppermute | solution.py:301
  418.6 25.5 %collective-permute-start.36 = (f32[128,2048]{1,0:T(8,128)S(1)}, f32[128,2048]{1,0:T(8,128)S(1)}, u32[]{:S(2)}, u32[]{:S(2)}) collective-permute-start(f32[128,2048]{1,0:T(8,128)S(1)} %collective-permute-done.22.refs_0_.refs_4_), channel_id=1, source_target_pairs={{0,1},{1,0},{2,3},{3,2},{4,5},{5,4},{6,7},{7,6},{8,9},{9,8},{10,11... | collective-permute-start | bytes 3145736 | tf_op jit(solution)/shard_map/ppermute | solution.py:284
  418.7 27.0 %collective-permute-start.37 = (f32[128,2048]{1,0:T(8,128)S(1)}, f32[128,2048]{1,0:T(8,128)S(1)}, u32[]{:S(2)}, u32[]{:S(2)}) collective-permute-start(f32[128,2048]{1,0:T(8,128)S(1)} %collective-permute-done.29.refs_2_.refs_6_), channel_id=1, source_target_pairs={{0,1},{1,0},{2,3},{3,2},{4,5},{5,4},{6,7},{7,6},{8,9},{9,8},{10,11... | collective-permute-start | bytes 3145736 | tf_op jit(solution)/shard_map/ppermute | solution.py:284
  422.0 45.2 %collective-permute-start.25 = (f32[128,2048]{1,0:T(8,128)}, f32[128,2048]{1,0:T(8,128)}, u32[]{:S(2)}, u32[]{:S(2)}) collective-permute-start(f32[128,2048]{1,0:T(8,128)} %add_multiply_fusion), channel_id=1, source_target_pairs={{0,1},{1,0},{2,3},{3,2},{4,5},{5,4},{6,7},{7,6},{8,9},{9,8},{10,11... | collective-permute-start | bytes 3145736 | tf_op jit(solution)/shard_map/ppermute | solution.py:284
  437.3 34.0 %collective-permute-start.34 = (f32[128,2048]{1,0:T(8,128)}, f32[128,2048]{1,0:T(8,128)S(1)}, u32[]{:S(2)}, u32[]{:S(2)}) collective-permute-start(f32[128,2048]{1,0:T(8,128)} %collective-permute-done.26.refs_0_.refs_4_), channel_id=1, source_target_pairs={{0,1},{1,0},{2,3},{3,2},{4,5},{5,4},{6,7},{7,6},{8,9},{9,8},{10,11... | collective-permute-start | bytes 3145736 | tf_op jit(solution)/shard_map/ppermute | solution.py:284
  440.3 32.6 %collective-permute-start.35 = (f32[128,2048]{1,0:T(8,128)}, f32[128,2048]{1,0:T(8,128)S(1)}, u32[]{:S(2)}, u32[]{:S(2)}) collective-permute-start(f32[128,2048]{1,0:T(8,128)} %collective-permute-done.30.refs_2_.refs_6_), channel_id=1, source_target_pairs={{0,1},{1,0},{2,3},{3,2},{4,5},{5,4},{6,7},{7,6},{8,9},{9,8},{10,11... | collective-permute-start | bytes 3145736 | tf_op jit(solution)/shard_map/ppermute | solution.py:284
  459.8 20.9 %collective-permute-start.32 = (f32[64,2048]{1,0:T(8,128)}, f32[64,2048]{1,0:T(8,128)S(1)}, u32[]{:S(2)}, u32[]{:S(2)}) collective-permute-start(f32[64,2048]{1,0:T(8,128)} %collective-permute-done.27.refs_0_.refs_4_), channel_id=1, source_target_pairs={{0,1},{1,0},{2,3},{3,2},{4,5},{5,4},{6,7},{7,6},{8,9},{9,8},{10,11... | collective-permute-start | bytes 1572872 | tf_op jit(solution)/shard_map/ppermute | solution.py:284
  470.8 105.1 %collective-permute-start.75 = (f32[1024,256]{1,0:T(8,128)}, f32[1024,256]{1,0:T(8,128)}, u32[]{:S(2)}, u32[]{:S(2)}) collective-permute-start(f32[1024,256]{1,0:T(8,128)} %constant_dynamic-slice_fusion.1), channel_id=1, source_target_pairs={{0,4},{4,0},{8,12},{12,8},{16,20},{20,16},{24,28},{28,24},{1,5},{5... | collective-permute-start | bytes 3145736 | tf_op jit(solution)/shard_map/ppermute | solution.py:801
  471.3 107.2 %collective-permute-start.74 = (f32[256,1024]{1,0:T(8,128)}, f32[256,1024]{1,0:T(8,128)}, u32[]{:S(2)}, u32[]{:S(2)}) collective-permute-start(f32[256,1024]{1,0:T(8,128)} %get-tuple-element.110), channel_id=1, source_target_pairs={{0,4},{4,0},{8,12},{12,8},{16,20},{20,16},{24,28},{28,24},{1,5},{5... | collective-permute-start | bytes 3145736 | tf_op jit(solution)/shard_map/ppermute | solution.py:801
  472.9 109.5 %collective-permute-start.73 = (f32[256,1024]{1,0:T(8,128)}, f32[256,1024]{1,0:T(8,128)}, u32[]{:S(2)}, u32[]{:S(2)}) collective-permute-start(f32[256,1024]{1,0:T(8,128)} %get-tuple-element.109), channel_id=1, source_target_pairs={{0,4},{4,0},{8,12},{12,8},{16,20},{20,16},{24,28},{28,24},{1,5},{5... | collective-permute-start | bytes 3145736 | tf_op jit(solution)/shard_map/ppermute | solution.py:801
  549.8 25.0 %collective-permute-start.42 = (f32[128,2048]{1,0:T(8,128)S(1)}, f32[128,2048]{1,0:T(8,128)S(1)}, u32[]{:S(2)}, u32[]{:S(2)}) collective-permute-start(f32[128,2048]{1,0:T(8,128)S(1)} %add.219), channel_id=1, source_target_pairs={{0,2},{2,0},{1,3},{3,1},{4,6},{6,4},{5,7},{7,5},{8,10},{10,8},{9,1... | collective-permute-start | bytes 3145736 | tf_op jit(solution)/shard_map/ppermute | solution.py:280
  (107 other events, 1290.2 us)

commit v2 on v1

--- a/solution.py
+++ b/solution.py
@@ -331,13 +331,6 @@
     return lax.dot_general(left, right, (((1,), (0,)), ((), ())), preferred_element_type=jnp.float32)
 
 
-def split_dot(left, right, dot):
-    left_high, right_high = left.astype(jnp.bfloat16), right.astype(jnp.bfloat16)
-    left_low = (left - left_high.astype(jnp.float32)).astype(jnp.bfloat16)
-    right_low = (right - right_high.astype(jnp.float32)).astype(jnp.bfloat16)
-    return dot(left_high, right_high) + (dot(left_low, right_high) + dot(left_high, right_low))
-
-
 def half_split_dot(left, right, dot):
     left_high = left.astype(jnp.bfloat16)
     left_low = (left - left_high.astype(jnp.float32)).astype(jnp.bfloat16)
@@ -351,18 +344,18 @@
     return centred * inverse, inverse
 
 
-def norm_start_kernel(core_ref, first_ref, tokens_ref, gain_ref, rates_ref, normed_ref, half_ref):
+def norm_start_kernel(core_ref, first_ref, tokens_ref, gain_ref, rates_ref, normed_ref, half_ref, info_ref):
     half = tokens_ref.shape[0] // 2
     for index, core in enumerate((core_ref[0], 1 - core_ref[0])):
         rows = tokens_ref[pl.ds(pl.multiple_of(core * half, half), half), :].astype(jnp.float32)
         normed = (norm_parts(rows)[0] * gain_ref[...]).astype(jnp.bfloat16)
         normed_ref[index * half : (index + 1) * half, :] = normed
         if index == 0:
-            half_ref[:half, :] = normed.astype(jnp.float32)
+            half_ref[...] = normed.astype(jnp.float32)
     heads, size = rates_ref.shape
-    half_ref[half:, :] = jnp.full((8, half_ref.shape[1]), first_ref[0], jnp.int32).astype(jnp.float32)
+    info_ref[...] = jnp.full(info_ref.shape, first_ref[0], jnp.int32).astype(jnp.float32)
     for head in range(heads):
-        half_ref[half : half + 1, head * size : (head + 1) * size] = rates_ref[head : head + 1, :]
+        info_ref[0:1, head * size : (head + 1) * size] = rates_ref[head : head + 1, :]
 
 
 def norm_start(core, first_start, tokens, gain, log_decay):
@@ -371,11 +364,13 @@
     return pl.pallas_call(
         norm_start_kernel,
         in_specs=[smem, smem, vmem, vmem, vmem],
-        out_specs=[vmem, vmem],
+        out_specs=[vmem, vmem, vmem],
         out_shape=[
             jax.ShapeDtypeStruct((rows, width), jnp.bfloat16),
-            jax.ShapeDtypeStruct((rows // 2 + 8, width), jnp.float32),
+            jax.ShapeDtypeStruct((rows // 2, width), jnp.float32),
+            jax.ShapeDtypeStruct((8, log_decay.size), jnp.float32),
         ],
+        compiler_params=pltpu.CompilerParams(vmem_limit_bytes=10 << 20),
         name="norm_start",
     )(core[None], first_start, tokens, gain[None], log_decay)
 
@@ -397,14 +392,16 @@
         out_specs=vmem,
         out_shape=jax.ShapeDtypeStruct((1, tokens.shape[1]), jnp.float32),
         cost_estimate=pl.CostEstimate(flops=10 * tokens.size, bytes_accessed=6 * tokens.size, transcendentals=0),
+        compiler_params=pltpu.CompilerParams(vmem_limit_bytes=10 << 20),
         name="gain_part",
     )(core[None], tokens, mine, other)
 
 
-def rows_product_kernel(parts, weights, tiles, scales, turned, shard_ref, *refs):
+def rows_product_kernel(parts, tiles, pieces, scales, turned, shard_ref, *refs):
+    weights = len(tiles)
     part_refs, slab_refs = refs[:parts], refs[parts : 2 * parts]
     weight_refs = refs[2 * parts : 2 * parts + weights]
-    outs = refs[len(refs) - weights - 2 : len(refs) - 1]
+    outs = refs[len(refs) - sum(pieces) - 2 : len(refs) - 1]
     x = refs[-1]
     step = pl.program_id(0)
     size = x.shape[0] // parts
@@ -416,18 +413,24 @@
             x[at, :] = part_refs[index][...].astype(jnp.bfloat16)
             outs[0][at, :] = slab_refs[index][...].astype(jnp.bfloat16)
 
-    start = 0
-    for weight, out, count, scale in zip(weight_refs, outs[1:], tiles, scales):
+    start, at = 0, 1
+    for weight, count, number, scale in zip(weight_refs, tiles, pieces, scales):
 
         @pl.when((step >= start) & (step < start + count))
-        def _(weight=weight, out=out, scale=scale):
+        def _(weight=weight, results=outs[at : at + number], scale=scale):
             found = (dot_nt if turned else dot_nn)(x[...], weight[...])
-            out[...] = (found * scale if scale != 1.0 else found).astype(out.dtype)
+            if scale != 1.0:
+                found = found * scale
+            high = found.astype(jnp.bfloat16)
+            results[0][...] = high
+            if len(results) == 2:
+                results[1][...] = (found - high.astype(jnp.float32)).astype(jnp.bfloat16)
 
         start += count
-
-
-def rows_product(parts, size, weights, kinds, scales, turned, shard, block, total, buffers=None):
+        at += number
+
+
+def rows_product(parts, size, weights, pieces, scales, turned, shard, block, total, buffers=None):
     count, width = len(parts), parts[0].shape[1]
     rows = count * size
     tile = 512
@@ -447,10 +450,10 @@
         else:
             in_specs.append(pl.BlockSpec((width, tile), lambda j, s, a=start, n=number: (0, at(j, a, n))))
     out_specs = [pl.BlockSpec((rows, slab), lambda j, s: (block, 0))]
-    for start, number in zip(starts, tiles):
-        out_specs.append(pl.BlockSpec((rows, tile), lambda j, s, a=start, n=number: (block, at(j, a, n))))
     out_shape = [jax.ShapeDtypeStruct((total, slab), jnp.bfloat16)]
-    out_shape += [jax.ShapeDtypeStruct((total, c), kind) for c, kind in zip(columns, kinds)]
+    for start, number, results, c in zip(starts, tiles, pieces, columns):
+        out_specs += [pl.BlockSpec((rows, tile), lambda j, s, a=start, n=number: (block, at(j, a, n)))] * results
+        out_shape += [jax.ShapeDtypeStruct((total, c), jnp.bfloat16)] * results
     operands = [*parts, *parts, *weights]
     aliases = {}
     if buffers is not None:
@@ -458,7 +461,7 @@
         in_specs += [pl.BlockSpec(memory_space=pl.ANY)] * len(buffers)
         operands += buffers
     return pl.pallas_call(
-        functools.partial(rows_product_kernel, count, len(weights), tiles, scales, turned),
+        functools.partial(rows_product_kernel, count, tiles, pieces, scales, turned),
         grid_spec=pltpu.PrefetchScalarGridSpec(
             num_scalar_prefetch=1,
             grid=(sum(tiles),),
@@ -470,11 +473,76 @@
         input_output_aliases=aliases,
         cost_estimate=pl.CostEstimate(
             flops=2 * rows * width * sum(columns),
-            bytes_accessed=4 * rows * width + 2 * width * sum(columns) + 4 * rows * sum(columns),
+            bytes_accessed=4 * rows * width + 2 * width * sum(columns) + 2 * rows * sum(columns),
             transcendentals=0,
         ),
+        compiler_params=pltpu.CompilerParams(vmem_limit_bytes=(40 if turned else 52) << 20),
         name="rows_product",
     )(shard[None], *operands)
+
+
+def rows_sum_kernel(counts, turned, *refs):
+    number = len(counts)
+    rows_refs, weight_refs = refs[:number], refs[number : 2 * number]
+    mine, other, total = refs[2 * number :]
+    step = pl.program_id(0)
+    start = 0
+    for rows, weight, count in zip(rows_refs, weight_refs, counts):
+
+        @pl.when((step >= start) & (step < start + count))
+        def _(rows=rows, weight=weight, start=start):
+            found = dot_nt(weight[...], rows[...]) if turned else dot_nn(rows[...], weight[...])
+            if start:
+                total[...] += found
+            else:
+                total[...] = jnp.where(step == 0, found, total[...] + found)
+
+        start += count
+
+    @pl.when(step == start - 1)
+    def _():
+        half = mine.shape[0]
+        mine[...] = total[:, :half].T if turned else total[:half, :]
+        other[...] = total[:, half:].T if turned else total[half:, :]
+
+
+def rows_sum(arrays, weights, block, rows, turned):
+    tile = 512
+    width = weights[0].shape[0] if turned else weights[0].shape[1]
+    counts = [a.shape[1] // tile for a in arrays]
+    starts = [sum(counts[:i]) for i in range(len(counts))]
+
+    def at(j, start, number):
+        return jnp.clip(j - start, 0, number - 1)
+
+    in_specs = [
+        pl.BlockSpec((rows, tile), lambda j, a=start, n=number: (block, at(j, a, n)))
+        for start, number in zip(starts, counts)
+    ]
+    for start, number in zip(starts, counts):
+        if turned:
+            in_specs.append(pl.BlockSpec((width, tile), lambda j, a=start, n=number: (0, at(j, a, n))))
+        else:
+            in_specs.append(pl.BlockSpec((tile, width), lambda j, a=start, n=number: (at(j, a, n), 0)))
+    half = pl.BlockSpec((rows // 2, width), lambda j: (0, 0))
+    depth = sum(a.shape[1] for a in arrays)
+    return pl.pallas_call(
+        functools.partial(rows_sum_kernel, counts, turned),
+        grid_spec=pltpu.PrefetchScalarGridSpec(
+            num_scalar_prefetch=0,
+            grid=(sum(counts),),
+            in_specs=in_specs,
+            out_specs=[half, half],
+            scratch_shapes=[pltpu.VMEM((width, rows) if turned else (rows, width), jnp.float32)],
+        ),
+        out_shape=[jax.ShapeDtypeStruct((rows // 2, width), jnp.float32)] * 2,
+        cost_estimate=pl.CostEstimate(
+            flops=2 * rows * width * depth,
+            bytes_accessed=2 * (rows + width) * depth + 4 * rows * width,
+            transcendentals=0,
+        ),
+        name="rows_sum",
+    )(*arrays, *weights)
 
 
 def round_rows_kernel(*refs):
@@ -495,6 +563,7 @@
         out_specs=vmem,
         out_shape=jax.ShapeDtypeStruct((rows, width), jnp.bfloat16),
         cost_estimate=pl.CostEstimate(flops=rows * width, bytes_accessed=6 * rows * width, transcendentals=0),
+        compiler_params=pltpu.CompilerParams(vmem_limit_bytes=14 << 20),
         name="round_rows",
     )(*parts)
 
@@ -526,7 +595,8 @@
 
 
 def retain_forward_kernel(
-    slot_ref, info_ref, places_ref, q_ref, k_ref, v_ref, gate_ref, retained_ref, gated_ref, state_ref, state
+    slot_ref, info_ref, places_ref, q_ref, q_rest_ref, k_ref, k_rest_ref, v_ref, gate_ref,
+    normed_ref, gated_ref, state_ref, weights_ref, scores_ref, column_ref, state,
 ):
     @pl.when(pl.program_id(0) == 0)
     def _():
@@ -534,37 +604,43 @@
 
     first = info_ref[0, 1:2, :1]
     seen, row = causal(first, places_ref[...])
+    number = lax.broadcasted_iota(jnp.int32, column_ref.shape[2:], 1)
     for head in range(state.shape[0]):
         key, val, lane = head_lanes(head)
         weights, reach, trail, keep = block_decay(info_ref[0, 0:1, lane], first, seen, row)
         q, k, v = q_ref[:, key], k_ref[:, key], v_ref[:, val]
         held = state[head].astype(jnp.bfloat16)
         state_ref[head, 0] = held
-        scores = (split_dot(q, k, dot_nt) * weights).astype(jnp.bfloat16)
-        retained = dot_nn(scores, v) + reach * dot_nn(q.astype(jnp.bfloat16), held)
+        scores = dot_nt(q, k) + (dot_nt(q_rest_ref[:, key], k) + dot_nt(q, k_rest_ref[:, key]))
+        scores = (scores * weights).astype(jnp.bfloat16)
+        retained = dot_nn(scores, v) + reach * dot_nn(q, held)
         state[head] = keep * state[head] + dot_tn((k * trail).astype(jnp.bfloat16), v)
-        retained_ref[:, val] = retained
-        normed, _ = norm_parts(retained)
-        gate = gate_ref[:, val]
+        normed, inverse = norm_parts(retained)
+        gate = gate_ref[:, val].astype(jnp.float32)
         gated_ref[:, val] = (gate * jax.nn.sigmoid(gate) * normed).astype(jnp.bfloat16)
+        normed_ref[:, val] = normed
+        weights_ref[head, 0] = weights
+        scores_ref[head, 0] = scores
+        column_ref[head, 0] = jnp.where(
+            number == 0, reach, jnp.where(number == 1, trail, jnp.where(number == 2, inverse, keep))
+        )
 
 
 def retain_backward_kernel(
-    slot_ref, info_ref, places_ref, q_ref, k_ref, v_ref, gate_ref, retained_ref, state_ref, up_ref,
+    slot_ref, q_ref, k_ref, v_ref, gate_ref, normed_ref, state_ref, weights_ref, scores_ref, column_ref, up_ref,
     dq_ref, dk_ref, dv_ref, dgate_ref, beyond,
 ):
     @pl.when(pl.program_id(0) == 0)
     def _():
         beyond[...] = jnp.zeros_like(beyond)
 
-    first = info_ref[0, 1:2, :1]
-    seen, row = causal(first, places_ref[...])
     for head in range(beyond.shape[0]):
-        key, val, lane = head_lanes(head)
-        weights, reach, trail, keep = block_decay(info_ref[0, 0:1, lane], first, seen, row)
-        q, k, v = q_ref[:, key], k_ref[:, key], v_ref[:, val]
-        gate, up = gate_ref[:, val], up_ref[:, val]
-        normed, inverse = norm_parts(retained_ref[:, val])
+        key, val, _ = head_lanes(head)
+        column = column_ref[head, 0]
+        reach, trail, inverse, keep = column[:, 0:1], column[:, 1:2], column[:, 2:3], column[0:1, 3:4]
+        weights, scores = weights_ref[head, 0], scores_ref[head, 0]
+        q, k, v, normed = q_ref[:, key], k_ref[:, key], v_ref[:, val], normed_ref[:, val]
+        gate, up = gate_ref[:, val].astype(jnp.float32), up_ref[:, val].astype(jnp.float32)
         sig = jax.nn.sigmoid(gate)
         silu = gate * sig
         dgate_ref[:, val] = (up * normed * (sig + silu * (1.0 - sig))).astype(jnp.bfloat16)
@@ -573,11 +649,9 @@
         mean_gn = jnp.mean(g * normed, axis=-1, keepdims=True)
         grad = (g - mean_g - normed * mean_gn) * inverse
         after_block = beyond[head].astype(jnp.bfloat16)
-        scores = (split_dot(q, k, dot_nt) * weights).astype(jnp.bfloat16)
         dscores = (half_split_dot(grad, v, dot_nt) * weights).astype(jnp.bfloat16)
         grad = grad.astype(jnp.bfloat16)
         q_reach = (q * reach).astype(jnp.bfloat16)
-        q, k = q.astype(jnp.bfloat16), k.astype(jnp.bfloat16)
         dq_ref[:, key] = (dot_nn(dscores, k) + reach * dot_nt(grad, state_ref[head, 0])).astype(jnp.bfloat16)
         dk = dot_tn(dscores, q) + trail * dot_nt(v, after_block)
         dk_ref[:, key] = (dk * (1.0 / math.sqrt(DK))).astype(jnp.bfloat16)
@@ -587,31 +661,37 @@
 
 def retain_specs(heads, blocks, width, reverse):
     at = (lambda b: blocks - 1 - b) if reverse else (lambda b: b)
-    info = pl.BlockSpec((1, 8, width), lambda b, slot: (slot[at(b)], 0, 0))
+    info = pl.BlockSpec((1, 8, width), lambda b, slot: (at(b), 0, 0))
     places = pl.BlockSpec((1, BLK), lambda b, slot: (0, 0))
     key = pl.BlockSpec((BLK, heads * DK), lambda b, slot: (slot[at(b)], 0))
     val = pl.BlockSpec((BLK, heads * DV), lambda b, slot: (slot[at(b)], 0))
-    state = pl.BlockSpec((heads, 1, DK, DV), lambda b, slot: (0, at(b), 0, 0))
-    return info, places, key, val, state
-
-
-def retain_forward(slot, info, places, q, k, v, gate):
-    rows, heads = q.shape[0], q.shape[1] // DK
+    held = [
+        pl.BlockSpec((heads, 1, up, across), lambda b, slot: (0, at(b), 0, 0))
+        for up, across in ((DK, DV), (BLK, BLK), (BLK, BLK), (BLK, 128))
+    ]
+    return info, places, key, val, held
+
+
+def retain_forward(slot, info, places, queries_keys, v, gate):
+    rows, heads = v.shape[0], v.shape[1] // DV
     blocks = rows // BLK
-    info_at, places_at, key, val, state = retain_specs(heads, blocks, info.shape[2], False)
+    info_at, places_at, key, val, held = retain_specs(heads, blocks, info.shape[2], False)
     return pl.pallas_call(
         retain_forward_kernel,
         grid_spec=pltpu.PrefetchScalarGridSpec(
             num_scalar_prefetch=1,
             grid=(blocks,),
-            in_specs=[info_at, places_at, key, key, val, val],
-            out_specs=[val, val, state],
+            in_specs=[info_at, places_at, key, key, key, key, val, val],
+            out_specs=[val, val, *held],
             scratch_shapes=[pltpu.VMEM((heads, DK, DV), jnp.float32)],
         ),
         out_shape=[
             jax.ShapeDtypeStruct((rows, heads * DV), jnp.float32),
             jax.ShapeDtypeStruct((rows, heads * DV), jnp.bfloat16),
             jax.ShapeDtypeStruct((heads, blocks, DK, DV), jnp.bfloat16),
+            jax.ShapeDtypeStruct((heads, blocks, BLK, BLK), jnp.float32),
+            jax.ShapeDtypeStruct((heads, blocks, BLK, BLK), jnp.bfloat16),
+            jax.ShapeDtypeStruct((heads, blocks, BLK, 128), jnp.float32),
         ],
         cost_estimate=pl.CostEstimate(
             flops=2 * heads * rows * (BLK * (3 * DK + DV) + 2 * DK * DV),
@@ -619,19 +699,19 @@
             transcendentals=rows * heads * (BLK + DV),
         ),
         name="retain_forward",
-    )(slot, info, places, q, k, v, gate)
-
-
-def retain_backward(slot, info, places, q, k, v, gate, retained, states, up):
-    rows, heads = q.shape[0], q.shape[1] // DK
+    )(slot, info, places, *queries_keys, v, gate)
+
+
+def retain_backward(slot, queries_keys, v, gate, normed, held, up):
+    rows, heads = v.shape[0], v.shape[1] // DV
     blocks = rows // BLK
-    info_at, places_at, key, val, state = retain_specs(heads, blocks, info.shape[2], True)
+    _, _, key, val, held_at = retain_specs(heads, blocks, 0, True)
     return pl.pallas_call(
         retain_backward_kernel,
         grid_spec=pltpu.PrefetchScalarGridSpec(
             num_scalar_prefetch=1,
             grid=(blocks,),
-            in_specs=[info_at, places_at, key, key, val, val, val, state, val],
+            in_specs=[key, key, val, val, val, *held_at, val],
             out_specs=[key, key, val, val],
             scratch_shapes=[pltpu.VMEM((heads, DK, DV), jnp.float32)],
         ),
@@ -647,7 +727,7 @@
             transcendentals=rows * heads * (BLK + DV),
         ),
         name="retain_backward",
-    )(slot, info, places, q, k, v, gate, retained, states, up)
+    )(slot, *queries_keys, v, gate, normed, *held, up)
 
 
 def norm_grad(grad, gain, centred_unit, inverse):
@@ -679,7 +759,6 @@
     rows, width = tokens.shape
     half = rows // 2
     total = shards * rows
-    own = (shards - 2) * rows
     quarter = half // 2
     slab = width // shards
     key_scale = 1.0 / math.sqrt(DK)
@@ -698,18 +777,23 @@
     def far_hops():
         return [[(i, (i + hop) % shards) for i in range(shards)] for hop in range(2, shards, 2)]
 
-    def over_steps(own_rows, steps, weights, kinds, scales, turned):
-        common = (weights, kinds, scales, turned, place)
-        found = rows_product([own_rows], rows, *common, shards - 2, total)
-        for index, parts in enumerate(steps):
-            last = index + 1 == len(steps)
-            found = rows_product(parts, quarter if last else half, *common, shards - 1 if last else index, total, found)
+    def over_steps(own_parts, steps, groups, weights, pieces, scales, turned):
+        common = (weights, pieces, scales, turned, place)
+        found = rows_product(own_parts, rows // len(own_parts), *common, shards - 2, total)
+        for index, group in enumerate(groups):
+            parts = [part for step in group for part in steps[step]]
+            last = index + 1 == len(groups)
+            block = shards - 1 if last else group[0] // len(group)
+            found = rows_product(parts, quarter if last else half, *common, block, total, found)
         return found
 
-    normed_own, normed_half = norm_start(core, first_start, tokens, first_gain, log_decay)
+    normed_own, normed_half, info = norm_start(core, first_start, tokens, first_gain, log_decay)
     came = ring_gather(normed_half, quarter)
-    info = [item[half:] for step in came[:-1] for item in (step[0], step[2])]
-    info = jnp.stack(info + [normed_half[half:], came[-1][1][quarter:]])
+    info = info[None]
+    for index in range(shards.bit_length() - 1):
+        moved = lax.ppermute(info, SEQ, [(i, i ^ (1 << index)) for i in range(shards)])
+        upper = (place >> index) & 1 == 1
+        info = jnp.concatenate([jnp.where(upper, moved, info), jnp.where(upper, info, moved)], axis=0)
     slot = ring_slots()
     lanes = jnp.arange(half)
     places = jnp.concatenate([core * half + lanes, (1 - core) * half + lanes]).astype(f32)[None]
@@ -735,18 +819,18 @@
     cotangent_far = far_parts(cotangent_far)
     cotangent_far = round_rows(cotangent_far)
 
-    in_slab, queries, keys, values, gate_pre = over_steps(
-        normed_own,
+    in_slab, *queries_keys, values, gate_pre = over_steps(
+        [normed_own],
         came,
+        [[step] for step in range(shards // 2)],
         [query_weight, key_weight, value_weight, gate_weight],
-        [f32, f32, bf16, f32],
+        [2, 2, 1, 1],
         [1.0, key_scale, 1.0, 1.0],
         False,
     )
-    retained, gated, states = retain_forward(slot, info, places, queries, keys, values, gate_pre)
-
-    out_other = matmul(gated[own + half : own + rows], output_weight)
-    out_mine = matmul(gated[own : own + half], output_weight)
+    normed, gated, *held = retain_forward(slot, info, places, queries_keys, values, gate_pre)
+
+    out_mine, out_other = rows_sum([gated], [output_weight], shards - 2, rows, False)
     residual = token_half + head_total(out_mine, out_other)
     mid_unit, mid_inverse = norm_parts(residual)
     normed_mid_half = 0.5 * (mid_unit * second_gain)
@@ -765,19 +849,20 @@
 
     hidden, grad_up_gate, grad_up = feed_forward(normed_mid_own, transpose_right(cotangent_own, down_weight))
 
-    def mid_part(at):
-        return transpose_right(grad_up_gate[at : at + half], gelu_weight) + transpose_right(
-            grad_up[at : at + half], linear_weight
-        )
-
-    mid_other = mid_part(half)
-    mid_mine = mid_part(0)
+    mid_mine, mid_other = rows_sum([grad_up_gate, grad_up], [gelu_weight, linear_weight], 0, rows, True)
     grad_mid = head_total(mid_mine, mid_other)
     grad_residual = cotangent_half + norm_grad(grad_mid, second_gain, mid_unit, mid_inverse)
     second_part = 0.5 * jnp.sum(grad_mid * mid_unit, axis=0)
     branch_came = ring_gather(grad_residual, quarter)
+    steps = list(range(shards // 2))
     branch_slab, grad_gated = over_steps(
-        jnp.concatenate([grad_residual, other_core(grad_residual)], axis=0), branch_came, [output_weight], [f32], [1.0], True
+        [grad_residual, other_core(grad_residual)],
+        branch_came,
+        [steps[:2]] + [[step] for step in steps[2:]] if shards > 4 else [[step] for step in steps],
+        [output_weight],
+        [1],
+        [1.0],
+        True,
     )
 
     mid_far = far_parts(mid_far)
@@ -785,10 +870,8 @@
     normed_mid_far = round_rows(mid_far)
     hidden_far, grad_up_gate_far, grad_up_far = feed_forward(normed_mid_far, grad_hidden_far)
 
-    res_other = matmul(hidden[half:], down_weight)
-    res_mine = matmul(hidden[:half], down_weight)
-    result = 0.5 * (after(residual, branch_came[1][0]) + head_total(res_mine, res_other))
-    output_rows = narrow(in_order(result, other_core(result)))
+    res_mine, res_other = rows_sum([hidden], [down_weight], 0, rows, False)
+    hidden_total = head_total(res_mine, res_other)
 
     def pair_slab(a):
         return lax.dynamic_slice_in_dim(a, shard // 2 * (2 * slab), 2 * slab, 1)
@@ -808,20 +891,18 @@
 
     wgrad_output = transpose_left(gated, branch_slab)
     grad_queries, grad_keys, grad_values, grad_gate_pre = retain_backward(
-        slot, info, places, queries, keys, values, gate_pre, retained, states, grad_gated
-    )
-
-    def in_part(at):
-        at = slice(own + at, own + at + half)
-        return (
-            transpose_right(grad_queries[at], query_weight)
-            + transpose_right(grad_keys[at], key_weight)
-            + transpose_right(grad_values[at], value_weight)
-            + transpose_right(grad_gate_pre[at], gate_weight)
-        )
-
-    in_other = in_part(half)
-    in_mine = in_part(0)
+        slot, queries_keys[::2], values, gate_pre, normed, held, grad_gated
+    )
+
+    in_mine, in_other = rows_sum(
+        [grad_queries, grad_keys, grad_values, grad_gate_pre],
+        [query_weight, key_weight, value_weight, gate_weight],
+        shards - 2,
+        rows,
+        True,
+    )
+    result = 0.5 * (after(residual, in_mine) + hidden_total)
+    output_rows = narrow(in_order(result, other_core(result)))
     grad_in = head_total(in_mine, in_other)
     wgrad_query = transpose_left(in_slab, grad_queries)
     wgrad_key = transpose_left(in_slab, grad_keys)
@@ -854,7 +935,7 @@
     tokens = lax.axis_size(SEQ) * arrays[0].shape[0]
     columns = sum(w.shape[1] for w in (*arrays[2:6], *arrays[8:10])) + arrays[6].shape[0] + arrays[10].shape[0]
     shards, groups = lax.axis_size(SEQ), lax.axis_size(HEAD)
-    if groups == 4 and shards % 2 == 0 and arrays[0].shape[0] == BLK and 4 * tokens <= groups * columns:
+    if groups == 4 and shards in (4, 8, 16) and arrays[0].shape[0] == BLK and 4 * tokens <= groups * columns:
         return local_gather(*arrays)
     return local_scatter(*arrays)
 

time: 593 us -> 577 us (0.973)
  matrix products: 94.9 us -> 57.6 us
  waiting for transfers between devices: 207 us -> 221 us
  starting transfers between devices: 69.3 us -> 77.5 us
    ppermute x0 -> x3, waiting for transfers between devices: none -> 35.5 us  [local_gather(): lax.ppermute(info, SEQ, [(i, i ^ 1 << index) for i in range(shards)])]
    dot_general x14 -> x2, matrix products: 38.9 us -> 6.39 us  [transpose_right(): lax.dot_general(left_side, right_side, (((1,), (1,)), ((), ())), preferre...]
    ppermute x8, waiting for transfers between devices: 77.6 us -> 46.7 us  [ring_gather(): lax.ppermute(rising, SEQ, up)]
    pallas_call x10 -> x13, Pallas kernels: 99.3 us -> 114 us  [the longest x9 84.1 us: rows_product(): pl.pallas_call(functools.partial(rows_product_kernel, count, tiles, piece...]
    ppermute x0 -> x3, starting transfers between devices: none -> 8.02 us  [local_gather(): lax.ppermute(info, SEQ, [(i, i ^ 1 << index) for i in range(shards)])]
    ppermute x6, waiting for transfers between devices: 26.4 us -> 19.2 us  [far_parts(): both = [item, lax.ppermute(item, HEAD, ACROSS)]]
    dot_general x8 -> x4, matrix products: 34 us -> 27.3 us  [matmul(): return jnp.dot(left_side, right_side, preferred_element_type=jnp.float32)]
    unnamed x165 -> x140, local copies, waits for them, and re-layouts: 17.3 us -> 19.6 us
  transfers between devices with their start and end apart: 76 -> 79, of which waited for: 20 -> 28; matrix products, arithmetic and copies ran while one was open for 22% -> 14% of each run, Pallas kernels for 22% -> 22%
where the time goes in v2:
time: 577 us; the launch traced here: 570 us
  waiting for transfers between devices  221 us (38%)
  Pallas kernels  165 us (29%)
  starting transfers between devices  77.5 us (13%)
  matrix products  57.6 us (10%)
  other arithmetic  23.1 us (4%)
  local copies, waits for them, and re-layouts  23 us (4%)
    pallas_call x9, Pallas kernels, rows_product(): pl.pallas_call(functools.partial(rows_product_kernel, count, tiles, piece...  84.1 us
    ppermute x6, waiting for transfers between devices, far_start(): return [lax.ppermute(share, SEQ, hop) for hop in far_hops()]  58.2 us
    ppermute x8, waiting for transfers between devices, ring_gather(): lax.ppermute(rising, SEQ, up)  46.7 us
    ppermute x4, waiting for transfers between devices, head_total(): return both + lax.ppermute(both, HEAD, ACROSS)  39.4 us
    ppermute x3, waiting for transfers between devices, local_gather(): lax.ppermute(info, SEQ, [(i, i ^ 1 << index) for i in range(shards)])  35.5 us
    pallas_call x4, Pallas kernels, rows_sum(): pl.pallas_call(functools.partial(rows_sum_kernel, counts, turned), grid_s...  30 us
    dot_general x4, matrix products, matmul(): return jnp.dot(left_side, right_side, preferred_element_type=jnp.float32)  27.3 us
    pallas_call x1, Pallas kernels, retain_backward(): pl.pallas_call(retain_backward_kernel, grid_spec=pltpu.PrefetchScalarGrid...  24.6 us
  transfers between devices with their start and end apart: 79, of which 28 were waited for; matrix products, arithmetic and copies ran while one was open for 14% of the time, Pallas kernels for 22%

profile of v2, /device:TPU:0, one launch (start us, length us, event | category | flops | bytes accessed | tf_op | source)
XLA Modules:
  0.0 570.2 jit_solution(458810376422954274)
XLA Ops:
  5.6 3.1 collective-permute-start.3
  8.7 23.2 %collective-permute-done.3.refs_0_.refs_4_ = f32[128,2048]{1,0:T(8,128)} collective-permute-done((f32[128,2048]{1,0:T(8,128)S(1)}, f32[128,2048]{1,0:T(8,128)}, u32[]{:S(2)}, u32[]{:S(2)}) %collective-permute-start.3) | collective-permute-done | bytes 1048608 | tf_op jit(solution)/shard_map/ppermute | solution.py:301
  35.7 11.2 %rows_product.9 = (bf16[2048,256]{1,0:T(8,128)(2,1)S(1)}, bf16[2048,512]{1,0:T(8,128)(2,1)}, bf16[2048,512]{1,0:T(8,128)(2,1)}, bf16[2048,512]{1,0:T(8,128)(2,1)...) custom-call(s32[1]{0:T(128)} %bitcast.5.shard_ref, ...), custom_call_target="tpu_custom_call" | custom-call | flops 3221225472 | bytes 16252928 | tf_op jit(solution)/shard_map/rows_product/pallas_call | solution.py:463
  46.9 9.8 %collective-permute-done = f32[1,8,512]{2,1,0:T(8,128)S(1)} collective-permute-done((f32[1,8,512]{2,1,0:T(8,128)S(1)}, f32[1,8,512]{2,1,0:T(8,128)S(1)}, u32[]{:S(2)}, u32[]{:S(2)}) %collective-permute-start) | collective-permute-done | bytes 16416 | tf_op jit(solution)/shard_map/ppermute | solution.py:794
  60.1 23.2 %collective-permute-done.1 = f32[2,8,512]{2,1,0:T(8,128)S(1)} collective-permute-done((f32[2,8,512]{2,1,0:T(8,128)S(1)}, f32[2,8,512]{2,1,0:T(8,128)S(1)}, u32[]{:S(2)}, u32[]{:S(2)}) %collective-permute-start.1) | collective-permute-done | bytes 32800 | tf_op jit(solution)/shard_map/ppermute | solution.py:794
  83.3 5.1 collective-permute-start.2
  89.0 2.4 collective-permute-done.2
  93.6 15.4 %rows_product.10 = (bf16[2048,256]{1,0:T(8,128)(2,1)S(1)}, bf16[2048,512]{1,0:T(8,128)(2,1)}, bf16[2048,512]{1,0:T(8,128)(2,1)}, bf16[2048,512]{1,0:T(8,128)(2,1...) custom-call(s32[1]{0:T(128)} %bitcast.5.shard_ref, ...), custom_call_target="tpu_custom_call", output_to_operand_aliasing={{0}: (13, {}), {1}: (14, {}), {2}: (15, {}), {3}: (16, {}),... | custom-call | flops 6442450944 | bytes 19922944 | tf_op jit(solution)/shard_map/rows_product/pallas_call | solution.py:463
  112.4 15.3 %rows_product.11 = (bf16[2048,256]{1,0:T(8,128)(2,1)S(1)}, bf16[2048,512]{1,0:T(8,128)(2,1)}, bf16[2048,512]{1,0:T(8,128)(2,1)}, bf16[2048,512]{1,0:T(8,128)(2,1...) custom-call(s32[1]{0:T(128)} %bitcast.5.shard_ref, ...), custom_call_target="tpu_custom_call", output_to_operand_aliasing={{0}: (13, {}), {1}: (14, {}), {2}: (15, {}), {3}: (16, {}),... | custom-call | flops 6442450944 | bytes 19922944 | tf_op jit(solution)/shard_map/rows_product/pallas_call | solution.py:463
  129.7 15.2 %rows_product.12 = (bf16[2048,256]{1,0:T(8,128)(2,1)S(1)}, bf16[2048,512]{1,0:T(8,128)(2,1)}, bf16[2048,512]{1,0:T(8,128)(2,1)}, bf16[2048,512]{1,0:T(8,128)(2,1...) custom-call(s32[1]{0:T(128)} %bitcast.5.shard_ref, ...), custom_call_target="tpu_custom_call", output_to_operand_aliasing={{0}: (13, {}), {1}: (14, {}), {2}: (15, {}), {3}: (16, {}),... | custom-call | flops 6442450944 | bytes 19922944 | tf_op jit(solution)/shard_map/rows_product/pallas_call | solution.py:463
  146.7 11.3 %rows_product.13 = (bf16[2048,256]{1,0:T(8,128)(2,1)}, bf16[2048,512]{1,0:T(8,128)(2,1)}, bf16[2048,512]{1,0:T(8,128)(2,1)}, bf16[2048,512]{1,0:T(8,128)(2,1)}, ...) custom-call(s32[1]{0:T(128)} %bitcast.5.shard_ref, ...), custom_call_target="tpu_custom_call", output_to_operand_aliasing={{0}: (13, {}), {1}: (14, {}), {2}: (15, {}), {3}: (16, {}),... | custom-call | flops 3221225472 | bytes 16252928 | tf_op jit(solution)/shard_map/rows_product/pallas_call | solution.py:463
  158.0 20.4 %retain_forward.1 = (f32[2048,1024]{1,0:T(8,128)}, bf16[2048,1024]{1,0:T(8,128)(2,1)}, bf16[2,8,256,512]{3,2,1,0:T(8,128)(2,1)}, f32[2,8,256,256]{3,2,1,0:T(8,12...) custom-call(s32[8]{0:T(128)} %compare_select_fusion.4.slot_ref, ...), custom_call_target="tpu_custom_call" | custom-call | flops 4831838208 | bytes 33554432 | tf_op jit(solution)/shard_map/retain_forward/pallas_call | solution.py:679
  178.5 4.6 rows_sum.4
  183.2 2.7 collective-permute-done.19
  189.1 23.5 %collective-permute-done.20 = f32[128,2048]{1,0:T(8,128)S(1)} collective-permute-done((f32[128,2048]{1,0:T(8,128)S(1)}, f32[128,2048]{1,0:T(8,128)S(1)}, u32[]{:S(2)}, u32[]{:S(2)}) %collective-permute-start.20) | collective-permute-done | bytes 1048608 | tf_op jit(solution)/shard_map/ppermute | solution.py:280
  216.6 2.8 collective-permute-start.72
  220.7 9.9 %collective-permute-done.64.refs_0_ = f32[64,2048]{1,0:T(8,128)S(1)} collective-permute-done((f32[64,2048]{1,0:T(8,128)S(1)}, f32[64,2048]{1,0:T(8,128)S(1)}, u32[]{:S(2)}, u32[]{:S(2)}) %collective-permute-start.64) | collective-permute-done | bytes 524320 | tf_op jit(solution)/shard_map/ppermute | solution.py:809
  232.2 20.4 %collective-permute-done.68.refs_4_ = f32[64,2048]{1,0:T(8,128)S(1)} collective-permute-done((f32[64,2048]{1,0:T(8,128)S(1)}, f32[64,2048]{1,0:T(8,128)S(1)}, u32[]{:S(2)}, u32[]{:S(2)}) %collective-permute-start.68) | collective-permute-done | bytes 524320 | tf_op jit(solution)/shard_map/ppermute | solution.py:809
  257.4 4.1 multiply_convert_fusion.4
  263.1 8.3 %rows_sum.5 = (f32[128,2048]{1,0:T(8,128)}, f32[128,2048]{1,0:T(8,128)}) custom-call(bf16[256,1024]{1,0:T(8,128)(2,1)} %get-tuple-element.166.refs_0_, bf16[256,1024]{1,0:T(8,128)(2,1)} %get-tuple-element.165.refs_1_, bf16[2048,1024]{1,0:T(8,128)(2,1)} %refs_2_.3, bf16[2048,1024]{1,0:T(8,128)(2,1)} %refs_3_.3), custom_call_target="tpu_custom_call" | custom-call | flops 2147483648 | bytes 11534336 | tf_op jit(solution)/shard_map/rows_sum/pallas_call | solution.py:529
  271.9 5.5 collective-permute-done.73.refs_9_
  281.0 2.6 round_rows.3
  287.6 9.6 %collective-permute-start.52 = (f32[64,2048]{1,0:T(8,128)S(1)}, f32[64,2048]{1,0:T(8,128)S(1)}, u32[]{:S(2)}, u32[]{:S(2)}) collective-permute-start(f32[64,2048]{1,0:T(8,128)S(1)} %constant_dynamic-slice_fusion.5), channel_id=1, source_target_pairs={{0,8},{4,12},{8,16},{12,20},{16,24},{20,28},{24,0},{28,4},{1,9},{5... | collective-permute-start | bytes 1572872 | tf_op jit(solution)/shard_map/ppermute | solution.py:809
  297.1 3.4 collective-permute-start.56
  301.0 5.1 fusion.66
  306.1 6.8 %collective-permute-done.52.refs_0_ = f32[64,2048]{1,0:T(8,128)S(1)} collective-permute-done((f32[64,2048]{1,0:T(8,128)S(1)}, f32[64,2048]{1,0:T(8,128)S(1)}, u32[]{:S(2)}, u32[]{:S(2)}) %collective-permute-start.52) | collective-permute-done | bytes 524320 | tf_op jit(solution)/shard_map/ppermute | solution.py:809
  313.4 21.1 %collective-permute-done.56.refs_4_ = f32[64,2048]{1,0:T(8,128)S(1)} collective-permute-done((f32[64,2048]{1,0:T(8,128)S(1)}, f32[64,2048]{1,0:T(8,128)S(1)}, u32[]{:S(2)}, u32[]{:S(2)}) %collective-permute-start.56) | collective-permute-done | bytes 524320 | tf_op jit(solution)/shard_map/ppermute | solution.py:809
  338.0 11.3 %collective-permute-done.57.refs_5_ = f32[64,2048]{1,0:T(8,128)S(1)} collective-permute-done((f32[64,2048]{1,0:T(8,128)S(1)}, f32[64,2048]{1,0:T(8,128)S(1)}, u32[]{:S(2)}, u32[]{:S(2)}) %collective-permute-start.57) | collective-permute-done | bytes 524320 | tf_op jit(solution)/shard_map/ppermute | solution.py:814
  349.3 7.8 %collective-permute-start.24 = (f32[128,2048]{1,0:T(8,128)S(1)}, f32[128,2048]{1,0:T(8,128)}, u32[]{:S(2)}, u32[]{:S(2)}) collective-permute-start(f32[128,2048]{1,0:T(8,128)S(1)} %convert_add_fusion.1.refs_0_.refs_2_), channel_id=1, source_target_pairs={{0,8},{8,16},{16,24},{24,28},{28,20},{20,12},{12,4},{4,0},{1,9},{9... | collective-permute-start | bytes 3145736 | tf_op jit(solution)/shard_map/ppermute | solution.py:301
  360.3 4.6 rows_sum.7
  364.9 3.1 fusion.34
  373.3 3.2 collective-permute-done.24.refs_0_.refs_8_
  376.4 4.1 collective-permute-start.25
  380.5 8.1 %collective-permute-done.28.refs_2_.refs_10_ = f32[128,2048]{1,0:T(8,128)} collective-permute-done((f32[128,2048]{1,0:T(8,128)S(1)}, f32[128,2048]{1,0:T(8,128)}, u32[]{:S(2)}, u32[]{:S(2)}) %collective-permute-start.28) | collective-permute-done | bytes 1048608 | tf_op jit(solution)/shard_map/ppermute | solution.py:301
  388.8 16.6 %fusion = (f32[768,1024]{1,0:T(8,128)S(1)}, f32[768,1024]{1,0:T(8,128)S(1)}) fusion(bf16[768,2048]{1,0:T(8,128)(2,1)S(1)} %round_rows.2, bf16[2048,1024]{1,0:T(8,128)(2,1)S(1)} %copy-done.53), kind=kOutput, calls=%fused_computation.1 | convolution fusion | flops 3269984256 | bytes 13631488 | tf_op jit(solution)/shard_map/dot_general | solution.py:40
  405.5 5.4 fusion.67
  416.0 4.4 convolution_add_fusion
  420.5 16.0 %collective-permute-done.26.refs_0_.refs_4_ = f32[128,2048]{1,0:T(8,128)S(1)} collective-permute-done((f32[128,2048]{1,0:T(8,128)S(1)}, f32[128,2048]{1,0:T(8,128)S(1)}, u32[]{:S(2)}, u32[]{:S(2)}) %collective-permute-start.26) | collective-permute-done | bytes 1048608 | tf_op jit(solution)/shard_map/ppermute | solution.py:301
  449.8 4.4 collective-permute-done.27.refs_0_.refs_4_
  458.7 7.8 %rows_product.15 = (bf16[2048,256]{1,0:T(8,128)(2,1)S(1)}, bf16[2048,1024]{1,0:T(8,128)(2,1)S(1)}) custom-call(s32[1]{0:T(128)} %bitcast.5.shard_ref, f32[128,2048]{1,0:T(8,128)} %collective-permute-done.24.refs_0_.refs_8_, f32[128,2048]{1,0:T(8,128)S(1)} %collective-permute-done.36.refs_1_.refs_9_, ...), custom_call_target="tpu_custom_call", output_to_operand_aliasing={{0}: (18, {}), {1}: (19, {})} | custom-call | flops 4294967296 | bytes 14680064 | tf_op jit(solution)/shard_map/rows_product/pallas_call | solution.py:463
  468.7 3.0 rows_product.16
  472.0 3.1 rows_product.17
  478.1 24.6 %retain_backward.1 = (bf16[2048,512]{1,0:T(8,128)(2,1)}, bf16[2048,512]{1,0:T(8,128)(2,1)}, bf16[2048,1024]{1,0:T(8,128)(2,1)}, bf16[2048,1024]{1,0:T(8,128)(2,1)}) custom-call(s32[8]{0:T(128)} %compare_select_fusion.4.slot_ref, bf16[2048,512]{1,0:T(8,128)(2,1)} %get-tuple-element.113.q_ref, bf16[2048,512]{1,0:T(8,128)(2,1)} %get-tuple-element.115.k_ref, ...), custom_call_target="tpu_custom_call" | custom-call | flops 10200547328 | bytes 54525952 | tf_op jit(solution)/shard_map/retain_backward/pallas_call | solution.py:709
  502.7 12.5 %rows_sum.6 = (f32[128,2048]{1,0:T(8,128)}, f32[128,2048]{1,0:T(8,128)}) custom-call(bf16[2048,512]{1,0:T(8,128)(2,1)} %get-tuple-element.136.refs_0_, bf16[2048,512]{1,0:T(8,128)(2,1)} %get-tuple-element.137.refs_1_, bf16[2048,1024]{1,0:T(8,128)(2,1)} %get-tuple-element.138.refs_2_, bf16[2048,1024]{1,0:T(8,128)(2,1)} %get-tuple-element.139.refs_3_, ...), custom_call_target="tpu_custom_call" | custom-call | flops 3221225472 | bytes 16252928 | tf_op jit(solution)/shard_map/rows_sum/pallas_call | solution.py:529
  518.6 4.6 fusion.65
  523.2 2.8 collective-permute-start.47
  540.0 2.4 dynamic-slice_add_fusion
  542.4 15.9 %collective-permute-done.45 = f32[128,2048]{1,0:T(8,128)S(1)} collective-permute-done((f32[128,2048]{1,0:T(8,128)S(1)}, f32[128,2048]{1,0:T(8,128)S(1)}, u32[]{:S(2)}, u32[]{:S(2)}) %collective-permute-start.45) | collective-permute-done | bytes 1048608 | tf_op jit(solution)/shard_map/ppermute | solution.py:280
  (341 shorter events, 115.5 us)
Async XLA Ops:
  5.6 26.3 %collective-permute-start.3 = (f32[128,2048]{1,0:T(8,128)S(1)}, f32[128,2048]{1,0:T(8,128)}, u32[]{:S(2)}, u32[]{:S(2)}) collective-permute-start(f32[128,2048]{1,0:T(8,128)S(1)} %get-tuple-element.83), channel_id=1, source_target_pairs={{0,8},{8,16},{16,24},{24,28},{28,20},{20,12},{12,4},{4,0},{1,9},{9... | collective-permute-start | bytes 3145736 | tf_op jit(solution)/shard_map/ppermute | solution.py:301
  8.7 25.0 %collective-permute-start.7 = (f32[128,2048]{1,0:T(8,128)S(1)}, f32[128,2048]{1,0:T(8,128)}, u32[]{:S(2)}, u32[]{:S(2)}) collective-permute-start(f32[128,2048]{1,0:T(8,128)S(1)} %get-tuple-element.83), channel_id=1, source_target_pairs={{8,0},{16,8},{24,16},{28,24},{20,28},{12,20},{4,12},{0,4},{9,1},{1... | collective-permute-start | bytes 3145736 | tf_op jit(solution)/shard_map/ppermute | solution.py:301
  31.9 24.9 %collective-permute-start.4 = (f32[128,2048]{1,0:T(8,128)}, f32[128,2048]{1,0:T(8,128)}, u32[]{:S(2)}, u32[]{:S(2)}) collective-permute-start(f32[128,2048]{1,0:T(8,128)} %collective-permute-done.3.refs_0_.refs_4_), channel_id=1, source_target_pairs={{0,8},{8,16},{16,24},{24,28},{28,20},{20,12},{12,4},{4,0},{1,9},{9... | collective-permute-start | bytes 3145736 | tf_op jit(solution)/shard_map/ppermute | solution.py:301
  33.7 24.4 %collective-permute-start.8 = (f32[128,2048]{1,0:T(8,128)}, f32[128,2048]{1,0:T(8,128)}, u32[]{:S(2)}, u32[]{:S(2)}) collective-permute-start(f32[128,2048]{1,0:T(8,128)} %collective-permute-done.7.refs_2_.refs_6_), channel_id=1, source_target_pairs={{8,0},{16,8},{24,16},{28,24},{20,28},{12,20},{4,12},{0,4},{9,1},{1... | collective-permute-start | bytes 3145736 | tf_op jit(solution)/shard_map/ppermute | solution.py:301
  33.9 22.9 %collective-permute-start = (f32[1,8,512]{2,1,0:T(8,128)S(1)}, f32[1,8,512]{2,1,0:T(8,128)S(1)}, u32[]{:S(2)}, u32[]{:S(2)}) collective-permute-start(f32[1,8,512]{2,1,0:T(8,128)S(1)} %bitcast.38), channel_id=1, source_target_pairs={{0,4},{4,0},{8,12},{12,8},{16,20},{20,16},{24,28},{28,24},{1,5},{5... | collective-permute-start | bytes 49160 | tf_op jit(solution)/shard_map/ppermute | solution.py:794
  35.7 55.7 %collective-permute-start.17 = (f32[128,2048]{1,0:T(8,128)}, f32[128,2048]{1,0:T(8,128)}, u32[]{:S(2)}, u32[]{:S(2)}) collective-permute-start(f32[128,2048]{1,0:T(8,128)} %collective-permute-done.3.refs_0_.refs_4_), channel_id=1, source_target_pairs={{0,1},{1,0},{2,3},{3,2},{4,5},{5,4},{6,7},{7,6},{8,9},{9,8},{10,11... | collective-permute-start | bytes 3145736 | tf_op jit(solution)/shard_map/ppermute | solution.py:284
  56.8 36.9 %collective-permute-start.18 = (f32[128,2048]{1,0:T(8,128)}, f32[128,2048]{1,0:T(8,128)}, u32[]{:S(2)}, u32[]{:S(2)}) collective-permute-start(f32[128,2048]{1,0:T(8,128)} %collective-permute-done.7.refs_2_.refs_6_), channel_id=1, source_target_pairs={{0,1},{1,0},{2,3},{3,2},{4,5},{5,4},{6,7},{7,6},{8,9},{9,8},{10,11... | collective-permute-start | bytes 3145736 | tf_op jit(solution)/shard_map/ppermute | solution.py:284
  56.8 36.3 %collective-permute-start.5 = (f32[128,2048]{1,0:T(8,128)}, f32[128,2048]{1,0:T(8,128)S(1)}, u32[]{:S(2)}, u32[]{:S(2)}) collective-permute-start(f32[128,2048]{1,0:T(8,128)} %collective-permute-done.4.refs_0_.refs_4_), channel_id=1, source_target_pairs={{0,8},{8,16},{16,24},{24,28},{28,20},{20,12},{12,4},{4,0},{1,9},{9... | collective-permute-start | bytes 3145736 | tf_op jit(solution)/shard_map/ppermute | solution.py:301
  58.0 35.1 %collective-permute-start.9 = (f32[128,2048]{1,0:T(8,128)}, f32[128,2048]{1,0:T(8,128)S(1)}, u32[]{:S(2)}, u32[]{:S(2)}) collective-permute-start(f32[128,2048]{1,0:T(8,128)} %collective-permute-done.8.refs_2_.refs_6_), channel_id=1, source_target_pairs={{8,0},{16,8},{24,16},{28,24},{20,28},{12,20},{4,12},{0,4},{9,1},{1... | collective-permute-start | bytes 3145736 | tf_op jit(solution)/shard_map/ppermute | solution.py:301
  58.9 24.4 %collective-permute-start.1 = (f32[2,8,512]{2,1,0:T(8,128)S(1)}, f32[2,8,512]{2,1,0:T(8,128)S(1)}, u32[]{:S(2)}, u32[]{:S(2)}) collective-permute-start(f32[2,8,512]{2,1,0:T(8,128)S(1)} %pad_maximum_fusion.4), channel_id=1, source_target_pairs={{0,8},{4,12},{8,0},{12,4},{16,24},{20,28},{24,16},{28,20},{1,9},{5... | collective-permute-start | bytes 98312 | tf_op jit(solution)/shard_map/ppermute | solution.py:794
  91.4 20.1 %collective-permute-start.16 = (f32[128,2048]{1,0:T(8,128)}, f32[128,2048]{1,0:T(8,128)S(1)}, u32[]{:S(2)}, u32[]{:S(2)}) collective-permute-start(f32[128,2048]{1,0:T(8,128)} %collective-permute-done.8.refs_2_.refs_6_), channel_id=1, source_target_pairs={{0,1},{1,0},{2,3},{3,2},{4,5},{5,4},{6,7},{7,6},{8,9},{9,8},{10,11... | collective-permute-start | bytes 3145736 | tf_op jit(solution)/shard_map/ppermute | solution.py:284
  93.1 35.2 %collective-permute-start.13 = (f32[128,2048]{1,0:T(8,128)S(1)}, f32[128,2048]{1,0:T(8,128)S(1)}, u32[]{:S(2)}, u32[]{:S(2)}) collective-permute-start(f32[128,2048]{1,0:T(8,128)S(1)} %collective-permute-done.5.refs_0_.refs_4_), channel_id=1, source_target_pairs={{0,1},{1,0},{2,3},{3,2},{4,5},{5,4},{6,7},{7,6},{8,9},{9,8},{10,11... | collective-permute-start | bytes 3145736 | tf_op jit(solution)/shard_map/ppermute | solution.py:284
  93.2 35.2 %collective-permute-start.14 = (f32[128,2048]{1,0:T(8,128)S(1)}, f32[128,2048]{1,0:T(8,128)S(1)}, u32[]{:S(2)}, u32[]{:S(2)}) collective-permute-start(f32[128,2048]{1,0:T(8,128)S(1)} %collective-permute-done.9.refs_2_.refs_6_), channel_id=1, source_target_pairs={{0,1},{1,0},{2,3},{3,2},{4,5},{5,4},{6,7},{7,6},{8,9},{9,8},{10,11... | collective-permute-start | bytes 3145736 | tf_op jit(solution)/shard_map/ppermute | solution.py:284
  187.3 25.3 %collective-permute-start.20 = (f32[128,2048]{1,0:T(8,128)S(1)}, f32[128,2048]{1,0:T(8,128)S(1)}, u32[]{:S(2)}, u32[]{:S(2)}) collective-permute-start(f32[128,2048]{1,0:T(8,128)S(1)} %add.176), channel_id=1, source_target_pairs={{0,2},{2,0},{1,3},{3,1},{4,6},{6,4},{5,7},{7,5},{8,10},{10,8},{9,1... | collective-permute-start | bytes 3145736 | tf_op jit(solution)/shard_map/ppermute | solution.py:280
  213.5 40.6 %collective-permute-start.21 = (f32[128,2048]{1,0:T(8,128)S(1)}, f32[128,2048]{1,0:T(8,128)S(1)}, u32[]{:S(2)}, u32[]{:S(2)}) collective-permute-start(f32[128,2048]{1,0:T(8,128)S(1)} %multiply_multiply_fusion.13), channel_id=1, source_target_pairs={{0,1},{1,0},{2,3},{3,2},{4,5},{5,4},{6,7},{7,6},{8,9},{9,8},{10,11... | collective-permute-start | bytes 3145736 | tf_op jit(solution)/shard_map/ppermute | solution.py:284
  215.0 37.6 %collective-permute-start.68 = (f32[64,2048]{1,0:T(8,128)S(1)}, f32[64,2048]{1,0:T(8,128)S(1)}, u32[]{:S(2)}, u32[]{:S(2)}) collective-permute-start(f32[64,2048]{1,0:T(8,128)S(1)} %constant_dynamic-slice_fusion.4), channel_id=1, source_target_pairs={{0,16},{4,20},{8,24},{12,28},{16,0},{20,4},{24,8},{28,12},{1,17},{... | collective-permute-start | bytes 1572872 | tf_op jit(solution)/shard_map/ppermute | solution.py:809
  216.6 37.6 %collective-permute-start.72 = (f32[64,2048]{1,0:T(8,128)S(1)}, f32[64,2048]{1,0:T(8,128)S(1)}, u32[]{:S(2)}, u32[]{:S(2)}) collective-permute-start(f32[64,2048]{1,0:T(8,128)S(1)} %constant_dynamic-slice_fusion.4), channel_id=1, source_target_pairs={{0,24},{4,28},{8,0},{12,4},{16,8},{20,12},{24,16},{28,20},{1,25},{... | collective-permute-start | bytes 1572872 | tf_op jit(solution)/shard_map/ppermute | solution.py:809
  230.7 40.8 %collective-permute-start.65 = (f32[64,2048]{1,0:T(8,128)S(1)}, f32[64,2048]{1,0:T(8,128)S(1)}, u32[]{:S(2)}, u32[]{:S(2)}) collective-permute-start(f32[64,2048]{1,0:T(8,128)S(1)} %collective-permute-done.64.refs_0_), channel_id=1, source_target_pairs={{0,2},{2,0},{1,3},{3,1},{4,6},{6,4},{5,7},{7,5},{8,10},{10,8},{9,1... | collective-permute-start | bytes 1572872 | tf_op jit(solution)/shard_map/ppermute | solution.py:814
  232.2 45.3 %collective-permute-start.66 = (f32[64,2048]{1,0:T(8,128)S(1)}, f32[64,2048]{1,0:T(8,128)}, u32[]{:S(2)}, u32[]{:S(2)}) collective-permute-start(f32[64,2048]{1,0:T(8,128)S(1)} %collective-permute-done.64.refs_0_), channel_id=1, source_target_pairs={{0,1},{1,0},{2,3},{3,2},{4,5},{5,4},{6,7},{7,6},{8,9},{9,8},{10,11... | collective-permute-start | bytes 1572872 | tf_op jit(solution)/shard_map/ppermute | solution.py:284
  254.1 23.9 %collective-permute-start.70 = (f32[64,2048]{1,0:T(8,128)S(1)}, f32[64,2048]{1,0:T(8,128)}, u32[]{:S(2)}, u32[]{:S(2)}) collective-permute-start(f32[64,2048]{1,0:T(8,128)S(1)} %collective-permute-done.68.refs_4_), channel_id=1, source_target_pairs={{0,1},{1,0},{2,3},{3,2},{4,5},{5,4},{6,7},{7,6},{8,9},{9,8},{10,11... | collective-permute-start | bytes 1572872 | tf_op jit(solution)/shard_map/ppermute | solution.py:284
  254.1 23.3 %collective-permute-start.73 = (f32[64,2048]{1,0:T(8,128)S(1)}, f32[64,2048]{1,0:T(8,128)}, u32[]{:S(2)}, u32[]{:S(2)}) collective-permute-start(f32[64,2048]{1,0:T(8,128)S(1)} %collective-permute-done.72.refs_8_), channel_id=1, source_target_pairs={{0,2},{2,0},{1,3},{3,1},{4,6},{6,4},{5,7},{7,5},{8,10},{10,8},{9,1... | collective-permute-start | bytes 1572872 | tf_op jit(solution)/shard_map/ppermute | solution.py:814
  286.0 49.1 %collective-permute-start.23 = (f32[128,2048]{1,0:T(8,128)S(1)}, f32[128,2048]{1,0:T(8,128)S(1)}, u32[]{:S(2)}, u32[]{:S(2)}) collective-permute-start(f32[128,2048]{1,0:T(8,128)S(1)} %add.181), channel_id=1, source_target_pairs={{0,2},{2,0},{1,3},{3,1},{4,6},{6,4},{5,7},{7,5},{8,10},{10,8},{9,1... | collective-permute-start | bytes 3145736 | tf_op jit(solution)/shard_map/ppermute | solution.py:280
  287.6 25.3 %collective-permute-start.52 = (f32[64,2048]{1,0:T(8,128)S(1)}, f32[64,2048]{1,0:T(8,128)S(1)}, u32[]{:S(2)}, u32[]{:S(2)}) collective-permute-start(f32[64,2048]{1,0:T(8,128)S(1)} %constant_dynamic-slice_fusion.5), channel_id=1, source_target_pairs={{0,8},{4,12},{8,16},{12,20},{16,24},{20,28},{24,0},{28,4},{1,9},{5... | collective-permute-start | bytes 1572872 | tf_op jit(solution)/shard_map/ppermute | solution.py:809
  297.1 37.4 %collective-permute-start.56 = (f32[64,2048]{1,0:T(8,128)S(1)}, f32[64,2048]{1,0:T(8,128)S(1)}, u32[]{:S(2)}, u32[]{:S(2)}) collective-permute-start(f32[64,2048]{1,0:T(8,128)S(1)} %constant_dynamic-slice_fusion.5), channel_id=1, source_target_pairs={{0,16},{4,20},{8,24},{12,28},{16,0},{20,4},{24,8},{28,12},{1,17},{... | collective-permute-start | bytes 1572872 | tf_op jit(solution)/shard_map/ppermute | solution.py:809
  300.5 34.5 %collective-permute-start.60 = (f32[64,2048]{1,0:T(8,128)S(1)}, f32[64,2048]{1,0:T(8,128)}, u32[]{:S(2)}, u32[]{:S(2)}) collective-permute-start(f32[64,2048]{1,0:T(8,128)S(1)} %constant_dynamic-slice_fusion.5), channel_id=1, source_target_pairs={{0,24},{4,28},{8,0},{12,4},{16,8},{20,12},{24,16},{28,20},{1,25},{... | collective-permute-start | bytes 1572872 | tf_op jit(solution)/shard_map/ppermute | solution.py:809
  312.9 24.9 %collective-permute-start.53 = (f32[64,2048]{1,0:T(8,128)S(1)}, f32[64,2048]{1,0:T(8,128)S(1)}, u32[]{:S(2)}, u32[]{:S(2)}) collective-permute-start(f32[64,2048]{1,0:T(8,128)S(1)} %collective-permute-done.52.refs_0_), channel_id=1, source_target_pairs={{0,2},{2,0},{1,3},{3,1},{4,6},{6,4},{5,7},{7,5},{8,10},{10,8},{9,1... | collective-permute-start | bytes 1572872 | tf_op jit(solution)/shard_map/ppermute | solution.py:814
  313.4 54.6 %collective-permute-start.54 = (f32[64,2048]{1,0:T(8,128)S(1)}, f32[64,2048]{1,0:T(8,128)}, u32[]{:S(2)}, u32[]{:S(2)}) collective-permute-start(f32[64,2048]{1,0:T(8,128)S(1)} %collective-permute-done.52.refs_0_), channel_id=1, source_target_pairs={{0,1},{1,0},{2,3},{3,2},{4,5},{5,4},{6,7},{7,6},{8,9},{9,8},{10,11... | collective-permute-start | bytes 1572872 | tf_op jit(solution)/shard_map/ppermute | solution.py:284
  335.1 33.0 %collective-permute-start.58 = (f32[64,2048]{1,0:T(8,128)S(1)}, f32[64,2048]{1,0:T(8,128)}, u32[]{:S(2)}, u32[]{:S(2)}) collective-permute-start(f32[64,2048]{1,0:T(8,128)S(1)} %collective-permute-done.56.refs_4_), channel_id=1, source_target_pairs={{0,1},{1,0},{2,3},{3,2},{4,5},{5,4},{6,7},{7,6},{8,9},{9,8},{10,11... | collective-permute-start | bytes 1572872 | tf_op jit(solution)/shard_map/ppermute | solution.py:284
  335.1 24.4 %collective-permute-start.61 = (f32[64,2048]{1,0:T(8,128)}, f32[64,2048]{1,0:T(8,128)S(1)}, u32[]{:S(2)}, u32[]{:S(2)}) collective-permute-start(f32[64,2048]{1,0:T(8,128)} %collective-permute-done.60.refs_8_), channel_id=1, source_target_pairs={{0,2},{2,0},{1,3},{3,1},{4,6},{6,4},{5,7},{7,5},{8,10},{10,8},{9,1... | collective-permute-start | bytes 1572872 | tf_op jit(solution)/shard_map/ppermute | solution.py:814
  337.8 30.8 %collective-permute-start.62 = (f32[64,2048]{1,0:T(8,128)}, f32[64,2048]{1,0:T(8,128)}, u32[]{:S(2)}, u32[]{:S(2)}) collective-permute-start(f32[64,2048]{1,0:T(8,128)} %collective-permute-done.60.refs_8_), channel_id=1, source_target_pairs={{0,1},{1,0},{2,3},{3,2},{4,5},{5,4},{6,7},{7,6},{8,9},{9,8},{10,11... | collective-permute-start | bytes 1572872 | tf_op jit(solution)/shard_map/ppermute | solution.py:284
  349.3 27.2 %collective-permute-start.24 = (f32[128,2048]{1,0:T(8,128)S(1)}, f32[128,2048]{1,0:T(8,128)}, u32[]{:S(2)}, u32[]{:S(2)}) collective-permute-start(f32[128,2048]{1,0:T(8,128)S(1)} %convert_add_fusion.1.refs_0_.refs_2_), channel_id=1, source_target_pairs={{0,8},{8,16},{16,24},{24,28},{28,20},{20,12},{12,4},{4,0},{1,9},{9... | collective-permute-start | bytes 3145736 | tf_op jit(solution)/shard_map/ppermute | solution.py:301
  359.5 29.1 %collective-permute-start.28 = (f32[128,2048]{1,0:T(8,128)S(1)}, f32[128,2048]{1,0:T(8,128)}, u32[]{:S(2)}, u32[]{:S(2)}) collective-permute-start(f32[128,2048]{1,0:T(8,128)S(1)} %convert_add_fusion.1.refs_0_.refs_2_), channel_id=1, source_target_pairs={{8,0},{16,8},{24,16},{28,24},{20,28},{12,20},{4,12},{0,4},{9,1},{1... | collective-permute-start | bytes 3145736 | tf_op jit(solution)/shard_map/ppermute | solution.py:301
  369.9 45.4 %collective-permute-start.41 = (f32[128,2048]{1,0:T(8,128)}, f32[128,2048]{1,0:T(8,128)S(1)}, u32[]{:S(2)}, u32[]{:S(2)}) collective-permute-start(f32[128,2048]{1,0:T(8,128)} %get-tuple-element.143), channel_id=1, source_target_pairs={{0,1},{1,0},{2,3},{3,2},{4,5},{5,4},{6,7},{7,6},{8,9},{9,8},{10,11... | collective-permute-start | bytes 3145736 | tf_op jit(solution)/shard_map/ppermute | solution.py:278
  376.4 34.8 %collective-permute-start.25 = (f32[128,2048]{1,0:T(8,128)}, f32[128,2048]{1,0:T(8,128)S(1)}, u32[]{:S(2)}, u32[]{:S(2)}) collective-permute-start(f32[128,2048]{1,0:T(8,128)} %collective-permute-done.24.refs_0_.refs_8_), channel_id=1, source_target_pairs={{0,8},{8,16},{16,24},{24,28},{28,20},{20,12},{12,4},{4,0},{1,9},{9... | collective-permute-start | bytes 3145736 | tf_op jit(solution)/shard_map/ppermute | solution.py:301
  388.6 24.6 %collective-permute-start.29 = (f32[128,2048]{1,0:T(8,128)}, f32[128,2048]{1,0:T(8,128)S(1)}, u32[]{:S(2)}, u32[]{:S(2)}) collective-permute-start(f32[128,2048]{1,0:T(8,128)} %collective-permute-done.28.refs_2_.refs_10_), channel_id=1, source_target_pairs={{8,0},{16,8},{24,16},{28,24},{20,28},{12,20},{4,12},{0,4},{9,1},{1... | collective-permute-start | bytes 3145736 | tf_op jit(solution)/shard_map/ppermute | solution.py:301
  411.2 25.2 %collective-permute-start.26 = (f32[128,2048]{1,0:T(8,128)S(1)}, f32[128,2048]{1,0:T(8,128)S(1)}, u32[]{:S(2)}, u32[]{:S(2)}) collective-permute-start(f32[128,2048]{1,0:T(8,128)S(1)} %collective-permute-done.25.refs_4_.refs_12_), channel_id=1, source_target_pairs={{0,8},{8,16},{16,24},{24,28},{28,20},{20,12},{12,4},{4,0},{1,9},{9... | collective-permute-start | bytes 3145736 | tf_op jit(solution)/shard_map/ppermute | solution.py:301
  413.2 25.2 %collective-permute-start.30 = (f32[128,2048]{1,0:T(8,128)S(1)}, f32[128,2048]{1,0:T(8,128)S(1)}, u32[]{:S(2)}, u32[]{:S(2)}) collective-permute-start(f32[128,2048]{1,0:T(8,128)S(1)} %collective-permute-done.29.refs_6_.refs_14_), channel_id=1, source_target_pairs={{8,0},{16,8},{24,16},{28,24},{20,28},{12,20},{4,12},{0,4},{9,1},{1... | collective-permute-start | bytes 3145736 | tf_op jit(solution)/shard_map/ppermute | solution.py:301
  415.4 24.4 %collective-permute-start.37 = (f32[128,2048]{1,0:T(8,128)}, f32[128,2048]{1,0:T(8,128)S(1)}, u32[]{:S(2)}, u32[]{:S(2)}) collective-permute-start(f32[128,2048]{1,0:T(8,128)} %collective-permute-done.28.refs_2_.refs_10_), channel_id=1, source_target_pairs={{0,1},{1,0},{2,3},{3,2},{4,5},{5,4},{6,7},{7,6},{8,9},{9,8},{10,11... | collective-permute-start | bytes 3145736 | tf_op jit(solution)/shard_map/ppermute | solution.py:284
  415.5 26.4 %collective-permute-start.38 = (f32[128,2048]{1,0:T(8,128)S(1)}, f32[128,2048]{1,0:T(8,128)S(1)}, u32[]{:S(2)}, u32[]{:S(2)}) collective-permute-start(f32[128,2048]{1,0:T(8,128)S(1)} %collective-permute-done.25.refs_4_.refs_12_), channel_id=1, source_target_pairs={{0,1},{1,0},{2,3},{3,2},{4,5},{5,4},{6,7},{7,6},{8,9},{9,8},{10,11... | collective-permute-start | bytes 3145736 | tf_op jit(solution)/shard_map/ppermute | solution.py:284
  420.4 27.9 %collective-permute-start.39 = (f32[128,2048]{1,0:T(8,128)S(1)}, f32[128,2048]{1,0:T(8,128)S(1)}, u32[]{:S(2)}, u32[]{:S(2)}) collective-permute-start(f32[128,2048]{1,0:T(8,128)S(1)} %collective-permute-done.29.refs_6_.refs_14_), channel_id=1, source_target_pairs={{0,1},{1,0},{2,3},{3,2},{4,5},{5,4},{6,7},{7,6},{8,9},{9,8},{10,11... | collective-permute-start | bytes 3145736 | tf_op jit(solution)/shard_map/ppermute | solution.py:284
  436.5 30.1 %collective-permute-start.34 = (f32[128,2048]{1,0:T(8,128)S(1)}, f32[128,2048]{1,0:T(8,128)S(1)}, u32[]{:S(2)}, u32[]{:S(2)}) collective-permute-start(f32[128,2048]{1,0:T(8,128)S(1)} %collective-permute-done.26.refs_0_.refs_4_), channel_id=1, source_target_pairs={{0,1},{1,0},{2,3},{3,2},{4,5},{5,4},{6,7},{7,6},{8,9},{9,8},{10,11... | collective-permute-start | bytes 3145736 | tf_op jit(solution)/shard_map/ppermute | solution.py:284
  438.4 28.5 %collective-permute-start.35 = (f32[128,2048]{1,0:T(8,128)S(1)}, f32[128,2048]{1,0:T(8,128)S(1)}, u32[]{:S(2)}, u32[]{:S(2)}) collective-permute-start(f32[128,2048]{1,0:T(8,128)S(1)} %collective-permute-done.30.refs_2_.refs_6_), channel_id=1, source_target_pairs={{0,1},{1,0},{2,3},{3,2},{4,5},{5,4},{6,7},{7,6},{8,9},{9,8},{10,11... | collective-permute-start | bytes 3145736 | tf_op jit(solution)/shard_map/ppermute | solution.py:284
  449.2 74.0 %collective-permute-start.42 = (f32[128,2048]{1,0:T(8,128)}, f32[128,2048]{1,0:T(8,128)}, u32[]{:S(2)}, u32[]{:S(2)}) collective-permute-start(f32[128,2048]{1,0:T(8,128)} %add.184), channel_id=1, source_target_pairs={{0,2},{2,0},{1,3},{3,1},{4,6},{6,4},{5,7},{7,5},{8,10},{10,8},{9,1... | collective-permute-start | bytes 3145736 | tf_op jit(solution)/shard_map/ppermute | solution.py:280
  466.6 73.4 %collective-permute-start.78 = (f32[1024,256]{1,0:T(8,128)}, f32[1024,256]{1,0:T(8,128)}, u32[]{:S(2)}, u32[]{:S(2)}) collective-permute-start(f32[1024,256]{1,0:T(8,128)} %constant_dynamic-slice_fusion.1), channel_id=1, source_target_pairs={{0,4},{4,0},{8,12},{12,8},{16,20},{20,16},{24,28},{28,24},{1,5},{5... | collective-permute-start | bytes 3145736 | tf_op jit(solution)/shard_map/ppermute | solution.py:884
  466.9 92.5 %collective-permute-start.77 = (f32[256,1024]{1,0:T(8,128)}, f32[256,1024]{1,0:T(8,128)}, u32[]{:S(2)}, u32[]{:S(2)}) collective-permute-start(f32[256,1024]{1,0:T(8,128)} %get-tuple-element.150), channel_id=1, source_target_pairs={{0,4},{4,0},{8,12},{12,8},{16,20},{20,16},{24,28},{28,24},{1,5},{5... | collective-permute-start | bytes 3145736 | tf_op jit(solution)/shard_map/ppermute | solution.py:884
  471.7 90.2 %collective-permute-start.76 = (f32[256,1024]{1,0:T(8,128)S(1)}, f32[256,1024]{1,0:T(8,128)}, u32[]{:S(2)}, u32[]{:S(2)}) collective-permute-start(f32[256,1024]{1,0:T(8,128)S(1)} %copy-done.63), channel_id=1, source_target_pairs={{0,4},{4,0},{8,12},{12,8},{16,20},{20,16},{24,28},{28,24},{1,5},{5... | collective-permute-start | bytes 3145736 | tf_op jit(solution)/shard_map/ppermute | solution.py:884
  533.3 25.0 %collective-permute-start.45 = (f32[128,2048]{1,0:T(8,128)S(1)}, f32[128,2048]{1,0:T(8,128)S(1)}, u32[]{:S(2)}, u32[]{:S(2)}) collective-permute-start(f32[128,2048]{1,0:T(8,128)S(1)} %add.187), channel_id=1, source_target_pairs={{0,2},{2,0},{1,3},{3,1},{4,6},{6,4},{5,7},{7,5},{8,10},{10,8},{9,1... | collective-permute-start | bytes 3145736 | tf_op jit(solution)/shard_map/ppermute | solution.py:280
  539.5 25.4 %collective-permute-start.43 = (f32[128,2048]{1,0:T(8,128)S(1)}, f32[128,2048]{1,0:T(8,128)S(1)}, u32[]{:S(2)}, u32[]{:S(2)}) collective-permute-start(f32[128,2048]{1,0:T(8,128)S(1)} %add_multiply_fusion), channel_id=1, source_target_pairs={{0,1},{1,0},{2,3},{3,2},{4,5},{5,4},{6,7},{7,6},{8,9},{9,8},{10,11... | collective-permute-start | bytes 3145736 | tf_op jit(solution)/shard_map/ppermute | solution.py:284
  (101 other events, 943.7 us)

commit v3 on v2

--- a/solution.py
+++ b/solution.py
@@ -288,22 +288,28 @@
     return list(range(0, count, 2)) + list(range(count - 1, 0, -2))
 
 
-def ring_gather(half, split):
+def ring_gather(pieces):
     count = lax.axis_size(SEQ)
     order = ring_order(count)
     up = [(order[i], order[(i + 1) % count]) for i in range(count)]
     down = [(target, source) for source, target in up]
     steps = []
-    rising = falling = half
+    rising, falling = list(pieces), list(pieces)
     for hop in range(1, count // 2 + 1):
-        if hop == count // 2:
-            rising, falling = rising[:split], falling[split:]
-        rising, falling = lax.ppermute(rising, SEQ, up), lax.ppermute(falling, SEQ, down)
-        others = other_core(rising), other_core(falling)
-        if hop == count // 2:
-            steps.append([rising, falling, *others])
+        last = hop == count // 2
+        if last and len(pieces) == 1:
+            middle = pieces[0].shape[0] // 2
+            rising, falling = [rising[0][:middle], None], [None, falling[0][middle:]]
+        for part in range(len(rising)):
+            rising[part] = None if last and part else lax.ppermute(rising[part], SEQ, up)
+            falling[part] = None if last and not part else lax.ppermute(falling[part], SEQ, down)
+        if last:
+            came = [rising[0], falling[1]]
+            steps.append(came + [other_core(part) for part in came])
         else:
-            steps.append([rising, others[0], falling, others[1]])
+            steps.append(
+                rising + [other_core(part) for part in rising] + falling + [other_core(part) for part in falling]
+            )
     return steps
 
 
@@ -344,14 +350,16 @@
     return centred * inverse, inverse
 
 
-def norm_start_kernel(core_ref, first_ref, tokens_ref, gain_ref, rates_ref, normed_ref, half_ref, info_ref):
+def norm_start_kernel(core_ref, first_ref, tokens_ref, gain_ref, rates_ref, normed_ref, first_half_ref, second_half_ref, info_ref):
     half = tokens_ref.shape[0] // 2
     for index, core in enumerate((core_ref[0], 1 - core_ref[0])):
         rows = tokens_ref[pl.ds(pl.multiple_of(core * half, half), half), :].astype(jnp.float32)
         normed = (norm_parts(rows)[0] * gain_ref[...]).astype(jnp.bfloat16)
         normed_ref[index * half : (index + 1) * half, :] = normed
         if index == 0:
-            half_ref[...] = normed.astype(jnp.float32)
+            part = first_half_ref.shape[0]
+            first_half_ref[...] = normed[:part].astype(jnp.float32)
+            second_half_ref[...] = normed[part:].astype(jnp.float32)
     heads, size = rates_ref.shape
     info_ref[...] = jnp.full(info_ref.shape, first_ref[0], jnp.int32).astype(jnp.float32)
     for head in range(heads):
@@ -364,10 +372,11 @@
     return pl.pallas_call(
         norm_start_kernel,
         in_specs=[smem, smem, vmem, vmem, vmem],
-        out_specs=[vmem, vmem, vmem],
+        out_specs=[vmem] * 4,
         out_shape=[
             jax.ShapeDtypeStruct((rows, width), jnp.bfloat16),
-            jax.ShapeDtypeStruct((rows // 2, width), jnp.float32),
+            jax.ShapeDtypeStruct((rows // 4, width), jnp.float32),
+            jax.ShapeDtypeStruct((rows // 4, width), jnp.float32),
             jax.ShapeDtypeStruct((8, log_decay.size), jnp.float32),
         ],
         compiler_params=pltpu.CompilerParams(vmem_limit_bytes=10 << 20),
@@ -397,37 +406,65 @@
     )(core[None], tokens, mine, other)
 
 
-def rows_product_kernel(parts, tiles, pieces, scales, turned, shard_ref, *refs):
-    weights = len(tiles)
-    part_refs, slab_refs = refs[:parts], refs[parts : 2 * parts]
-    weight_refs = refs[2 * parts : 2 * parts + weights]
-    outs = refs[len(refs) - sum(pieces) - 2 : len(refs) - 1]
-    x = refs[-1]
-    step = pl.program_id(0)
-    size = x.shape[0] // parts
-
-    @pl.when(step == 0)
-    def _():
-        for index in range(parts):
-            at = slice(index * size, (index + 1) * size)
-            x[at, :] = part_refs[index][...].astype(jnp.bfloat16)
-            outs[0][at, :] = slab_refs[index][...].astype(jnp.bfloat16)
-
-    start, at = 0, 1
-    for weight, count, number, scale in zip(weight_refs, tiles, pieces, scales):
-
-        @pl.when((step >= start) & (step < start + count))
-        def _(weight=weight, results=outs[at : at + number], scale=scale):
-            found = (dot_nt if turned else dot_nn)(x[...], weight[...])
+def rows_product_kernel(parts, size, pieces, scales, tile, turned, block, shard_ref, *refs):
+    weights = len(pieces)
+    results = 1 + sum(pieces)
+    part_refs, weight_refs = refs[:parts], refs[parts : parts + weights]
+    scratch = refs[len(refs) - 2 * results - parts - weights - 3 :]
+    outs, staged, scratch = scratch[:results], scratch[results : 2 * results], scratch[2 * results :]
+    held, kept, x, read, written = scratch[:parts], scratch[parts : parts + weights], *scratch[parts + weights :]
+    rows = x.shape[0]
+    slab = staged[0].shape[1]
+    loads = []
+
+    def load(source, target):
+        copy = pltpu.make_async_copy(source, target, read.at[len(loads)])
+        copy.start()
+        loads.append(copy)
+        return copy
+
+    arrive = [load(part.at[pl.ds(0, size), :], target) for part, target in zip(part_refs, held)]
+    ready = []
+    for weight, target in zip(weight_refs, kept):
+        for start in range(0, weight.shape[0 if turned else 1], tile):
+            at = pl.ds(start, tile)
+            if turned:
+                ready.append(load(weight.at[at, :], target.at[at, :]))
+            else:
+                ready.append(load(weight.at[:, at], target.at[:, at]))
+    for index, copy in enumerate(arrive):
+        copy.wait()
+        at = slice(index * size, (index + 1) * size)
+        x[at, :] = held[index][...].astype(jnp.bfloat16)
+        column = pl.ds(pl.multiple_of(shard_ref[0] * slab, slab), slab)
+        staged[0][at, :] = held[index][:, column].astype(jnp.bfloat16)
+    stores = []
+
+    def store(index, column):
+        target = outs[index].at[pl.ds(block * rows, rows), column]
+        copy = pltpu.make_async_copy(staged[index].at[:, column], target, written.at[len(stores)])
+        copy.start()
+        stores.append(copy)
+
+    store(0, pl.ds(0, slab))
+    result, number = 1, 0
+    for weight, count, scale in zip(kept, pieces, scales):
+        for start in range(0, weight.shape[0 if turned else 1], tile):
+            at = slice(start, start + tile)
+            ready[number].wait()
+            number += 1
+            found = dot_nt(x[...], weight[at, :]) if turned else dot_nn(x[...], weight[:, at])
             if scale != 1.0:
                 found = found * scale
             high = found.astype(jnp.bfloat16)
-            results[0][...] = high
-            if len(results) == 2:
-                results[1][...] = (found - high.astype(jnp.float32)).astype(jnp.bfloat16)
-
-        start += count
-        at += number
+            staged[result][:, at] = high
+            store(result, pl.ds(start, tile))
+            if count == 2:
+                staged[result + 1][:, at] = (found - high.astype(jnp.float32)).astype(jnp.bfloat16)
+                store(result + 1, pl.ds(start, tile))
+        result += count
+    for copy in stores:
+        copy.wait()
 
 
 def rows_product(parts, size, weights, pieces, scales, turned, shard, block, total, buffers=None):
@@ -435,105 +472,83 @@
     rows = count * size
     tile = 512
     columns = [w.shape[0] if turned else w.shape[1] for w in weights]
-    tiles = [c // tile for c in columns]
-    starts = [sum(tiles[:i]) for i in range(len(tiles))]
     slab = width // lax.axis_size(SEQ)
-
-    def at(j, start, number):
-        return jnp.clip(j - start, 0, number - 1)
-
-    in_specs = [pl.BlockSpec((size, width), lambda j, s: (0, 0)) for _ in parts]
-    in_specs += [pl.BlockSpec((size, slab), lambda j, s: (0, s[0])) for _ in parts]
-    for start, number in zip(starts, tiles):
-        if turned:
-            in_specs.append(pl.BlockSpec((tile, width), lambda j, s, a=start, n=number: (at(j, a, n), 0)))
-        else:
-            in_specs.append(pl.BlockSpec((width, tile), lambda j, s, a=start, n=number: (0, at(j, a, n))))
-    out_specs = [pl.BlockSpec((rows, slab), lambda j, s: (block, 0))]
-    out_shape = [jax.ShapeDtypeStruct((total, slab), jnp.bfloat16)]
-    for start, number, results, c in zip(starts, tiles, pieces, columns):
-        out_specs += [pl.BlockSpec((rows, tile), lambda j, s, a=start, n=number: (block, at(j, a, n)))] * results
-        out_shape += [jax.ShapeDtypeStruct((total, c), jnp.bfloat16)] * results
-    operands = [*parts, *parts, *weights]
+    widths = [slab] + [c for c, results in zip(columns, pieces) for _ in range(results)]
+    operands = [*parts, *weights]
     aliases = {}
     if buffers is not None:
         aliases = {1 + len(operands) + i: i for i in range(len(buffers))}
-        in_specs += [pl.BlockSpec(memory_space=pl.ANY)] * len(buffers)
         operands += buffers
+    anywhere = pl.BlockSpec(memory_space=pl.ANY)
+    tiles = [c // tile for c in columns]
     return pl.pallas_call(
-        functools.partial(rows_product_kernel, count, tiles, pieces, scales, turned),
+        functools.partial(rows_product_kernel, count, size, pieces, scales, tile, turned, block),
         grid_spec=pltpu.PrefetchScalarGridSpec(
             num_scalar_prefetch=1,
-            grid=(sum(tiles),),
-            in_specs=in_specs,
-            out_specs=out_specs,
-            scratch_shapes=[pltpu.VMEM((rows, width), jnp.bfloat16)],
+            grid=(1,),
+            in_specs=[anywhere] * len(operands),
+            out_specs=[anywhere] * len(widths),
+            scratch_shapes=[pltpu.VMEM((rows, c), jnp.bfloat16) for c in widths]
+            + [pltpu.VMEM((size, width), part.dtype) for part in parts]
+            + [pltpu.VMEM(w.shape, w.dtype) for w in weights]
+            + [
+                pltpu.VMEM((rows, width), jnp.bfloat16),
+                pltpu.SemaphoreType.DMA((count + sum(tiles),)),
+                pltpu.SemaphoreType.DMA((1 + sum(a * b for a, b in zip(tiles, pieces)),)),
+            ],
         ),
-        out_shape=out_shape,
+        out_shape=[jax.ShapeDtypeStruct((total, c), jnp.bfloat16) for c in widths],
         input_output_aliases=aliases,
         cost_estimate=pl.CostEstimate(
             flops=2 * rows * width * sum(columns),
             bytes_accessed=4 * rows * width + 2 * width * sum(columns) + 2 * rows * sum(columns),
             transcendentals=0,
         ),
-        compiler_params=pltpu.CompilerParams(vmem_limit_bytes=(40 if turned else 52) << 20),
+        compiler_params=pltpu.CompilerParams(vmem_limit_bytes=(48 if turned else 52) << 20),
         name="rows_product",
     )(shard[None], *operands)
 
 
-def rows_sum_kernel(counts, turned, *refs):
-    number = len(counts)
+def rows_sum_kernel(number, tile, turned, *refs):
     rows_refs, weight_refs = refs[:number], refs[number : 2 * number]
-    mine, other, total = refs[2 * number :]
-    step = pl.program_id(0)
-    start = 0
-    for rows, weight, count in zip(rows_refs, weight_refs, counts):
-
-        @pl.when((step >= start) & (step < start + count))
-        def _(rows=rows, weight=weight, start=start):
-            found = dot_nt(weight[...], rows[...]) if turned else dot_nn(rows[...], weight[...])
-            if start:
-                total[...] += found
-            else:
-                total[...] = jnp.where(step == 0, found, total[...] + found)
-
-        start += count
-
-    @pl.when(step == start - 1)
-    def _():
-        half = mine.shape[0]
-        mine[...] = total[:, :half].T if turned else total[:half, :]
-        other[...] = total[:, half:].T if turned else total[half:, :]
+    mine, other, total = refs[2 * number : 2 * number + 3]
+    held, done = refs[2 * number + 3 : -1], refs[-1]
+    pieces = []
+    for rows, weight, kept in zip(rows_refs, weight_refs, held):
+        for start in range(0, rows.shape[1], tile):
+            at = pl.ds(start, tile)
+            source, target = (weight.at[:, at], kept.at[:, at]) if turned else (weight.at[at, :], kept.at[at, :])
+            copy = pltpu.make_async_copy(source, target, done.at[len(pieces)])
+            copy.start()
+            pieces.append((copy, rows, kept, slice(start, start + tile)))
+    for index, (copy, rows, kept, at) in enumerate(pieces):
+        copy.wait()
+        if turned:
+            found = dot_nt(rows[:, at], kept[:, at])
+        else:
+            found = dot_nn(rows[:, at], kept[at, :])
+        total[...] = total[...] + found if index else found
+    half = mine.shape[0]
+    mine[...] = total[:half, :]
+    other[...] = total[half:, :]
 
 
 def rows_sum(arrays, weights, block, rows, turned):
     tile = 512
     width = weights[0].shape[0] if turned else weights[0].shape[1]
-    counts = [a.shape[1] // tile for a in arrays]
-    starts = [sum(counts[:i]) for i in range(len(counts))]
-
-    def at(j, start, number):
-        return jnp.clip(j - start, 0, number - 1)
-
-    in_specs = [
-        pl.BlockSpec((rows, tile), lambda j, a=start, n=number: (block, at(j, a, n)))
-        for start, number in zip(starts, counts)
-    ]
-    for start, number in zip(starts, counts):
-        if turned:
-            in_specs.append(pl.BlockSpec((width, tile), lambda j, a=start, n=number: (0, at(j, a, n))))
-        else:
-            in_specs.append(pl.BlockSpec((tile, width), lambda j, a=start, n=number: (at(j, a, n), 0)))
     half = pl.BlockSpec((rows // 2, width), lambda j: (0, 0))
     depth = sum(a.shape[1] for a in arrays)
     return pl.pallas_call(
-        functools.partial(rows_sum_kernel, counts, turned),
+        functools.partial(rows_sum_kernel, len(arrays), tile, turned),
         grid_spec=pltpu.PrefetchScalarGridSpec(
             num_scalar_prefetch=0,
-            grid=(sum(counts),),
-            in_specs=in_specs,
+            grid=(1,),
+            in_specs=[pl.BlockSpec((rows, a.shape[1]), lambda j: (block, 0)) for a in arrays]
+            + [pl.BlockSpec(memory_space=pl.ANY)] * len(weights),
             out_specs=[half, half],
-            scratch_shapes=[pltpu.VMEM((width, rows) if turned else (rows, width), jnp.float32)],
+            scratch_shapes=[pltpu.VMEM((rows, width), jnp.float32)]
+            + [pltpu.VMEM(w.shape, w.dtype) for w in weights]
+            + [pltpu.SemaphoreType.DMA((depth // tile,))],
         ),
         out_shape=[jax.ShapeDtypeStruct((rows // 2, width), jnp.float32)] * 2,
         cost_estimate=pl.CostEstimate(
@@ -563,7 +578,6 @@
         out_specs=vmem,
         out_shape=jax.ShapeDtypeStruct((rows, width), jnp.bfloat16),
         cost_estimate=pl.CostEstimate(flops=rows * width, bytes_accessed=6 * rows * width, transcendentals=0),
-        compiler_params=pltpu.CompilerParams(vmem_limit_bytes=14 << 20),
         name="round_rows",
     )(*parts)
 
@@ -784,11 +798,11 @@
             parts = [part for step in group for part in steps[step]]
             last = index + 1 == len(groups)
             block = shards - 1 if last else group[0] // len(group)
-            found = rows_product(parts, quarter if last else half, *common, block, total, found)
+            found = rows_product(parts, parts[0].shape[0], *common, block, total, found)
         return found
 
-    normed_own, normed_half, info = norm_start(core, first_start, tokens, first_gain, log_decay)
-    came = ring_gather(normed_half, quarter)
+    normed_own, *normed_half, info = norm_start(core, first_start, tokens, first_gain, log_decay)
+    came = ring_gather(normed_half)
     info = info[None]
     for index in range(shards.bit_length() - 1):
         moved = lax.ppermute(info, SEQ, [(i, i ^ (1 << index)) for i in range(shards)])
@@ -815,7 +829,7 @@
             parts += both + [other_core(part) for part in both]
         return parts
 
-    cotangent_far = far_start(after(0.5 * cotangent_half, came[-1][0]))
+    cotangent_far = far_start(after(0.5 * cotangent_half, came[-1][1]))
     cotangent_far = far_parts(cotangent_far)
     cotangent_far = round_rows(cotangent_far)
 
@@ -853,7 +867,7 @@
     grad_mid = head_total(mid_mine, mid_other)
     grad_residual = cotangent_half + norm_grad(grad_mid, second_gain, mid_unit, mid_inverse)
     second_part = 0.5 * jnp.sum(grad_mid * mid_unit, axis=0)
-    branch_came = ring_gather(grad_residual, quarter)
+    branch_came = ring_gather([grad_residual])
     steps = list(range(shards // 2))
     branch_slab, grad_gated = over_steps(
         [grad_residual, other_core(grad_residual)],
@@ -871,7 +885,7 @@
     hidden_far, grad_up_gate_far, grad_up_far = feed_forward(normed_mid_far, grad_hidden_far)
 
     res_mine, res_other = rows_sum([hidden], [down_weight], 0, rows, False)
-    hidden_total = head_total(res_mine, res_other)
+    hidden_total = head_total(res_mine, after(res_other, branch_came[0][0]))
 
     def pair_slab(a):
         return lax.dynamic_slice_in_dim(a, shard // 2 * (2 * slab), 2 * slab, 1)
@@ -881,7 +895,7 @@
         found = found + transpose_left(left_far, right_far)
         kept = lax.dynamic_slice_in_dim(found, shard % 2 * slab, slab, dim)
         sent = lax.dynamic_slice_in_dim(found, (1 - shard % 2) * slab, slab, dim)
-        sent = lax.ppermute(after(sent, branch_came[-1][0]), SEQ, [(i, i ^ 1) for i in range(shards)])
+        sent = lax.ppermute(after(sent, branch_came[-1][1]), SEQ, [(i, i ^ 1) for i in range(shards)])
         return kept + sent
 
     mid_slab, mid_slab_far = pair_slab(normed_mid_own), pair_slab(normed_mid_far)
@@ -912,9 +926,10 @@
     gains = exchange_sum(jnp.concatenate([first_part, second_part[None]]), SEQ)
     gains = gains + other_core(gains)
     grad_half = 0.5 * (grad_residual + norm_grad(grad_in, first_gain, first_unit, first_inverse))
-    grad_tokens = narrow(in_order(grad_half, other_core(grad_half)))
-    gains = after(gains, grad_in)
-    gains = slab_of(gains + lax.ppermute(gains, HEAD, ACROSS), shard)
+    other_half = other_core(grad_half)
+    grad_tokens = narrow(in_order(grad_half, other_half))
+    gains = gains + lax.ppermute(after(gains, grad_in), HEAD, ACROSS)
+    gains = slab_of(gains, shard)
     return (
         output_rows,
         grad_tokens,

time: 577 us -> 552 us (0.957)
  Pallas kernels: 165 us -> 153 us
  waiting for transfers between devices: 221 us -> 209 us
  local copies, waits for them, and re-layouts: 23 us -> 17 us
    pallas_call x13, Pallas kernels: 114 us -> 96.1 us  [the longest x9 70.7 us: rows_product(): pl.pallas_call(functools.partial(rows_product_kernel, count, size, pieces...]
    ppermute x3, waiting for transfers between devices: 35.5 us -> 25.5 us  [local_gather(): lax.ppermute(info, SEQ, [(i, i ^ 1 << index) for i in range(shards)])]
    ppermute x6, waiting for transfers between devices: 19.2 us -> 28.6 us  [far_parts(): both = [item, lax.ppermute(item, HEAD, ACROSS)]]
    ppermute x20 -> x26, waiting for transfers between devices: 60.8 us -> 51.6 us  [the longest x11 39.5 us: ring_gather(): lax.ppermute(rising[part], SEQ, up)]
    unnamed x140 -> x146, local copies, waits for them, and re-layouts: 19.6 us -> 12 us
    ppermute x20 -> x26, starting transfers between devices: 28.9 us -> 36 us  [the longest x11 22.7 us: ring_gather(): lax.ppermute(rising[part], SEQ, up)]
    dot_general x4, matrix products: 27.3 us -> 21.4 us  [matmul(): return jnp.dot(left_side, right_side, preferred_element_type=jnp.float32)]
  transfers between devices with their start and end apart: 79 -> 91, of which waited for: 28 -> 27; matrix products, arithmetic and copies ran while one was open for 14% -> 14% of each run, Pallas kernels for 22% -> 22%
where the time goes in v3:
time: 552 us; the launch traced here: 543 us
  waiting for transfers between devices  209 us (38%)
  Pallas kernels  153 us (28%)
  starting transfers between devices  82.6 us (15%)
  matrix products  55.3 us (10%)
  other arithmetic  23.8 us (4%)
  local copies, waits for them, and re-layouts  17 us (3%)
    pallas_call x9, Pallas kernels, rows_product(): pl.pallas_call(functools.partial(rows_product_kernel, count, size, pieces...  70.7 us
    ppermute x6, waiting for transfers between devices, far_start(): return [lax.ppermute(share, SEQ, hop) for hop in far_hops()]  55.9 us
    ppermute x11, waiting for transfers between devices, ring_gather(): lax.ppermute(rising[part], SEQ, up)  39.5 us
    ppermute x4, waiting for transfers between devices, head_total(): return both + lax.ppermute(both, HEAD, ACROSS)  38.2 us
    ppermute x6, waiting for transfers between devices, far_parts(): both = [item, lax.ppermute(item, HEAD, ACROSS)]  28.6 us
    ppermute x3, waiting for transfers between devices, local_gather(): lax.ppermute(info, SEQ, [(i, i ^ 1 << index) for i in range(shards)])  25.5 us
    pallas_call x4, Pallas kernels, rows_sum(): pl.pallas_call(functools.partial(rows_sum_kernel, len(arrays), tile, turn...  25.5 us
    dot_general x11, matrix products, transpose_left(): lax.dot_general(left_side, right_side, (((0,), (0,)), ((), ())), preferre...  25.3 us
  transfers between devices with their start and end apart: 91, of which 27 were waited for; matrix products, arithmetic and copies ran while one was open for 14% of the time, Pallas kernels for 22%

profile of v3, /device:TPU:0, one launch (start us, length us, event | category | flops | bytes accessed | tf_op | source)
XLA Modules:
  0.0 543.3 jit_solution(12707940901198958424)
XLA Ops:
  6.2 3.1 collective-permute-start.3
  14.5 18.5 %collective-permute-done = f32[1,8,512]{2,1,0:T(8,128)S(1)} collective-permute-done((f32[1,8,512]{2,1,0:T(8,128)S(1)}, f32[1,8,512]{2,1,0:T(8,128)S(1)}, u32[]{:S(2)}, u32[]{:S(2)}) %collective-permute-start) | collective-permute-done | bytes 16416 | tf_op jit(solution)/shard_map/ppermute | solution.py:808
  34.4 3.1 collective-permute-done.1
  39.4 4.0 collective-permute-done.2
  46.5 7.0 %rows_product.9 = (bf16[2048,256]{1,0:T(8,128)(2,1)S(1)}, bf16[2048,512]{1,0:T(8,128)(2,1)}, bf16[2048,512]{1,0:T(8,128)(2,1)}, bf16[2048,512]{1,0:T(8,128)(2,1)...) custom-call(s32[1]{0:T(128)} %bitcast.5.shard_ref, ...), custom_call_target="tpu_custom_call" | custom-call | flops 3221225472 | bytes 16252928 | tf_op jit(solution)/shard_map/rows_product/pallas_call | solution.py:484
  58.5 10.9 %collective-permute-done.14.refs_1_ = f32[64,2048]{1,0:T(8,128)S(1)} collective-permute-done((f32[64,2048]{1,0:T(8,128)S(1)}, f32[64,2048]{1,0:T(8,128)S(1)}, u32[]{:S(2)}, u32[]{:S(2)}) %collective-permute-start.14) | collective-permute-done | bytes 524320 | tf_op jit(solution)/shard_map/ppermute | solution.py:304
  74.1 4.8 collective-permute-done.5.refs_0_
  78.9 11.2 %rows_product.10 = (bf16[2048,256]{1,0:T(8,128)(2,1)}, bf16[2048,512]{1,0:T(8,128)(2,1)}, bf16[2048,512]{1,0:T(8,128)(2,1)}, bf16[2048,512]{1,0:T(8,128)(2,1)}, ...) custom-call(s32[1]{0:T(128)} %bitcast.5.shard_ref, ...), custom_call_target="tpu_custom_call", output_to_operand_aliasing={{0}: (13, {}), {1}: (14, {}), {2}: (15, {}), {3}: (16, {}),... | custom-call | flops 6442450944 | bytes 19922944 | tf_op jit(solution)/shard_map/rows_product/pallas_call | solution.py:484
  92.8 4.6 collective-permute-done.20.refs_4_
  97.9 11.1 %rows_product.11 = (bf16[2048,256]{1,0:T(8,128)(2,1)}, bf16[2048,512]{1,0:T(8,128)(2,1)}, bf16[2048,512]{1,0:T(8,128)(2,1)}, bf16[2048,512]{1,0:T(8,128)(2,1)}, ...) custom-call(s32[1]{0:T(128)} %bitcast.5.shard_ref, ...), custom_call_target="tpu_custom_call", output_to_operand_aliasing={{0}: (13, {}), {1}: (14, {}), {2}: (15, {}), {3}: (16, {}),... | custom-call | flops 6442450944 | bytes 19922944 | tf_op jit(solution)/shard_map/rows_product/pallas_call | solution.py:484
  110.8 11.1 %rows_product.12 = (bf16[2048,256]{1,0:T(8,128)(2,1)}, bf16[2048,512]{1,0:T(8,128)(2,1)}, bf16[2048,512]{1,0:T(8,128)(2,1)}, bf16[2048,512]{1,0:T(8,128)(2,1)}, ...) custom-call(s32[1]{0:T(128)} %bitcast.5.shard_ref, ...), custom_call_target="tpu_custom_call", output_to_operand_aliasing={{0}: (13, {}), {1}: (14, {}), {2}: (15, {}), {3}: (16, {}),... | custom-call | flops 6442450944 | bytes 19922944 | tf_op jit(solution)/shard_map/rows_product/pallas_call | solution.py:484
  122.7 7.3 %rows_product.13 = (bf16[2048,256]{1,0:T(8,128)(2,1)}, bf16[2048,512]{1,0:T(8,128)(2,1)}, bf16[2048,512]{1,0:T(8,128)(2,1)}, bf16[2048,512]{1,0:T(8,128)(2,1)}, ...) custom-call(s32[1]{0:T(128)} %bitcast.5.shard_ref, ...), custom_call_target="tpu_custom_call", output_to_operand_aliasing={{0}: (9, {}), {1}: (10, {}), {2}: (11, {}), {3}: (12, {}), ... | custom-call | flops 3221225472 | bytes 16252928 | tf_op jit(solution)/shard_map/rows_product/pallas_call | solution.py:484
  130.0 20.5 %retain_forward.1 = (f32[2048,1024]{1,0:T(8,128)}, bf16[2048,1024]{1,0:T(8,128)(2,1)}, bf16[2,8,256,512]{3,2,1,0:T(8,128)(2,1)}, f32[2,8,256,256]{3,2,1,0:T(8,12...) custom-call(s32[8]{0:T(128)} %compare_select_fusion.4.slot_ref, ...), custom_call_target="tpu_custom_call" | custom-call | flops 4831838208 | bytes 33554432 | tf_op jit(solution)/shard_map/retain_forward/pallas_call | solution.py:693
  150.5 5.3 rows_sum.4
  162.0 23.4 %collective-permute-done.32 = f32[128,2048]{1,0:T(8,128)} collective-permute-done((f32[128,2048]{1,0:T(8,128)S(1)}, f32[128,2048]{1,0:T(8,128)}, u32[]{:S(2)}, u32[]{:S(2)}) %collective-permute-start.32) | collective-permute-done | bytes 1048608 | tf_op jit(solution)/shard_map/ppermute | solution.py:280
  195.3 9.5 %collective-permute-done.76.refs_0_ = f32[64,2048]{1,0:T(8,128)} collective-permute-done((f32[64,2048]{1,0:T(8,128)S(1)}, f32[64,2048]{1,0:T(8,128)}, u32[]{:S(2)}, u32[]{:S(2)}) %collective-permute-start.76) | collective-permute-done | bytes 524320 | tf_op jit(solution)/shard_map/ppermute | solution.py:823
  206.5 20.2 %collective-permute-done.80.refs_4_ = f32[64,2048]{1,0:T(8,128)} collective-permute-done((f32[64,2048]{1,0:T(8,128)S(1)}, f32[64,2048]{1,0:T(8,128)}, u32[]{:S(2)}, u32[]{:S(2)}) %collective-permute-start.80) | collective-permute-done | bytes 524320 | tf_op jit(solution)/shard_map/ppermute | solution.py:823
  231.6 4.5 multiply_convert_fusion.4
  237.7 6.7 %rows_sum.5 = (f32[128,2048]{1,0:T(8,128)}, f32[128,2048]{1,0:T(8,128)}) custom-call(bf16[256,1024]{1,0:T(8,128)(2,1)} %get-tuple-element.170.refs_0_, bf16[256,1024]{1,0:T(8,128)(2,1)} %get-tuple-element.169.refs_1_, bf16[2048,1024]{1,0:T(8,128)(2,1)} %refs_2_.4, bf16[2048,1024]{1,0:T(8,128)(2,1)} %refs_3_.3), custom_call_target="tpu_custom_call" | custom-call | flops 2147483648 | bytes 11534336 | tf_op jit(solution)/shard_map/rows_sum/pallas_call | solution.py:541
  245.0 7.1 %collective-permute-done.85.refs_9_ = f32[64,2048]{1,0:T(8,128)} collective-permute-done((f32[64,2048]{1,0:T(8,128)}, f32[64,2048]{1,0:T(8,128)}, u32[]{:S(2)}, u32[]{:S(2)}) %collective-permute-start.85) | collective-permute-done | bytes 524320 | tf_op jit(solution)/shard_map/ppermute | solution.py:828
  255.9 4.8 round_rows.3
  264.3 9.8 %collective-permute-start.64 = (f32[64,2048]{1,0:T(8,128)S(1)}, f32[64,2048]{1,0:T(8,128)}, u32[]{:S(2)}, u32[]{:S(2)}) collective-permute-start(f32[64,2048]{1,0:T(8,128)S(1)} %constant_dynamic-slice_fusion.5), channel_id=1, source_target_pairs={{0,8},{4,12},{8,16},{12,20},{16,24},{20,28},{24,0},{28,4},{1,9},{5... | collective-permute-start | bytes 1572872 | tf_op jit(solution)/shard_map/ppermute | solution.py:823
  274.2 3.5 collective-permute-start.68
  277.7 7.3 %fusion.66 = f32[768,1024]{1,0:T(8,128)} fusion(bf16[768,2048]{1,0:T(8,128)(2,1)S(1)} %copy-done.26, bf16[1024,2048]{1,0:T(8,128)(2,1)} %refs_1_.5), kind=kOutput, calls=%fused_computation.158 | convolution fusion | flops 3221225472 | bytes 10485760 | tf_op jit(solution)/shard_map/dot_general | solution.py:50
  285.0 5.1 collective-permute-done.64.refs_0_
  290.7 21.1 %collective-permute-done.68.refs_4_ = f32[64,2048]{1,0:T(8,128)} collective-permute-done((f32[64,2048]{1,0:T(8,128)S(1)}, f32[64,2048]{1,0:T(8,128)}, u32[]{:S(2)}, u32[]{:S(2)}) %collective-permute-start.68) | collective-permute-done | bytes 524320 | tf_op jit(solution)/shard_map/ppermute | solution.py:823
  315.2 11.5 %collective-permute-done.69.refs_5_ = f32[64,2048]{1,0:T(8,128)S(1)} collective-permute-done((f32[64,2048]{1,0:T(8,128)}, f32[64,2048]{1,0:T(8,128)S(1)}, u32[]{:S(2)}, u32[]{:S(2)}) %collective-permute-start.69) | collective-permute-done | bytes 524320 | tf_op jit(solution)/shard_map/ppermute | solution.py:828
  327.0 9.9 %collective-permute-done.73.refs_9_ = f32[64,2048]{1,0:T(8,128)S(1)} collective-permute-done((f32[64,2048]{1,0:T(8,128)}, f32[64,2048]{1,0:T(8,128)S(1)}, u32[]{:S(2)}, u32[]{:S(2)}) %collective-permute-start.73) | collective-permute-done | bytes 524320 | tf_op jit(solution)/shard_map/ppermute | solution.py:828
  336.9 7.1 %collective-permute-start.36 = (f32[128,2048]{1,0:T(8,128)S(1)}, f32[128,2048]{1,0:T(8,128)}, u32[]{:S(2)}, u32[]{:S(2)}) collective-permute-start(f32[128,2048]{1,0:T(8,128)S(1)} %convert_add_fusion.1.refs_0_), channel_id=1, source_target_pairs={{0,8},{8,16},{16,24},{24,28},{28,20},{20,12},{12,4},{4,0},{1,9},{9... | collective-permute-start | bytes 3145736 | tf_op jit(solution)/shard_map/ppermute | solution.py:304
  344.1 5.3 rows_sum.7
  349.4 3.0 fusion.34
  358.3 4.8 round_rows.2
  367.7 12.2 %fusion = (f32[768,1024]{1,0:T(8,128)S(1)}, f32[768,1024]{1,0:T(8,128)S(1)}) fusion(bf16[768,2048]{1,0:T(8,128)(2,1)} %round_rows.2, bf16[2048,1024]{1,0:T(8,128)(2,1)} %refs_2_.4), kind=kOutput, calls=%fused_computation.1 | convolution fusion | flops 3269984256 | bytes 13631488 | tf_op jit(solution)/shard_map/dot_general | solution.py:40
  380.5 3.5 fusion.67
  384.1 4.7 collective-permute-done.41.refs_6_
  393.8 3.3 convolution_add_fusion
  397.2 16.5 %collective-permute-done.38.refs_0_ = f32[128,2048]{1,0:T(8,128)S(1)} collective-permute-done((f32[128,2048]{1,0:T(8,128)S(1)}, f32[128,2048]{1,0:T(8,128)S(1)}, u32[]{:S(2)}, u32[]{:S(2)}) %collective-permute-start.38) | collective-permute-done | bytes 1048608 | tf_op jit(solution)/shard_map/ppermute | solution.py:304
  422.3 4.5 rows_product.14
  428.4 3.6 collective-permute-done.39.refs_0_
  432.6 9.1 %rows_product.15 = (bf16[2048,256]{1,0:T(8,128)(2,1)S(1)}, bf16[2048,1024]{1,0:T(8,128)(2,1)}) custom-call(s32[1]{0:T(128)} %bitcast.5.shard_ref, f32[128,2048]{1,0:T(8,128)} %collective-permute-done.36.refs_0_, f32[128,2048]{1,0:T(8,128)S(1)} %collective-permute-done.48.refs_1_, ...), custom_call_target="tpu_custom_call", output_to_operand_aliasing={{0}: (10, {}), {1}: (11, {})} | custom-call | flops 4294967296 | bytes 14680064 | tf_op jit(solution)/shard_map/rows_product/pallas_call | solution.py:484
  443.8 5.3 rows_product.16
  450.8 4.0 rows_product.17
  454.8 24.8 %retain_backward.1 = (bf16[2048,512]{1,0:T(8,128)(2,1)}, bf16[2048,512]{1,0:T(8,128)(2,1)}, bf16[2048,1024]{1,0:T(8,128)(2,1)}, bf16[2048,1024]{1,0:T(8,128)(2,1)}) custom-call(s32[8]{0:T(128)} %compare_select_fusion.4.slot_ref, bf16[2048,512]{1,0:T(8,128)(2,1)} %get-tuple-element.116.q_ref, bf16[2048,512]{1,0:T(8,128)(2,1)} %get-tuple-element.118.k_ref, ...), custom_call_target="tpu_custom_call" | custom-call | flops 10200547328 | bytes 54525952 | tf_op jit(solution)/shard_map/retain_backward/pallas_call | solution.py:723
  479.6 8.2 %rows_sum.6 = (f32[128,2048]{1,0:T(8,128)}, f32[128,2048]{1,0:T(8,128)}) custom-call(bf16[2048,512]{1,0:T(8,128)(2,1)} %get-tuple-element.139.refs_0_, bf16[2048,512]{1,0:T(8,128)(2,1)} %get-tuple-element.140.refs_1_, bf16[2048,1024]{1,0:T(8,128)(2,1)} %get-tuple-element.141.refs_2_, bf16[2048,1024]{1,0:T(8,128)(2,1)} %get-tuple-element.142.refs_3_, ...), custom_call_target="tpu_custom_call" | custom-call | flops 3221225472 | bytes 16252928 | tf_op jit(solution)/shard_map/rows_sum/pallas_call | solution.py:541
  491.1 4.6 fusion.65
  495.7 3.0 collective-permute-start.59
  509.4 2.9 collective-permute-done.61
  516.9 14.8 %collective-permute-done.57 = f32[128,2048]{1,0:T(8,128)S(1)} collective-permute-done((f32[128,2048]{1,0:T(8,128)S(1)}, f32[128,2048]{1,0:T(8,128)S(1)}, u32[]{:S(2)}, u32[]{:S(2)}) %collective-permute-start.57) | collective-permute-done | bytes 1048608 | tf_op jit(solution)/shard_map/ppermute | solution.py:280
  (369 shorter events, 128.5 us)
Async XLA Ops:
  6.2 26.7 %collective-permute-start.3 = (f32[64,2048]{1,0:T(8,128)}, f32[64,2048]{1,0:T(8,128)S(1)}, u32[]{:S(2)}, u32[]{:S(2)}) collective-permute-start(f32[64,2048]{1,0:T(8,128)} %get-tuple-element.85), channel_id=1, source_target_pairs={{0,8},{8,16},{16,24},{24,28},{28,20},{20,12},{12,4},{4,0},{1,9},{9... | collective-permute-start | bytes 1572872 | tf_op jit(solution)/shard_map/ppermute | solution.py:304
  9.3 23.8 %collective-permute-start.13 = (f32[64,2048]{1,0:T(8,128)S(1)}, f32[64,2048]{1,0:T(8,128)S(1)}, u32[]{:S(2)}, u32[]{:S(2)}) collective-permute-start(f32[64,2048]{1,0:T(8,128)S(1)} %get-tuple-element.86), channel_id=1, source_target_pairs={{0,8},{8,16},{16,24},{24,28},{28,20},{20,12},{12,4},{4,0},{1,9},{9... | collective-permute-start | bytes 1572872 | tf_op jit(solution)/shard_map/ppermute | solution.py:304
  10.9 22.1 %collective-permute-start = (f32[1,8,512]{2,1,0:T(8,128)S(1)}, f32[1,8,512]{2,1,0:T(8,128)S(1)}, u32[]{:S(2)}, u32[]{:S(2)}) collective-permute-start(f32[1,8,512]{2,1,0:T(8,128)S(1)} %bitcast.38), channel_id=1, source_target_pairs={{0,4},{4,0},{8,12},{12,8},{16,20},{20,16},{24,28},{28,24},{1,5},{5... | collective-permute-start | bytes 49160 | tf_op jit(solution)/shard_map/ppermute | solution.py:808
  11.3 32.4 %collective-permute-start.18 = (f32[64,2048]{1,0:T(8,128)}, f32[64,2048]{1,0:T(8,128)S(1)}, u32[]{:S(2)}, u32[]{:S(2)}) collective-permute-start(f32[64,2048]{1,0:T(8,128)} %get-tuple-element.85), channel_id=1, source_target_pairs={{8,0},{16,8},{24,16},{28,24},{20,28},{12,20},{4,12},{0,4},{9,1},{1... | collective-permute-start | bytes 1572872 | tf_op jit(solution)/shard_map/ppermute | solution.py:305
  12.9 32.3 %collective-permute-start.7 = (f32[64,2048]{1,0:T(8,128)S(1)}, f32[64,2048]{1,0:T(8,128)S(1)}, u32[]{:S(2)}, u32[]{:S(2)}) collective-permute-start(f32[64,2048]{1,0:T(8,128)S(1)} %get-tuple-element.86), channel_id=1, source_target_pairs={{8,0},{16,8},{24,16},{28,24},{20,28},{12,20},{4,12},{0,4},{9,1},{1... | collective-permute-start | bytes 1572872 | tf_op jit(solution)/shard_map/ppermute | solution.py:305
  43.7 25.8 %collective-permute-start.14 = (f32[64,2048]{1,0:T(8,128)S(1)}, f32[64,2048]{1,0:T(8,128)S(1)}, u32[]{:S(2)}, u32[]{:S(2)}) collective-permute-start(f32[64,2048]{1,0:T(8,128)S(1)} %collective-permute-done.13.refs_1_), channel_id=1, source_target_pairs={{0,8},{8,16},{16,24},{24,28},{28,20},{20,12},{12,4},{4,0},{1,9},{9... | collective-permute-start | bytes 1572872 | tf_op jit(solution)/shard_map/ppermute | solution.py:304
  45.2 24.2 %collective-permute-start.19 = (f32[64,2048]{1,0:T(8,128)S(1)}, f32[64,2048]{1,0:T(8,128)S(1)}, u32[]{:S(2)}, u32[]{:S(2)}) collective-permute-start(f32[64,2048]{1,0:T(8,128)S(1)} %collective-permute-done.18.refs_4_), channel_id=1, source_target_pairs={{8,0},{16,8},{24,16},{28,24},{20,28},{12,20},{4,12},{0,4},{9,1},{1... | collective-permute-start | bytes 1572872 | tf_op jit(solution)/shard_map/ppermute | solution.py:305
  58.2 20.6 %collective-permute-start.5 = (f32[64,2048]{1,0:T(8,128)S(1)}, f32[64,2048]{1,0:T(8,128)S(1)}, u32[]{:S(2)}, u32[]{:S(2)}) collective-permute-start(f32[64,2048]{1,0:T(8,128)S(1)} %collective-permute-done.4.refs_0_), channel_id=1, source_target_pairs={{0,8},{8,16},{16,24},{24,28},{28,20},{20,12},{12,4},{4,0},{1,9},{9... | collective-permute-start | bytes 1572872 | tf_op jit(solution)/shard_map/ppermute | solution.py:304
  71.2 19.4 %collective-permute-start.26 = (f32[64,2048]{1,0:T(8,128)S(1)}, f32[64,2048]{1,0:T(8,128)S(1)}, u32[]{:S(2)}, u32[]{:S(2)}) collective-permute-start(f32[64,2048]{1,0:T(8,128)S(1)} %collective-permute-done.8.refs_5_), channel_id=1, source_target_pairs={{0,1},{1,0},{2,3},{3,2},{4,5},{5,4},{6,7},{7,6},{8,9},{9,8},{10,11... | collective-permute-start | bytes 1572872 | tf_op jit(solution)/shard_map/ppermute | solution.py:284
  72.1 20.1 %collective-permute-start.15 = (f32[64,2048]{1,0:T(8,128)S(1)}, f32[64,2048]{1,0:T(8,128)S(1)}, u32[]{:S(2)}, u32[]{:S(2)}) collective-permute-start(f32[64,2048]{1,0:T(8,128)S(1)} %collective-permute-done.14.refs_1_), channel_id=1, source_target_pairs={{0,8},{8,16},{16,24},{24,28},{28,20},{20,12},{12,4},{4,0},{1,9},{9... | collective-permute-start | bytes 1572872 | tf_op jit(solution)/shard_map/ppermute | solution.py:304
  73.4 24.0 %collective-permute-start.20 = (f32[64,2048]{1,0:T(8,128)S(1)}, f32[64,2048]{1,0:T(8,128)S(1)}, u32[]{:S(2)}, u32[]{:S(2)}) collective-permute-start(f32[64,2048]{1,0:T(8,128)S(1)} %collective-permute-done.19.refs_4_), channel_id=1, source_target_pairs={{8,0},{16,8},{24,16},{28,24},{20,28},{12,20},{4,12},{0,4},{9,1},{1... | collective-permute-start | bytes 1572872 | tf_op jit(solution)/shard_map/ppermute | solution.py:305
  90.1 19.6 %collective-permute-start.22 = (f32[64,2048]{1,0:T(8,128)S(1)}, f32[64,2048]{1,0:T(8,128)S(1)}, u32[]{:S(2)}, u32[]{:S(2)}) collective-permute-start(f32[64,2048]{1,0:T(8,128)S(1)} %collective-permute-done.9.refs_5_), channel_id=1, source_target_pairs={{0,1},{1,0},{2,3},{3,2},{4,5},{5,4},{6,7},{7,6},{8,9},{9,8},{10,11... | collective-permute-start | bytes 1572872 | tf_op jit(solution)/shard_map/ppermute | solution.py:284
  160.1 25.4 %collective-permute-start.32 = (f32[128,2048]{1,0:T(8,128)S(1)}, f32[128,2048]{1,0:T(8,128)}, u32[]{:S(2)}, u32[]{:S(2)}) collective-permute-start(f32[128,2048]{1,0:T(8,128)S(1)} %add.176), channel_id=1, source_target_pairs={{0,2},{2,0},{1,3},{3,1},{4,6},{6,4},{5,7},{7,5},{8,10},{10,8},{9,1... | collective-permute-start | bytes 3145736 | tf_op jit(solution)/shard_map/ppermute | solution.py:280
  187.6 40.9 %collective-permute-start.33 = (f32[128,2048]{1,0:T(8,128)S(1)}, f32[128,2048]{1,0:T(8,128)S(1)}, u32[]{:S(2)}, u32[]{:S(2)}) collective-permute-start(f32[128,2048]{1,0:T(8,128)S(1)} %multiply_multiply_fusion.13), channel_id=1, source_target_pairs={{0,1},{1,0},{2,3},{3,2},{4,5},{5,4},{6,7},{7,6},{8,9},{9,8},{10,11... | collective-permute-start | bytes 3145736 | tf_op jit(solution)/shard_map/ppermute | solution.py:284
  189.8 36.9 %collective-permute-start.80 = (f32[64,2048]{1,0:T(8,128)S(1)}, f32[64,2048]{1,0:T(8,128)}, u32[]{:S(2)}, u32[]{:S(2)}) collective-permute-start(f32[64,2048]{1,0:T(8,128)S(1)} %constant_dynamic-slice_fusion.4), channel_id=1, source_target_pairs={{0,16},{4,20},{8,24},{12,28},{16,0},{20,4},{24,8},{28,12},{1,17},{... | collective-permute-start | bytes 1572872 | tf_op jit(solution)/shard_map/ppermute | solution.py:823
  191.4 37.1 %collective-permute-start.84 = (f32[64,2048]{1,0:T(8,128)S(1)}, f32[64,2048]{1,0:T(8,128)}, u32[]{:S(2)}, u32[]{:S(2)}) collective-permute-start(f32[64,2048]{1,0:T(8,128)S(1)} %constant_dynamic-slice_fusion.4), channel_id=1, source_target_pairs={{0,24},{4,28},{8,0},{12,4},{16,8},{20,12},{24,16},{28,20},{1,25},{... | collective-permute-start | bytes 1572872 | tf_op jit(solution)/shard_map/ppermute | solution.py:823
  204.8 39.6 %collective-permute-start.77 = (f32[64,2048]{1,0:T(8,128)}, f32[64,2048]{1,0:T(8,128)}, u32[]{:S(2)}, u32[]{:S(2)}) collective-permute-start(f32[64,2048]{1,0:T(8,128)} %collective-permute-done.76.refs_0_), channel_id=1, source_target_pairs={{0,2},{2,0},{1,3},{3,1},{4,6},{6,4},{5,7},{7,5},{8,10},{10,8},{9,1... | collective-permute-start | bytes 1572872 | tf_op jit(solution)/shard_map/ppermute | solution.py:828
  206.5 45.6 %collective-permute-start.78 = (f32[64,2048]{1,0:T(8,128)}, f32[64,2048]{1,0:T(8,128)}, u32[]{:S(2)}, u32[]{:S(2)}) collective-permute-start(f32[64,2048]{1,0:T(8,128)} %collective-permute-done.76.refs_0_), channel_id=1, source_target_pairs={{0,1},{1,0},{2,3},{3,2},{4,5},{5,4},{6,7},{7,6},{8,9},{9,8},{10,11... | collective-permute-start | bytes 1572872 | tf_op jit(solution)/shard_map/ppermute | solution.py:284
  228.5 24.2 %collective-permute-start.82 = (f32[64,2048]{1,0:T(8,128)}, f32[64,2048]{1,0:T(8,128)}, u32[]{:S(2)}, u32[]{:S(2)}) collective-permute-start(f32[64,2048]{1,0:T(8,128)} %collective-permute-done.80.refs_4_), channel_id=1, source_target_pairs={{0,1},{1,0},{2,3},{3,2},{4,5},{5,4},{6,7},{7,6},{8,9},{9,8},{10,11... | collective-permute-start | bytes 1572872 | tf_op jit(solution)/shard_map/ppermute | solution.py:284
  228.5 23.6 %collective-permute-start.85 = (f32[64,2048]{1,0:T(8,128)}, f32[64,2048]{1,0:T(8,128)}, u32[]{:S(2)}, u32[]{:S(2)}) collective-permute-start(f32[64,2048]{1,0:T(8,128)} %collective-permute-done.84.refs_8_), channel_id=1, source_target_pairs={{0,2},{2,0},{1,3},{3,1},{4,6},{6,4},{5,7},{7,5},{8,10},{10,8},{9,1... | collective-permute-start | bytes 1572872 | tf_op jit(solution)/shard_map/ppermute | solution.py:828
  262.5 49.8 %collective-permute-start.35 = (f32[128,2048]{1,0:T(8,128)S(1)}, f32[128,2048]{1,0:T(8,128)S(1)}, u32[]{:S(2)}, u32[]{:S(2)}) collective-permute-start(f32[128,2048]{1,0:T(8,128)S(1)} %add.181), channel_id=1, source_target_pairs={{0,2},{2,0},{1,3},{3,1},{4,6},{6,4},{5,7},{7,5},{8,10},{10,8},{9,1... | collective-permute-start | bytes 3145736 | tf_op jit(solution)/shard_map/ppermute | solution.py:280
  264.3 25.8 %collective-permute-start.64 = (f32[64,2048]{1,0:T(8,128)S(1)}, f32[64,2048]{1,0:T(8,128)}, u32[]{:S(2)}, u32[]{:S(2)}) collective-permute-start(f32[64,2048]{1,0:T(8,128)S(1)} %constant_dynamic-slice_fusion.5), channel_id=1, source_target_pairs={{0,8},{4,12},{8,16},{12,20},{16,24},{20,28},{24,0},{28,4},{1,9},{5... | collective-permute-start | bytes 1572872 | tf_op jit(solution)/shard_map/ppermute | solution.py:823
  274.2 37.6 %collective-permute-start.68 = (f32[64,2048]{1,0:T(8,128)S(1)}, f32[64,2048]{1,0:T(8,128)}, u32[]{:S(2)}, u32[]{:S(2)}) collective-permute-start(f32[64,2048]{1,0:T(8,128)S(1)} %constant_dynamic-slice_fusion.5), channel_id=1, source_target_pairs={{0,16},{4,20},{8,24},{12,28},{16,0},{20,4},{24,8},{28,12},{1,17},{... | collective-permute-start | bytes 1572872 | tf_op jit(solution)/shard_map/ppermute | solution.py:823
  277.7 34.6 %collective-permute-start.72 = (f32[64,2048]{1,0:T(8,128)S(1)}, f32[64,2048]{1,0:T(8,128)}, u32[]{:S(2)}, u32[]{:S(2)}) collective-permute-start(f32[64,2048]{1,0:T(8,128)S(1)} %constant_dynamic-slice_fusion.5), channel_id=1, source_target_pairs={{0,24},{4,28},{8,0},{12,4},{16,8},{20,12},{24,16},{28,20},{1,25},{... | collective-permute-start | bytes 1572872 | tf_op jit(solution)/shard_map/ppermute | solution.py:823
  290.1 24.9 %collective-permute-start.65 = (f32[64,2048]{1,0:T(8,128)}, f32[64,2048]{1,0:T(8,128)S(1)}, u32[]{:S(2)}, u32[]{:S(2)}) collective-permute-start(f32[64,2048]{1,0:T(8,128)} %collective-permute-done.64.refs_0_), channel_id=1, source_target_pairs={{0,2},{2,0},{1,3},{3,1},{4,6},{6,4},{5,7},{7,5},{8,10},{10,8},{9,1... | collective-permute-start | bytes 1572872 | tf_op jit(solution)/shard_map/ppermute | solution.py:828
  290.7 61.8 %collective-permute-start.66 = (f32[64,2048]{1,0:T(8,128)}, f32[64,2048]{1,0:T(8,128)}, u32[]{:S(2)}, u32[]{:S(2)}) collective-permute-start(f32[64,2048]{1,0:T(8,128)} %collective-permute-done.64.refs_0_), channel_id=1, source_target_pairs={{0,1},{1,0},{2,3},{3,2},{4,5},{5,4},{6,7},{7,6},{8,9},{9,8},{10,11... | collective-permute-start | bytes 1572872 | tf_op jit(solution)/shard_map/ppermute | solution.py:284
  312.3 40.2 %collective-permute-start.70 = (f32[64,2048]{1,0:T(8,128)}, f32[64,2048]{1,0:T(8,128)}, u32[]{:S(2)}, u32[]{:S(2)}) collective-permute-start(f32[64,2048]{1,0:T(8,128)} %collective-permute-done.68.refs_4_), channel_id=1, source_target_pairs={{0,1},{1,0},{2,3},{3,2},{4,5},{5,4},{6,7},{7,6},{8,9},{9,8},{10,11... | collective-permute-start | bytes 1572872 | tf_op jit(solution)/shard_map/ppermute | solution.py:284
  312.3 24.6 %collective-permute-start.73 = (f32[64,2048]{1,0:T(8,128)}, f32[64,2048]{1,0:T(8,128)S(1)}, u32[]{:S(2)}, u32[]{:S(2)}) collective-permute-start(f32[64,2048]{1,0:T(8,128)} %collective-permute-done.72.refs_8_), channel_id=1, source_target_pairs={{0,2},{2,0},{1,3},{3,1},{4,6},{6,4},{5,7},{7,5},{8,10},{10,8},{9,1... | collective-permute-start | bytes 1572872 | tf_op jit(solution)/shard_map/ppermute | solution.py:828
  315.0 38.0 %collective-permute-start.74 = (f32[64,2048]{1,0:T(8,128)}, f32[64,2048]{1,0:T(8,128)}, u32[]{:S(2)}, u32[]{:S(2)}) collective-permute-start(f32[64,2048]{1,0:T(8,128)} %collective-permute-done.72.refs_8_), channel_id=1, source_target_pairs={{0,1},{1,0},{2,3},{3,2},{4,5},{5,4},{6,7},{7,6},{8,9},{9,8},{10,11... | collective-permute-start | bytes 1572872 | tf_op jit(solution)/shard_map/ppermute | solution.py:284
  326.8 36.4 %collective-permute-start.40 = (f32[128,2048]{1,0:T(8,128)S(1)}, f32[128,2048]{1,0:T(8,128)S(1)}, u32[]{:S(2)}, u32[]{:S(2)}) collective-permute-start(f32[128,2048]{1,0:T(8,128)S(1)} %convert_add_fusion.1.refs_0_), channel_id=1, source_target_pairs={{8,0},{16,8},{24,16},{28,24},{20,28},{12,20},{4,12},{0,4},{9,1},{1... | collective-permute-start | bytes 3145736 | tf_op jit(solution)/shard_map/ppermute | solution.py:305
  336.9 28.1 %collective-permute-start.36 = (f32[128,2048]{1,0:T(8,128)S(1)}, f32[128,2048]{1,0:T(8,128)}, u32[]{:S(2)}, u32[]{:S(2)}) collective-permute-start(f32[128,2048]{1,0:T(8,128)S(1)} %convert_add_fusion.1.refs_0_), channel_id=1, source_target_pairs={{0,8},{8,16},{16,24},{24,28},{28,20},{20,12},{12,4},{4,0},{1,9},{9... | collective-permute-start | bytes 3145736 | tf_op jit(solution)/shard_map/ppermute | solution.py:304
  363.1 25.6 %collective-permute-start.41 = (f32[128,2048]{1,0:T(8,128)S(1)}, f32[128,2048]{1,0:T(8,128)}, u32[]{:S(2)}, u32[]{:S(2)}) collective-permute-start(f32[128,2048]{1,0:T(8,128)S(1)} %collective-permute-done.40.refs_2_), channel_id=1, source_target_pairs={{8,0},{16,8},{24,16},{28,24},{20,28},{12,20},{4,12},{0,4},{9,1},{1... | collective-permute-start | bytes 3145736 | tf_op jit(solution)/shard_map/ppermute | solution.py:305
  365.1 24.0 %collective-permute-start.37 = (f32[128,2048]{1,0:T(8,128)}, f32[128,2048]{1,0:T(8,128)S(1)}, u32[]{:S(2)}, u32[]{:S(2)}) collective-permute-start(f32[128,2048]{1,0:T(8,128)} %collective-permute-done.36.refs_0_), channel_id=1, source_target_pairs={{0,8},{8,16},{16,24},{24,28},{28,20},{20,12},{12,4},{4,0},{1,9},{9... | collective-permute-start | bytes 3145736 | tf_op jit(solution)/shard_map/ppermute | solution.py:304
  388.8 25.7 %collective-permute-start.42 = (f32[128,2048]{1,0:T(8,128)}, f32[128,2048]{1,0:T(8,128)S(1)}, u32[]{:S(2)}, u32[]{:S(2)}) collective-permute-start(f32[128,2048]{1,0:T(8,128)} %collective-permute-done.41.refs_6_), channel_id=1, source_target_pairs={{8,0},{16,8},{24,16},{28,24},{20,28},{12,20},{4,12},{0,4},{9,1},{1... | collective-permute-start | bytes 3145736 | tf_op jit(solution)/shard_map/ppermute | solution.py:305
  389.1 24.6 %collective-permute-start.38 = (f32[128,2048]{1,0:T(8,128)S(1)}, f32[128,2048]{1,0:T(8,128)S(1)}, u32[]{:S(2)}, u32[]{:S(2)}) collective-permute-start(f32[128,2048]{1,0:T(8,128)S(1)} %collective-permute-done.37.refs_4_), channel_id=1, source_target_pairs={{0,8},{8,16},{16,24},{24,28},{28,20},{20,12},{12,4},{4,0},{1,9},{9... | collective-permute-start | bytes 3145736 | tf_op jit(solution)/shard_map/ppermute | solution.py:304
  393.3 24.2 %collective-permute-start.53 = (f32[128,2048]{1,0:T(8,128)S(1)}, f32[128,2048]{1,0:T(8,128)S(1)}, u32[]{:S(2)}, u32[]{:S(2)}) collective-permute-start(f32[128,2048]{1,0:T(8,128)S(1)} %copy-done.72), channel_id=1, source_target_pairs={{0,1},{1,0},{2,3},{3,2},{4,5},{5,4},{6,7},{7,6},{8,9},{9,8},{10,11... | collective-permute-start | bytes 3145736 | tf_op jit(solution)/shard_map/ppermute | solution.py:278
  393.4 24.1 %collective-permute-start.50 = (f32[128,2048]{1,0:T(8,128)S(1)}, f32[128,2048]{1,0:T(8,128)S(1)}, u32[]{:S(2)}, u32[]{:S(2)}) collective-permute-start(f32[128,2048]{1,0:T(8,128)S(1)} %collective-permute-done.37.refs_4_), channel_id=1, source_target_pairs={{0,1},{1,0},{2,3},{3,2},{4,5},{5,4},{6,7},{7,6},{8,9},{9,8},{10,11... | collective-permute-start | bytes 3145736 | tf_op jit(solution)/shard_map/ppermute | solution.py:284
  397.1 30.7 %collective-permute-start.51 = (f32[128,2048]{1,0:T(8,128)}, f32[128,2048]{1,0:T(8,128)}, u32[]{:S(2)}, u32[]{:S(2)}) collective-permute-start(f32[128,2048]{1,0:T(8,128)} %collective-permute-done.41.refs_6_), channel_id=1, source_target_pairs={{0,1},{1,0},{2,3},{3,2},{4,5},{5,4},{6,7},{7,6},{8,9},{9,8},{10,11... | collective-permute-start | bytes 3145736 | tf_op jit(solution)/shard_map/ppermute | solution.py:284
  413.7 28.0 %collective-permute-start.46 = (f32[128,2048]{1,0:T(8,128)S(1)}, f32[128,2048]{1,0:T(8,128)S(1)}, u32[]{:S(2)}, u32[]{:S(2)}) collective-permute-start(f32[128,2048]{1,0:T(8,128)S(1)} %collective-permute-done.38.refs_0_), channel_id=1, source_target_pairs={{0,1},{1,0},{2,3},{3,2},{4,5},{5,4},{6,7},{7,6},{8,9},{9,8},{10,11... | collective-permute-start | bytes 3145736 | tf_op jit(solution)/shard_map/ppermute | solution.py:284
  414.5 28.9 %collective-permute-start.47 = (f32[128,2048]{1,0:T(8,128)S(1)}, f32[128,2048]{1,0:T(8,128)S(1)}, u32[]{:S(2)}, u32[]{:S(2)}) collective-permute-start(f32[128,2048]{1,0:T(8,128)S(1)} %collective-permute-done.42.refs_2_), channel_id=1, source_target_pairs={{0,1},{1,0},{2,3},{3,2},{4,5},{5,4},{6,7},{7,6},{8,9},{9,8},{10,11... | collective-permute-start | bytes 3145736 | tf_op jit(solution)/shard_map/ppermute | solution.py:284
  427.9 67.9 %collective-permute-start.54 = (f32[128,2048]{1,0:T(8,128)}, f32[128,2048]{1,0:T(8,128)}, u32[]{:S(2)}, u32[]{:S(2)}) collective-permute-start(f32[128,2048]{1,0:T(8,128)} %add.184), channel_id=1, source_target_pairs={{0,2},{2,0},{1,3},{3,1},{4,6},{6,4},{5,7},{7,5},{8,10},{10,8},{9,1... | collective-permute-start | bytes 3145736 | tf_op jit(solution)/shard_map/ppermute | solution.py:280
  432.0 18.8 %collective-permute-start.45 = (f32[64,2048]{1,0:T(8,128)S(1)}, f32[64,2048]{1,0:T(8,128)S(1)}, u32[]{:S(2)}, u32[]{:S(2)}) collective-permute-start(f32[64,2048]{1,0:T(8,128)S(1)} %collective-permute-done.43.refs_1_), channel_id=1, source_target_pairs={{0,1},{1,0},{2,3},{3,2},{4,5},{5,4},{6,7},{7,6},{8,9},{9,8},{10,11... | collective-permute-start | bytes 1572872 | tf_op jit(solution)/shard_map/ppermute | solution.py:284
  441.7 72.8 %collective-permute-start.90 = (f32[1024,256]{1,0:T(8,128)}, f32[1024,256]{1,0:T(8,128)}, u32[]{:S(2)}, u32[]{:S(2)}) collective-permute-start(f32[1024,256]{1,0:T(8,128)} %constant_dynamic-slice_fusion.1), channel_id=1, source_target_pairs={{0,4},{4,0},{8,12},{12,8},{16,20},{20,16},{24,28},{28,24},{1,5},{5... | collective-permute-start | bytes 3145736 | tf_op jit(solution)/shard_map/ppermute | solution.py:898
  443.3 89.5 %collective-permute-start.89 = (f32[256,1024]{1,0:T(8,128)}, f32[256,1024]{1,0:T(8,128)}, u32[]{:S(2)}, u32[]{:S(2)}) collective-permute-start(f32[256,1024]{1,0:T(8,128)} %get-tuple-element.154), channel_id=1, source_target_pairs={{0,4},{4,0},{8,12},{12,8},{16,20},{20,16},{24,28},{28,24},{1,5},{5... | collective-permute-start | bytes 3145736 | tf_op jit(solution)/shard_map/ppermute | solution.py:898
  449.2 86.0 %collective-permute-start.88 = (f32[256,1024]{1,0:T(8,128)}, f32[256,1024]{1,0:T(8,128)}, u32[]{:S(2)}, u32[]{:S(2)}) collective-permute-start(f32[256,1024]{1,0:T(8,128)} %get-tuple-element.153), channel_id=1, source_target_pairs={{0,4},{4,0},{8,12},{12,8},{16,20},{20,16},{24,28},{28,24},{1,5},{5... | collective-permute-start | bytes 3145736 | tf_op jit(solution)/shard_map/ppermute | solution.py:898
  487.8 18.7 %collective-permute-start.56 = (f32[128,2048]{1,0:T(8,128)}, f32[128,2048]{1,0:T(8,128)S(1)}, u32[]{:S(2)}, u32[]{:S(2)}) collective-permute-start(f32[128,2048]{1,0:T(8,128)} %get-tuple-element.148.other_ref), channel_id=1, source_target_pairs={{0,1},{1,0},{2,3},{3,2},{4,5},{5,4},{6,7},{7,6},{8,9},{9,8},{10,11... | collective-permute-start | bytes 3145736 | tf_op jit(solution)/shard_map/ppermute | solution.py:278
  506.6 25.1 %collective-permute-start.57 = (f32[128,2048]{1,0:T(8,128)S(1)}, f32[128,2048]{1,0:T(8,128)S(1)}, u32[]{:S(2)}, u32[]{:S(2)}) collective-permute-start(f32[128,2048]{1,0:T(8,128)S(1)} %add.187), channel_id=1, source_target_pairs={{0,2},{2,0},{1,3},{3,1},{4,6},{6,4},{5,7},{7,5},{8,10},{10,8},{9,1... | collective-permute-start | bytes 3145736 | tf_op jit(solution)/shard_map/ppermute | solution.py:280
  514.0 24.1 %collective-permute-start.55 = (f32[128,2048]{1,0:T(8,128)S(1)}, f32[128,2048]{1,0:T(8,128)S(1)}, u32[]{:S(2)}, u32[]{:S(2)}) collective-permute-start(f32[128,2048]{1,0:T(8,128)S(1)} %add_multiply_fusion), channel_id=1, source_target_pairs={{0,1},{1,0},{2,3},{3,2},{4,5},{5,4},{6,7},{7,6},{8,9},{9,8},{10,11... | collective-permute-start | bytes 3145736 | tf_op jit(solution)/shard_map/ppermute | solution.py:284
  (116 other events, 1248.2 us)

commit v4 on v3

--- a/solution.py
+++ b/solution.py
@@ -861,7 +861,8 @@
         grad_up_gate, grad_up = back(grad_hidden)
         return hidden.astype(bf16), grad_up_gate.astype(bf16), grad_up.astype(bf16)
 
-    hidden, grad_up_gate, grad_up = feed_forward(normed_mid_own, transpose_right(cotangent_own, down_weight))
+    grad_hidden_own = transpose_right(cotangent_own, down_weight)
+    hidden, grad_up_gate, grad_up = feed_forward(normed_mid_own, grad_hidden_own)
 
     mid_mine, mid_other = rows_sum([grad_up_gate, grad_up], [gelu_weight, linear_weight], 0, rows, True)
     grad_mid = head_total(mid_mine, mid_other)
@@ -895,7 +896,7 @@
         found = found + transpose_left(left_far, right_far)
         kept = lax.dynamic_slice_in_dim(found, shard % 2 * slab, slab, dim)
         sent = lax.dynamic_slice_in_dim(found, (1 - shard % 2) * slab, slab, dim)
-        sent = lax.ppermute(after(sent, branch_came[-1][1]), SEQ, [(i, i ^ 1) for i in range(shards)])
+        sent = lax.ppermute(after(sent, branch_came[-2][0]), SEQ, [(i, i ^ 1) for i in range(shards)])
         return kept + sent
 
     mid_slab, mid_slab_far = pair_slab(normed_mid_own), pair_slab(normed_mid_far)

time: 552 us -> 601 us (1.089)
  waiting for transfers between devices: 209 us -> 250 us
  starting transfers between devices: 82.6 us -> 90.1 us
    ppermute x11, waiting for transfers between devices: 39.5 us -> 92.1 us  [ring_gather(): lax.ppermute(rising[part], SEQ, up)]
    ppermute x6, waiting for transfers between devices: 28.6 us -> 21.2 us  [far_parts(): both = [item, lax.ppermute(item, HEAD, ACROSS)]]
    unnamed x146 -> x144, local copies, waits for them, and re-layouts: 12 us -> 12.4 us
  transfers between devices with their start and end apart: 91 -> 91, of which waited for: 27 -> 26; matrix products, arithmetic and copies ran while one was open for 14% -> 13% of each run, Pallas kernels for 22% -> 20%
where the time goes in v4:
time: 601 us; the launch traced here: 591 us
  waiting for transfers between devices  250 us (42%)
  Pallas kernels  153 us (25%)
  starting transfers between devices  90.1 us (15%)
  matrix products  54.6 us (9%)
  other arithmetic  25 us (4%)
  local copies, waits for them, and re-layouts  15.2 us (3%)
    ppermute x11, waiting for transfers between devices, ring_gather(): lax.ppermute(rising[part], SEQ, up)  92.1 us
    pallas_call x9, Pallas kernels, rows_product(): pl.pallas_call(functools.partial(rows_product_kernel, count, size, pieces...  70.6 us
    ppermute x6, waiting for transfers between devices, far_start(): return [lax.ppermute(share, SEQ, hop) for hop in far_hops()]  55.9 us
    ppermute x4, waiting for transfers between devices, head_total(): return both + lax.ppermute(both, HEAD, ACROSS)  39.8 us
    ppermute x11, starting transfers between devices, ring_gather(): lax.ppermute(rising[part], SEQ, up)  27.9 us
    ppermute x3, waiting for transfers between devices, local_gather(): lax.ppermute(info, SEQ, [(i, i ^ 1 << index) for i in range(shards)])  25.5 us
    pallas_call x4, Pallas kernels, rows_sum(): pl.pallas_call(functools.partial(rows_sum_kernel, len(arrays), tile, turn...  25.5 us
    pallas_call x1, Pallas kernels, retain_backward(): pl.pallas_call(retain_backward_kernel, grid_spec=pltpu.PrefetchScalarGrid...  24.8 us
  transfers between devices with their start and end apart: 91, of which 26 were waited for; matrix products, arithmetic and copies ran while one was open for 13% of the time, Pallas kernels for 20%

profile of v4, /device:TPU:0, one launch (start us, length us, event | category | flops | bytes accessed | tf_op | source)
XLA Modules:
  0.0 591.0 jit_solution(14912925416442035079)
XLA Ops:
  6.2 3.1 collective-permute-start.3
  14.5 18.5 %collective-permute-done = f32[1,8,512]{2,1,0:T(8,128)S(1)} collective-permute-done((f32[1,8,512]{2,1,0:T(8,128)S(1)}, f32[1,8,512]{2,1,0:T(8,128)S(1)}, u32[]{:S(2)}, u32[]{:S(2)}) %collective-permute-start) | collective-permute-done | bytes 16416 | tf_op jit(solution)/shard_map/ppermute | solution.py:808
  34.4 3.1 collective-permute-done.1
  39.4 4.0 collective-permute-done.2
  46.5 7.0 %rows_product.9 = (bf16[2048,256]{1,0:T(8,128)(2,1)S(1)}, bf16[2048,512]{1,0:T(8,128)(2,1)}, bf16[2048,512]{1,0:T(8,128)(2,1)}, bf16[2048,512]{1,0:T(8,128)(2,1)...) custom-call(s32[1]{0:T(128)} %bitcast.5.shard_ref, ...), custom_call_target="tpu_custom_call" | custom-call | flops 3221225472 | bytes 16252928 | tf_op jit(solution)/shard_map/rows_product/pallas_call | solution.py:484
  58.5 10.9 %collective-permute-done.14.refs_1_ = f32[64,2048]{1,0:T(8,128)S(1)} collective-permute-done((f32[64,2048]{1,0:T(8,128)S(1)}, f32[64,2048]{1,0:T(8,128)S(1)}, u32[]{:S(2)}, u32[]{:S(2)}) %collective-permute-start.14) | collective-permute-done | bytes 524320 | tf_op jit(solution)/shard_map/ppermute | solution.py:304
  74.1 4.8 collective-permute-done.5.refs_0_
  78.9 11.2 %rows_product.10 = (bf16[2048,256]{1,0:T(8,128)(2,1)}, bf16[2048,512]{1,0:T(8,128)(2,1)}, bf16[2048,512]{1,0:T(8,128)(2,1)}, bf16[2048,512]{1,0:T(8,128)(2,1)}, ...) custom-call(s32[1]{0:T(128)} %bitcast.5.shard_ref, ...), custom_call_target="tpu_custom_call", output_to_operand_aliasing={{0}: (13, {}), {1}: (14, {}), {2}: (15, {}), {3}: (16, {}),... | custom-call | flops 6442450944 | bytes 19922944 | tf_op jit(solution)/shard_map/rows_product/pallas_call | solution.py:484
  92.8 4.6 collective-permute-done.20.refs_4_
  97.9 11.1 %rows_product.11 = (bf16[2048,256]{1,0:T(8,128)(2,1)}, bf16[2048,512]{1,0:T(8,128)(2,1)}, bf16[2048,512]{1,0:T(8,128)(2,1)}, bf16[2048,512]{1,0:T(8,128)(2,1)}, ...) custom-call(s32[1]{0:T(128)} %bitcast.5.shard_ref, ...), custom_call_target="tpu_custom_call", output_to_operand_aliasing={{0}: (13, {}), {1}: (14, {}), {2}: (15, {}), {3}: (16, {}),... | custom-call | flops 6442450944 | bytes 19922944 | tf_op jit(solution)/shard_map/rows_product/pallas_call | solution.py:484
  110.8 11.1 %rows_product.12 = (bf16[2048,256]{1,0:T(8,128)(2,1)}, bf16[2048,512]{1,0:T(8,128)(2,1)}, bf16[2048,512]{1,0:T(8,128)(2,1)}, bf16[2048,512]{1,0:T(8,128)(2,1)}, ...) custom-call(s32[1]{0:T(128)} %bitcast.5.shard_ref, ...), custom_call_target="tpu_custom_call", output_to_operand_aliasing={{0}: (13, {}), {1}: (14, {}), {2}: (15, {}), {3}: (16, {}),... | custom-call | flops 6442450944 | bytes 19922944 | tf_op jit(solution)/shard_map/rows_product/pallas_call | solution.py:484
  122.7 7.3 %rows_product.13 = (bf16[2048,256]{1,0:T(8,128)(2,1)}, bf16[2048,512]{1,0:T(8,128)(2,1)}, bf16[2048,512]{1,0:T(8,128)(2,1)}, bf16[2048,512]{1,0:T(8,128)(2,1)}, ...) custom-call(s32[1]{0:T(128)} %bitcast.5.shard_ref, ...), custom_call_target="tpu_custom_call", output_to_operand_aliasing={{0}: (9, {}), {1}: (10, {}), {2}: (11, {}), {3}: (12, {}), ... | custom-call | flops 3221225472 | bytes 16252928 | tf_op jit(solution)/shard_map/rows_product/pallas_call | solution.py:484
  130.0 20.5 %retain_forward.1 = (f32[2048,1024]{1,0:T(8,128)}, bf16[2048,1024]{1,0:T(8,128)(2,1)}, bf16[2,8,256,512]{3,2,1,0:T(8,128)(2,1)}, f32[2,8,256,256]{3,2,1,0:T(8,12...) custom-call(s32[8]{0:T(128)} %compare_select_fusion.4.slot_ref, ...), custom_call_target="tpu_custom_call" | custom-call | flops 4831838208 | bytes 33554432 | tf_op jit(solution)/shard_map/retain_forward/pallas_call | solution.py:693
  150.5 5.3 rows_sum.4
  155.9 2.8 collective-permute-done.31
  162.0 23.4 %collective-permute-done.32 = f32[128,2048]{1,0:T(8,128)} collective-permute-done((f32[128,2048]{1,0:T(8,128)S(1)}, f32[128,2048]{1,0:T(8,128)}, u32[]{:S(2)}, u32[]{:S(2)}) %collective-permute-start.32) | collective-permute-done | bytes 1048608 | tf_op jit(solution)/shard_map/ppermute | solution.py:280
  191.3 2.7 collective-permute-start.84
  195.3 9.5 %collective-permute-done.76.refs_0_ = f32[64,2048]{1,0:T(8,128)} collective-permute-done((f32[64,2048]{1,0:T(8,128)S(1)}, f32[64,2048]{1,0:T(8,128)}, u32[]{:S(2)}, u32[]{:S(2)}) %collective-permute-start.76) | collective-permute-done | bytes 524320 | tf_op jit(solution)/shard_map/ppermute | solution.py:823
  206.5 20.2 %collective-permute-done.80.refs_4_ = f32[64,2048]{1,0:T(8,128)} collective-permute-done((f32[64,2048]{1,0:T(8,128)S(1)}, f32[64,2048]{1,0:T(8,128)}, u32[]{:S(2)}, u32[]{:S(2)}) %collective-permute-start.80) | collective-permute-done | bytes 524320 | tf_op jit(solution)/shard_map/ppermute | solution.py:823
  231.6 4.5 multiply_convert_fusion.4
  237.7 6.7 %rows_sum.5 = (f32[128,2048]{1,0:T(8,128)}, f32[128,2048]{1,0:T(8,128)}) custom-call(bf16[256,1024]{1,0:T(8,128)(2,1)} %get-tuple-element.170.refs_0_, bf16[256,1024]{1,0:T(8,128)(2,1)} %get-tuple-element.169.refs_1_, bf16[2048,1024]{1,0:T(8,128)(2,1)} %refs_2_.4, bf16[2048,1024]{1,0:T(8,128)(2,1)} %refs_3_.3), custom_call_target="tpu_custom_call" | custom-call | flops 2147483648 | bytes 11534336 | tf_op jit(solution)/shard_map/rows_sum/pallas_call | solution.py:541
  245.0 7.1 %collective-permute-done.85.refs_9_ = f32[64,2048]{1,0:T(8,128)} collective-permute-done((f32[64,2048]{1,0:T(8,128)}, f32[64,2048]{1,0:T(8,128)}, u32[]{:S(2)}, u32[]{:S(2)}) %collective-permute-start.85) | collective-permute-done | bytes 524320 | tf_op jit(solution)/shard_map/ppermute | solution.py:828
  255.9 4.8 round_rows.3
  264.3 9.9 %collective-permute-start.64 = (f32[64,2048]{1,0:T(8,128)S(1)}, f32[64,2048]{1,0:T(8,128)}, u32[]{:S(2)}, u32[]{:S(2)}) collective-permute-start(f32[64,2048]{1,0:T(8,128)S(1)} %constant_dynamic-slice_fusion.5), channel_id=1, source_target_pairs={{0,8},{4,12},{8,16},{12,20},{16,24},{20,28},{24,0},{28,4},{1,9},{5... | collective-permute-start | bytes 1572872 | tf_op jit(solution)/shard_map/ppermute | solution.py:823
  274.2 3.5 collective-permute-start.68
  277.7 7.3 %fusion.66 = f32[768,1024]{1,0:T(8,128)} fusion(bf16[768,2048]{1,0:T(8,128)(2,1)S(1)} %copy-done.26, bf16[1024,2048]{1,0:T(8,128)(2,1)} %refs_1_.5), kind=kOutput, calls=%fused_computation.158 | convolution fusion | flops 3221225472 | bytes 10485760 | tf_op jit(solution)/shard_map/dot_general | solution.py:50
  285.0 5.1 collective-permute-done.64.refs_0_
  290.7 21.1 %collective-permute-done.68.refs_4_ = f32[64,2048]{1,0:T(8,128)} collective-permute-done((f32[64,2048]{1,0:T(8,128)S(1)}, f32[64,2048]{1,0:T(8,128)}, u32[]{:S(2)}, u32[]{:S(2)}) %collective-permute-start.68) | collective-permute-done | bytes 524320 | tf_op jit(solution)/shard_map/ppermute | solution.py:823
  315.3 11.5 %collective-permute-done.69.refs_5_ = f32[64,2048]{1,0:T(8,128)S(1)} collective-permute-done((f32[64,2048]{1,0:T(8,128)}, f32[64,2048]{1,0:T(8,128)S(1)}, u32[]{:S(2)}, u32[]{:S(2)}) %collective-permute-start.69) | collective-permute-done | bytes 524320 | tf_op jit(solution)/shard_map/ppermute | solution.py:828
  326.8 7.6 %collective-permute-start.36 = (f32[128,2048]{1,0:T(8,128)S(1)}, f32[128,2048]{1,0:T(8,128)S(1)}, u32[]{:S(2)}, u32[]{:S(2)}) collective-permute-start(f32[128,2048]{1,0:T(8,128)S(1)} %convert_add_fusion.1.refs_0_), channel_id=1, source_target_pairs={{0,8},{8,16},{16,24},{24,28},{28,20},{20,12},{12,4},{4,0},{1,9},{9... | collective-permute-start | bytes 3145736 | tf_op jit(solution)/shard_map/ppermute | solution.py:304
  337.8 5.3 rows_sum.7
  343.1 3.1 fusion.34
  352.0 4.8 round_rows.2
  356.8 7.1 %collective-permute-start.37 = (f32[128,2048]{1,0:T(8,128)S(1)}, f32[128,2048]{1,0:T(8,128)S(1)}, u32[]{:S(2)}, u32[]{:S(2)}) collective-permute-start(f32[128,2048]{1,0:T(8,128)S(1)} %collective-permute-done.36.refs_0_), channel_id=1, source_target_pairs={{0,8},{8,16},{16,24},{24,28},{28,20},{20,12},{12,4},{4,0},{1,9},{9... | collective-permute-start | bytes 3145736 | tf_op jit(solution)/shard_map/ppermute | solution.py:304
  366.0 12.2 %fusion = (f32[768,1024]{1,0:T(8,128)S(1)}, f32[768,1024]{1,0:T(8,128)S(1)}) fusion(bf16[768,2048]{1,0:T(8,128)(2,1)} %round_rows.2, bf16[2048,1024]{1,0:T(8,128)(2,1)} %refs_2_.4), kind=kOutput, calls=%fused_computation.1 | convolution fusion | flops 3269984256 | bytes 13631488 | tf_op jit(solution)/shard_map/dot_general | solution.py:40
  378.7 3.5 fusion.67
  382.4 4.8 collective-permute-done.37.refs_4_
  396.3 15.9 %collective-permute-done.38.refs_0_ = f32[128,2048]{1,0:T(8,128)S(1)} collective-permute-done((f32[128,2048]{1,0:T(8,128)S(1)}, f32[128,2048]{1,0:T(8,128)S(1)}, u32[]{:S(2)}, u32[]{:S(2)}) %collective-permute-start.38) | collective-permute-done | bytes 1048608 | tf_op jit(solution)/shard_map/ppermute | solution.py:304
  417.8 4.1 rows_product.14
  428.9 9.2 %rows_product.15 = (bf16[2048,256]{1,0:T(8,128)(2,1)S(1)}, bf16[2048,1024]{1,0:T(8,128)(2,1)}) custom-call(s32[1]{0:T(128)} %bitcast.5.shard_ref, f32[128,2048]{1,0:T(8,128)S(1)} %copy-done.7, f32[128,2048]{1,0:T(8,128)S(1)} %collective-permute-done.48.refs_1_, ...), custom_call_target="tpu_custom_call", output_to_operand_aliasing={{0}: (10, {}), {1}: (11, {})} | custom-call | flops 4294967296 | bytes 14680064 | tf_op jit(solution)/shard_map/rows_product/pallas_call | solution.py:484
  438.1 5.5 rows_product.16
  443.7 53.8 %collective-permute-done.39.refs_0_ = f32[64,2048]{1,0:T(8,128)S(1)} collective-permute-done((f32[64,2048]{1,0:T(8,128)}, f32[64,2048]{1,0:T(8,128)S(1)}, u32[]{:S(2)}, u32[]{:S(2)}) %collective-permute-start.39) | collective-permute-done | bytes 524320 | tf_op jit(solution)/shard_map/ppermute | solution.py:304
  505.6 4.0 rows_product.17
  509.6 24.8 %retain_backward.1 = (bf16[2048,512]{1,0:T(8,128)(2,1)}, bf16[2048,512]{1,0:T(8,128)(2,1)}, bf16[2048,1024]{1,0:T(8,128)(2,1)}, bf16[2048,1024]{1,0:T(8,128)(2,1)}) custom-call(s32[8]{0:T(128)} %compare_select_fusion.4.slot_ref, bf16[2048,512]{1,0:T(8,128)(2,1)} %get-tuple-element.116.q_ref, bf16[2048,512]{1,0:T(8,128)(2,1)} %get-tuple-element.118.k_ref, ...), custom_call_target="tpu_custom_call" | custom-call | flops 10200547328 | bytes 54525952 | tf_op jit(solution)/shard_map/retain_backward/pallas_call | solution.py:723
  534.4 8.2 %rows_sum.6 = (f32[128,2048]{1,0:T(8,128)}, f32[128,2048]{1,0:T(8,128)}) custom-call(bf16[2048,512]{1,0:T(8,128)(2,1)} %get-tuple-element.139.refs_0_, bf16[2048,512]{1,0:T(8,128)(2,1)} %get-tuple-element.140.refs_1_, bf16[2048,1024]{1,0:T(8,128)(2,1)} %get-tuple-element.141.refs_2_, bf16[2048,1024]{1,0:T(8,128)(2,1)} %get-tuple-element.142.refs_3_, ...), custom_call_target="tpu_custom_call" | custom-call | flops 3221225472 | bytes 16252928 | tf_op jit(solution)/shard_map/rows_sum/pallas_call | solution.py:541
  545.9 4.6 fusion.65
  556.5 3.4 collective-permute-start.60
  564.1 16.3 %collective-permute-done.57 = f32[128,2048]{1,0:T(8,128)S(1)} collective-permute-done((f32[128,2048]{1,0:T(8,128)S(1)}, f32[128,2048]{1,0:T(8,128)S(1)}, u32[]{:S(2)}, u32[]{:S(2)}) %collective-permute-start.57) | collective-permute-done | bytes 1048608 | tf_op jit(solution)/shard_map/ppermute | solution.py:280
  (367 shorter events, 127.8 us)
Async XLA Ops:
  6.2 26.7 %collective-permute-start.3 = (f32[64,2048]{1,0:T(8,128)}, f32[64,2048]{1,0:T(8,128)S(1)}, u32[]{:S(2)}, u32[]{:S(2)}) collective-permute-start(f32[64,2048]{1,0:T(8,128)} %get-tuple-element.85), channel_id=1, source_target_pairs={{0,8},{8,16},{16,24},{24,28},{28,20},{20,12},{12,4},{4,0},{1,9},{9... | collective-permute-start | bytes 1572872 | tf_op jit(solution)/shard_map/ppermute | solution.py:304
  9.3 23.8 %collective-permute-start.13 = (f32[64,2048]{1,0:T(8,128)S(1)}, f32[64,2048]{1,0:T(8,128)S(1)}, u32[]{:S(2)}, u32[]{:S(2)}) collective-permute-start(f32[64,2048]{1,0:T(8,128)S(1)} %get-tuple-element.86), channel_id=1, source_target_pairs={{0,8},{8,16},{16,24},{24,28},{28,20},{20,12},{12,4},{4,0},{1,9},{9... | collective-permute-start | bytes 1572872 | tf_op jit(solution)/shard_map/ppermute | solution.py:304
  10.9 22.1 %collective-permute-start = (f32[1,8,512]{2,1,0:T(8,128)S(1)}, f32[1,8,512]{2,1,0:T(8,128)S(1)}, u32[]{:S(2)}, u32[]{:S(2)}) collective-permute-start(f32[1,8,512]{2,1,0:T(8,128)S(1)} %bitcast.38), channel_id=1, source_target_pairs={{0,4},{4,0},{8,12},{12,8},{16,20},{20,16},{24,28},{28,24},{1,5},{5... | collective-permute-start | bytes 49160 | tf_op jit(solution)/shard_map/ppermute | solution.py:808
  11.3 32.4 %collective-permute-start.18 = (f32[64,2048]{1,0:T(8,128)}, f32[64,2048]{1,0:T(8,128)S(1)}, u32[]{:S(2)}, u32[]{:S(2)}) collective-permute-start(f32[64,2048]{1,0:T(8,128)} %get-tuple-element.85), channel_id=1, source_target_pairs={{8,0},{16,8},{24,16},{28,24},{20,28},{12,20},{4,12},{0,4},{9,1},{1... | collective-permute-start | bytes 1572872 | tf_op jit(solution)/shard_map/ppermute | solution.py:305
  12.9 32.3 %collective-permute-start.7 = (f32[64,2048]{1,0:T(8,128)S(1)}, f32[64,2048]{1,0:T(8,128)S(1)}, u32[]{:S(2)}, u32[]{:S(2)}) collective-permute-start(f32[64,2048]{1,0:T(8,128)S(1)} %get-tuple-element.86), channel_id=1, source_target_pairs={{8,0},{16,8},{24,16},{28,24},{20,28},{12,20},{4,12},{0,4},{9,1},{1... | collective-permute-start | bytes 1572872 | tf_op jit(solution)/shard_map/ppermute | solution.py:305
  43.7 25.8 %collective-permute-start.14 = (f32[64,2048]{1,0:T(8,128)S(1)}, f32[64,2048]{1,0:T(8,128)S(1)}, u32[]{:S(2)}, u32[]{:S(2)}) collective-permute-start(f32[64,2048]{1,0:T(8,128)S(1)} %collective-permute-done.13.refs_1_), channel_id=1, source_target_pairs={{0,8},{8,16},{16,24},{24,28},{28,20},{20,12},{12,4},{4,0},{1,9},{9... | collective-permute-start | bytes 1572872 | tf_op jit(solution)/shard_map/ppermute | solution.py:304
  45.2 24.2 %collective-permute-start.19 = (f32[64,2048]{1,0:T(8,128)S(1)}, f32[64,2048]{1,0:T(8,128)S(1)}, u32[]{:S(2)}, u32[]{:S(2)}) collective-permute-start(f32[64,2048]{1,0:T(8,128)S(1)} %collective-permute-done.18.refs_4_), channel_id=1, source_target_pairs={{8,0},{16,8},{24,16},{28,24},{20,28},{12,20},{4,12},{0,4},{9,1},{1... | collective-permute-start | bytes 1572872 | tf_op jit(solution)/shard_map/ppermute | solution.py:305
  58.2 20.6 %collective-permute-start.5 = (f32[64,2048]{1,0:T(8,128)S(1)}, f32[64,2048]{1,0:T(8,128)S(1)}, u32[]{:S(2)}, u32[]{:S(2)}) collective-permute-start(f32[64,2048]{1,0:T(8,128)S(1)} %collective-permute-done.4.refs_0_), channel_id=1, source_target_pairs={{0,8},{8,16},{16,24},{24,28},{28,20},{20,12},{12,4},{4,0},{1,9},{9... | collective-permute-start | bytes 1572872 | tf_op jit(solution)/shard_map/ppermute | solution.py:304
  71.2 19.4 %collective-permute-start.26 = (f32[64,2048]{1,0:T(8,128)S(1)}, f32[64,2048]{1,0:T(8,128)S(1)}, u32[]{:S(2)}, u32[]{:S(2)}) collective-permute-start(f32[64,2048]{1,0:T(8,128)S(1)} %collective-permute-done.8.refs_5_), channel_id=1, source_target_pairs={{0,1},{1,0},{2,3},{3,2},{4,5},{5,4},{6,7},{7,6},{8,9},{9,8},{10,11... | collective-permute-start | bytes 1572872 | tf_op jit(solution)/shard_map/ppermute | solution.py:284
  71.4 18.7 %collective-permute-start.9 = (f32[64,2048]{1,0:T(8,128)S(1)}, f32[64,2048]{1,0:T(8,128)S(1)}, u32[]{:S(2)}, u32[]{:S(2)}) collective-permute-start(f32[64,2048]{1,0:T(8,128)S(1)} %collective-permute-done.8.refs_5_), channel_id=1, source_target_pairs={{8,0},{16,8},{24,16},{28,24},{20,28},{12,20},{4,12},{0,4},{9,1},{1... | collective-permute-start | bytes 1572872 | tf_op jit(solution)/shard_map/ppermute | solution.py:305
  72.1 20.1 %collective-permute-start.15 = (f32[64,2048]{1,0:T(8,128)S(1)}, f32[64,2048]{1,0:T(8,128)S(1)}, u32[]{:S(2)}, u32[]{:S(2)}) collective-permute-start(f32[64,2048]{1,0:T(8,128)S(1)} %collective-permute-done.14.refs_1_), channel_id=1, source_target_pairs={{0,8},{8,16},{16,24},{24,28},{28,20},{20,12},{12,4},{4,0},{1,9},{9... | collective-permute-start | bytes 1572872 | tf_op jit(solution)/shard_map/ppermute | solution.py:304
  73.4 24.0 %collective-permute-start.20 = (f32[64,2048]{1,0:T(8,128)S(1)}, f32[64,2048]{1,0:T(8,128)S(1)}, u32[]{:S(2)}, u32[]{:S(2)}) collective-permute-start(f32[64,2048]{1,0:T(8,128)S(1)} %collective-permute-done.19.refs_4_), channel_id=1, source_target_pairs={{8,0},{16,8},{24,16},{28,24},{20,28},{12,20},{4,12},{0,4},{9,1},{1... | collective-permute-start | bytes 1572872 | tf_op jit(solution)/shard_map/ppermute | solution.py:305
  90.1 19.6 %collective-permute-start.22 = (f32[64,2048]{1,0:T(8,128)S(1)}, f32[64,2048]{1,0:T(8,128)S(1)}, u32[]{:S(2)}, u32[]{:S(2)}) collective-permute-start(f32[64,2048]{1,0:T(8,128)S(1)} %collective-permute-done.9.refs_5_), channel_id=1, source_target_pairs={{0,1},{1,0},{2,3},{3,2},{4,5},{5,4},{6,7},{7,6},{8,9},{9,8},{10,11... | collective-permute-start | bytes 1572872 | tf_op jit(solution)/shard_map/ppermute | solution.py:284
  160.1 25.4 %collective-permute-start.32 = (f32[128,2048]{1,0:T(8,128)S(1)}, f32[128,2048]{1,0:T(8,128)}, u32[]{:S(2)}, u32[]{:S(2)}) collective-permute-start(f32[128,2048]{1,0:T(8,128)S(1)} %add.176), channel_id=1, source_target_pairs={{0,2},{2,0},{1,3},{3,1},{4,6},{6,4},{5,7},{7,5},{8,10},{10,8},{9,1... | collective-permute-start | bytes 3145736 | tf_op jit(solution)/shard_map/ppermute | solution.py:280
  187.6 40.9 %collective-permute-start.33 = (f32[128,2048]{1,0:T(8,128)S(1)}, f32[128,2048]{1,0:T(8,128)S(1)}, u32[]{:S(2)}, u32[]{:S(2)}) collective-permute-start(f32[128,2048]{1,0:T(8,128)S(1)} %multiply_multiply_fusion.13), channel_id=1, source_target_pairs={{0,1},{1,0},{2,3},{3,2},{4,5},{5,4},{6,7},{7,6},{8,9},{9,8},{10,11... | collective-permute-start | bytes 3145736 | tf_op jit(solution)/shard_map/ppermute | solution.py:284
  189.8 37.0 %collective-permute-start.80 = (f32[64,2048]{1,0:T(8,128)S(1)}, f32[64,2048]{1,0:T(8,128)}, u32[]{:S(2)}, u32[]{:S(2)}) collective-permute-start(f32[64,2048]{1,0:T(8,128)S(1)} %constant_dynamic-slice_fusion.4), channel_id=1, source_target_pairs={{0,16},{4,20},{8,24},{12,28},{16,0},{20,4},{24,8},{28,12},{1,17},{... | collective-permute-start | bytes 1572872 | tf_op jit(solution)/shard_map/ppermute | solution.py:823
  191.3 37.2 %collective-permute-start.84 = (f32[64,2048]{1,0:T(8,128)S(1)}, f32[64,2048]{1,0:T(8,128)}, u32[]{:S(2)}, u32[]{:S(2)}) collective-permute-start(f32[64,2048]{1,0:T(8,128)S(1)} %constant_dynamic-slice_fusion.4), channel_id=1, source_target_pairs={{0,24},{4,28},{8,0},{12,4},{16,8},{20,12},{24,16},{28,20},{1,25},{... | collective-permute-start | bytes 1572872 | tf_op jit(solution)/shard_map/ppermute | solution.py:823
  204.8 39.6 %collective-permute-start.77 = (f32[64,2048]{1,0:T(8,128)}, f32[64,2048]{1,0:T(8,128)}, u32[]{:S(2)}, u32[]{:S(2)}) collective-permute-start(f32[64,2048]{1,0:T(8,128)} %collective-permute-done.76.refs_0_), channel_id=1, source_target_pairs={{0,2},{2,0},{1,3},{3,1},{4,6},{6,4},{5,7},{7,5},{8,10},{10,8},{9,1... | collective-permute-start | bytes 1572872 | tf_op jit(solution)/shard_map/ppermute | solution.py:828
  206.5 45.6 %collective-permute-start.78 = (f32[64,2048]{1,0:T(8,128)}, f32[64,2048]{1,0:T(8,128)}, u32[]{:S(2)}, u32[]{:S(2)}) collective-permute-start(f32[64,2048]{1,0:T(8,128)} %collective-permute-done.76.refs_0_), channel_id=1, source_target_pairs={{0,1},{1,0},{2,3},{3,2},{4,5},{5,4},{6,7},{7,6},{8,9},{9,8},{10,11... | collective-permute-start | bytes 1572872 | tf_op jit(solution)/shard_map/ppermute | solution.py:284
  228.5 24.2 %collective-permute-start.82 = (f32[64,2048]{1,0:T(8,128)}, f32[64,2048]{1,0:T(8,128)}, u32[]{:S(2)}, u32[]{:S(2)}) collective-permute-start(f32[64,2048]{1,0:T(8,128)} %collective-permute-done.80.refs_4_), channel_id=1, source_target_pairs={{0,1},{1,0},{2,3},{3,2},{4,5},{5,4},{6,7},{7,6},{8,9},{9,8},{10,11... | collective-permute-start | bytes 1572872 | tf_op jit(solution)/shard_map/ppermute | solution.py:284
  228.5 23.6 %collective-permute-start.85 = (f32[64,2048]{1,0:T(8,128)}, f32[64,2048]{1,0:T(8,128)}, u32[]{:S(2)}, u32[]{:S(2)}) collective-permute-start(f32[64,2048]{1,0:T(8,128)} %collective-permute-done.84.refs_8_), channel_id=1, source_target_pairs={{0,2},{2,0},{1,3},{3,1},{4,6},{6,4},{5,7},{7,5},{8,10},{10,8},{9,1... | collective-permute-start | bytes 1572872 | tf_op jit(solution)/shard_map/ppermute | solution.py:828
  262.5 49.8 %collective-permute-start.35 = (f32[128,2048]{1,0:T(8,128)S(1)}, f32[128,2048]{1,0:T(8,128)S(1)}, u32[]{:S(2)}, u32[]{:S(2)}) collective-permute-start(f32[128,2048]{1,0:T(8,128)S(1)} %add.181), channel_id=1, source_target_pairs={{0,2},{2,0},{1,3},{3,1},{4,6},{6,4},{5,7},{7,5},{8,10},{10,8},{9,1... | collective-permute-start | bytes 3145736 | tf_op jit(solution)/shard_map/ppermute | solution.py:280
  264.3 25.8 %collective-permute-start.64 = (f32[64,2048]{1,0:T(8,128)S(1)}, f32[64,2048]{1,0:T(8,128)}, u32[]{:S(2)}, u32[]{:S(2)}) collective-permute-start(f32[64,2048]{1,0:T(8,128)S(1)} %constant_dynamic-slice_fusion.5), channel_id=1, source_target_pairs={{0,8},{4,12},{8,16},{12,20},{16,24},{20,28},{24,0},{28,4},{1,9},{5... | collective-permute-start | bytes 1572872 | tf_op jit(solution)/shard_map/ppermute | solution.py:823
  274.2 37.6 %collective-permute-start.68 = (f32[64,2048]{1,0:T(8,128)S(1)}, f32[64,2048]{1,0:T(8,128)}, u32[]{:S(2)}, u32[]{:S(2)}) collective-permute-start(f32[64,2048]{1,0:T(8,128)S(1)} %constant_dynamic-slice_fusion.5), channel_id=1, source_target_pairs={{0,16},{4,20},{8,24},{12,28},{16,0},{20,4},{24,8},{28,12},{1,17},{... | collective-permute-start | bytes 1572872 | tf_op jit(solution)/shard_map/ppermute | solution.py:823
  277.7 34.6 %collective-permute-start.72 = (f32[64,2048]{1,0:T(8,128)S(1)}, f32[64,2048]{1,0:T(8,128)}, u32[]{:S(2)}, u32[]{:S(2)}) collective-permute-start(f32[64,2048]{1,0:T(8,128)S(1)} %constant_dynamic-slice_fusion.5), channel_id=1, source_target_pairs={{0,24},{4,28},{8,0},{12,4},{16,8},{20,12},{24,16},{28,20},{1,25},{... | collective-permute-start | bytes 1572872 | tf_op jit(solution)/shard_map/ppermute | solution.py:823
  290.1 24.9 %collective-permute-start.65 = (f32[64,2048]{1,0:T(8,128)}, f32[64,2048]{1,0:T(8,128)S(1)}, u32[]{:S(2)}, u32[]{:S(2)}) collective-permute-start(f32[64,2048]{1,0:T(8,128)} %collective-permute-done.64.refs_0_), channel_id=1, source_target_pairs={{0,2},{2,0},{1,3},{3,1},{4,6},{6,4},{5,7},{7,5},{8,10},{10,8},{9,1... | collective-permute-start | bytes 1572872 | tf_op jit(solution)/shard_map/ppermute | solution.py:828
  290.7 55.6 %collective-permute-start.66 = (f32[64,2048]{1,0:T(8,128)}, f32[64,2048]{1,0:T(8,128)}, u32[]{:S(2)}, u32[]{:S(2)}) collective-permute-start(f32[64,2048]{1,0:T(8,128)} %collective-permute-done.64.refs_0_), channel_id=1, source_target_pairs={{0,1},{1,0},{2,3},{3,2},{4,5},{5,4},{6,7},{7,6},{8,9},{9,8},{10,11... | collective-permute-start | bytes 1572872 | tf_op jit(solution)/shard_map/ppermute | solution.py:284
  312.3 33.9 %collective-permute-start.70 = (f32[64,2048]{1,0:T(8,128)}, f32[64,2048]{1,0:T(8,128)}, u32[]{:S(2)}, u32[]{:S(2)}) collective-permute-start(f32[64,2048]{1,0:T(8,128)} %collective-permute-done.68.refs_4_), channel_id=1, source_target_pairs={{0,1},{1,0},{2,3},{3,2},{4,5},{5,4},{6,7},{7,6},{8,9},{9,8},{10,11... | collective-permute-start | bytes 1572872 | tf_op jit(solution)/shard_map/ppermute | solution.py:284
  312.3 24.6 %collective-permute-start.73 = (f32[64,2048]{1,0:T(8,128)}, f32[64,2048]{1,0:T(8,128)S(1)}, u32[]{:S(2)}, u32[]{:S(2)}) collective-permute-start(f32[64,2048]{1,0:T(8,128)} %collective-permute-done.72.refs_8_), channel_id=1, source_target_pairs={{0,2},{2,0},{1,3},{3,1},{4,6},{6,4},{5,7},{7,5},{8,10},{10,8},{9,1... | collective-permute-start | bytes 1572872 | tf_op jit(solution)/shard_map/ppermute | solution.py:828
  315.0 31.7 %collective-permute-start.74 = (f32[64,2048]{1,0:T(8,128)}, f32[64,2048]{1,0:T(8,128)}, u32[]{:S(2)}, u32[]{:S(2)}) collective-permute-start(f32[64,2048]{1,0:T(8,128)} %collective-permute-done.72.refs_8_), channel_id=1, source_target_pairs={{0,1},{1,0},{2,3},{3,2},{4,5},{5,4},{6,7},{7,6},{8,9},{9,8},{10,11... | collective-permute-start | bytes 1572872 | tf_op jit(solution)/shard_map/ppermute | solution.py:284
  326.8 30.0 %collective-permute-start.36 = (f32[128,2048]{1,0:T(8,128)S(1)}, f32[128,2048]{1,0:T(8,128)S(1)}, u32[]{:S(2)}, u32[]{:S(2)}) collective-permute-start(f32[128,2048]{1,0:T(8,128)S(1)} %convert_add_fusion.1.refs_0_), channel_id=1, source_target_pairs={{0,8},{8,16},{16,24},{24,28},{28,20},{20,12},{12,4},{4,0},{1,9},{9... | collective-permute-start | bytes 3145736 | tf_op jit(solution)/shard_map/ppermute | solution.py:304
  337.0 29.0 %collective-permute-start.40 = (f32[128,2048]{1,0:T(8,128)S(1)}, f32[128,2048]{1,0:T(8,128)}, u32[]{:S(2)}, u32[]{:S(2)}) collective-permute-start(f32[128,2048]{1,0:T(8,128)S(1)} %convert_add_fusion.1.refs_0_), channel_id=1, source_target_pairs={{8,0},{16,8},{24,16},{28,24},{20,28},{12,20},{4,12},{0,4},{9,1},{1... | collective-permute-start | bytes 3145736 | tf_op jit(solution)/shard_map/ppermute | solution.py:305
  356.8 30.4 %collective-permute-start.37 = (f32[128,2048]{1,0:T(8,128)S(1)}, f32[128,2048]{1,0:T(8,128)S(1)}, u32[]{:S(2)}, u32[]{:S(2)}) collective-permute-start(f32[128,2048]{1,0:T(8,128)S(1)} %collective-permute-done.36.refs_0_), channel_id=1, source_target_pairs={{0,8},{8,16},{16,24},{24,28},{28,20},{20,12},{12,4},{4,0},{1,9},{9... | collective-permute-start | bytes 3145736 | tf_op jit(solution)/shard_map/ppermute | solution.py:304
  366.0 23.4 %collective-permute-start.41 = (f32[128,2048]{1,0:T(8,128)}, f32[128,2048]{1,0:T(8,128)}, u32[]{:S(2)}, u32[]{:S(2)}) collective-permute-start(f32[128,2048]{1,0:T(8,128)} %collective-permute-done.40.refs_2_), channel_id=1, source_target_pairs={{8,0},{16,8},{24,16},{28,24},{20,28},{12,20},{4,12},{0,4},{9,1},{1... | collective-permute-start | bytes 3145736 | tf_op jit(solution)/shard_map/ppermute | solution.py:305
  387.2 25.0 %collective-permute-start.38 = (f32[128,2048]{1,0:T(8,128)S(1)}, f32[128,2048]{1,0:T(8,128)S(1)}, u32[]{:S(2)}, u32[]{:S(2)}) collective-permute-start(f32[128,2048]{1,0:T(8,128)S(1)} %collective-permute-done.37.refs_4_), channel_id=1, source_target_pairs={{0,8},{8,16},{16,24},{24,28},{28,20},{20,12},{12,4},{4,0},{1,9},{9... | collective-permute-start | bytes 3145736 | tf_op jit(solution)/shard_map/ppermute | solution.py:304
  389.4 24.8 %collective-permute-start.42 = (f32[128,2048]{1,0:T(8,128)}, f32[128,2048]{1,0:T(8,128)S(1)}, u32[]{:S(2)}, u32[]{:S(2)}) collective-permute-start(f32[128,2048]{1,0:T(8,128)} %collective-permute-done.41.refs_6_), channel_id=1, source_target_pairs={{8,0},{16,8},{24,16},{28,24},{20,28},{12,20},{4,12},{0,4},{9,1},{1... | collective-permute-start | bytes 3145736 | tf_op jit(solution)/shard_map/ppermute | solution.py:305
  391.9 23.5 %collective-permute-start.53 = (f32[128,2048]{1,0:T(8,128)S(1)}, f32[128,2048]{1,0:T(8,128)S(1)}, u32[]{:S(2)}, u32[]{:S(2)}) collective-permute-start(f32[128,2048]{1,0:T(8,128)S(1)} %copy-done.71), channel_id=1, source_target_pairs={{0,1},{1,0},{2,3},{3,2},{4,5},{5,4},{6,7},{7,6},{8,9},{9,8},{10,11... | collective-permute-start | bytes 3145736 | tf_op jit(solution)/shard_map/ppermute | solution.py:278
  392.0 24.4 %collective-permute-start.50 = (f32[128,2048]{1,0:T(8,128)S(1)}, f32[128,2048]{1,0:T(8,128)S(1)}, u32[]{:S(2)}, u32[]{:S(2)}) collective-permute-start(f32[128,2048]{1,0:T(8,128)S(1)} %collective-permute-done.37.refs_4_), channel_id=1, source_target_pairs={{0,1},{1,0},{2,3},{3,2},{4,5},{5,4},{6,7},{7,6},{8,9},{9,8},{10,11... | collective-permute-start | bytes 3145736 | tf_op jit(solution)/shard_map/ppermute | solution.py:284
  396.3 28.9 %collective-permute-start.51 = (f32[128,2048]{1,0:T(8,128)}, f32[128,2048]{1,0:T(8,128)}, u32[]{:S(2)}, u32[]{:S(2)}) collective-permute-start(f32[128,2048]{1,0:T(8,128)} %collective-permute-done.41.refs_6_), channel_id=1, source_target_pairs={{0,1},{1,0},{2,3},{3,2},{4,5},{5,4},{6,7},{7,6},{8,9},{9,8},{10,11... | collective-permute-start | bytes 3145736 | tf_op jit(solution)/shard_map/ppermute | solution.py:284
  415.4 82.6 %collective-permute-start.90 = (f32[1024,256]{1,0:T(8,128)}, f32[1024,256]{1,0:T(8,128)}, u32[]{:S(2)}, u32[]{:S(2)}) collective-permute-start(f32[1024,256]{1,0:T(8,128)} %constant_dynamic-slice_fusion.1), channel_id=1, source_target_pairs={{0,4},{4,0},{8,12},{12,8},{16,20},{20,16},{24,28},{28,24},{1,5},{5... | collective-permute-start | bytes 3145736 | tf_op jit(solution)/shard_map/ppermute | solution.py:899
  416.4 84.4 %collective-permute-start.89 = (f32[256,1024]{1,0:T(8,128)S(1)}, f32[256,1024]{1,0:T(8,128)}, u32[]{:S(2)}, u32[]{:S(2)}) collective-permute-start(f32[256,1024]{1,0:T(8,128)S(1)} %get-tuple-element.154), channel_id=1, source_target_pairs={{0,4},{4,0},{8,12},{12,8},{16,20},{20,16},{24,28},{28,24},{1,5},{5... | collective-permute-start | bytes 3145736 | tf_op jit(solution)/shard_map/ppermute | solution.py:899
  425.2 78.0 %collective-permute-start.88 = (f32[256,1024]{1,0:T(8,128)S(1)}, f32[256,1024]{1,0:T(8,128)}, u32[]{:S(2)}, u32[]{:S(2)}) collective-permute-start(f32[256,1024]{1,0:T(8,128)S(1)} %get-tuple-element.153), channel_id=1, source_target_pairs={{0,4},{4,0},{8,12},{12,8},{16,20},{20,16},{24,28},{28,24},{1,5},{5... | collective-permute-start | bytes 3145736 | tf_op jit(solution)/shard_map/ppermute | solution.py:899
  426.1 71.3 %collective-permute-start.39 = (f32[64,2048]{1,0:T(8,128)}, f32[64,2048]{1,0:T(8,128)S(1)}, u32[]{:S(2)}, u32[]{:S(2)}) collective-permute-start(f32[64,2048]{1,0:T(8,128)} %slice.16), channel_id=1, source_target_pairs={{0,8},{8,16},{16,24},{24,28},{28,20},{20,12},{12,4},{4,0},{1,9},{9... | collective-permute-start | bytes 1572872 | tf_op jit(solution)/shard_map/ppermute | solution.py:304
  428.5 69.5 %collective-permute-start.43 = (f32[64,2048]{1,0:T(8,128)S(1)}, f32[64,2048]{1,0:T(8,128)S(1)}, u32[]{:S(2)}, u32[]{:S(2)}) collective-permute-start(f32[64,2048]{1,0:T(8,128)S(1)} %slice.17), channel_id=1, source_target_pairs={{8,0},{16,8},{24,16},{28,24},{20,28},{12,20},{4,12},{0,4},{9,1},{1... | collective-permute-start | bytes 1572872 | tf_op jit(solution)/shard_map/ppermute | solution.py:305
  497.4 53.2 %collective-permute-start.54 = (f32[128,2048]{1,0:T(8,128)}, f32[128,2048]{1,0:T(8,128)}, u32[]{:S(2)}, u32[]{:S(2)}) collective-permute-start(f32[128,2048]{1,0:T(8,128)} %add.184), channel_id=1, source_target_pairs={{0,2},{2,0},{1,3},{3,1},{4,6},{6,4},{5,7},{7,5},{8,10},{10,8},{9,1... | collective-permute-start | bytes 3145736 | tf_op jit(solution)/shard_map/ppermute | solution.py:280
  554.9 25.6 %collective-permute-start.57 = (f32[128,2048]{1,0:T(8,128)S(1)}, f32[128,2048]{1,0:T(8,128)S(1)}, u32[]{:S(2)}, u32[]{:S(2)}) collective-permute-start(f32[128,2048]{1,0:T(8,128)S(1)} %add.187), channel_id=1, source_target_pairs={{0,2},{2,0},{1,3},{3,1},{4,6},{6,4},{5,7},{7,5},{8,10},{10,8},{9,1... | collective-permute-start | bytes 3145736 | tf_op jit(solution)/shard_map/ppermute | solution.py:280
  562.1 24.7 %collective-permute-start.55 = (f32[128,2048]{1,0:T(8,128)S(1)}, f32[128,2048]{1,0:T(8,128)S(1)}, u32[]{:S(2)}, u32[]{:S(2)}) collective-permute-start(f32[128,2048]{1,0:T(8,128)S(1)} %add_multiply_fusion), channel_id=1, source_target_pairs={{0,1},{1,0},{2,3},{3,2},{4,5},{5,4},{6,7},{7,6},{8,9},{9,8},{10,11... | collective-permute-start | bytes 3145736 | tf_op jit(solution)/shard_map/ppermute | solution.py:284
  562.1 21.0 %collective-permute-start.61 = (f32[2,2048]{1,0:T(2,128)S(1)}, f32[2,2048]{1,0:T(2,128)S(1)}, u32[]{:S(2)}, u32[]{:S(2)}) collective-permute-start(f32[2,2048]{1,0:T(2,128)S(1)} %fusion.92), channel_id=1, source_target_pairs={{0,4},{4,0},{8,12},{12,8},{16,20},{20,16},{24,28},{28,24},{1,5},{5... | collective-permute-start | bytes 49160 | tf_op jit(solution)/shard_map/ppermute | solution.py:260
  (115 other events, 1386.6 us)
